TPU v7x, 32 devices: a whole 2x2x4 slice. The times are simulated.
32 devices in a mesh: grid: 16 (over z, y, x), mode: 2 (over core).
Axes of the slice: x: 2, y: 2, z: 4, core: 2. Of those that a mesh axis runs over, the one named last changes fastest.
Arguments:
- field: bfloat16 [288, 96, 8, 128], P('mode', 'grid'), may hold values from -6 to 6
- coupling: bfloat16 [11, 288, 288], P(None, 'mode'), may hold values from -0.0390625 to 0.0390625
- coefs: bfloat16 [11, 96, 8, 128], P(None, 'grid'), may hold values from 0.25 to 2
Outputs:
- applied: bfloat16 [288, 96, 8, 128], P('mode', 'grid')
All inputs are finite; a program needn't handle non-finite values.
Results may differ from a plain program's by a relative error of at most 0.005.
Values may be sent and summed in bfloat16 or wider, within the bound.
No kernel may reach another device: no remote copies, remote signals or barrier semaphores. Data moves between devices by JAX's collectives and lax.ppermute only.
A program may use at most 128 MiB of HBM per device.

v0:
```python
import jax
import jax.numpy as jnp
from jax import lax
from jax.sharding import PartitionSpec as P


def padded_2(block, sides, width):
    for axis, dim in sides:
        count = lax.axis_size(axis)
        forward = [(i, i + 1) for i in range(count - 1)]
        backward = [(target, source) for source, target in forward]
        low = lax.ppermute(
            lax.slice_in_dim(block, block.shape[dim] - width, None, axis=dim), axis, forward
        )
        high = lax.ppermute(lax.slice_in_dim(block, 0, width, axis=dim), axis, backward)
        block = jnp.concatenate([low, block, high], axis=dim)
    return block


def mix_modes(coupling, whole):
    total_modes = whole.shape[0]
    flat = whole.reshape(total_modes, -1)

    def one_term(weights):
        return jnp.dot(weights, flat, preferred_element_type=jnp.float32).astype(jnp.bfloat16)

    result = lax.map(one_term, coupling)
    return result.reshape((coupling.shape[0], coupling.shape[1]) + whole.shape[1:])


def stencil_sum(mixed_ext, coef_ext):

    def step(total, inputs):
        values, coef = inputs
        values = values.astype(jnp.float32)
        coef = coef.astype(jnp.float32)
        padded = jnp.pad(values, ((0, 0), (0, 0), (1, 1), (1, 1)))
        cpad = jnp.pad(coef, ((0, 0), (1, 1), (1, 1)))
        centre = padded[:, 1:-1, 1:-1, 1:-1]
        ccen = cpad[1:-1, 1:-1, 1:-1]
        shifts = [
            (slice(2, None), slice(1, -1), slice(1, -1)),
            (slice(0, -2), slice(1, -1), slice(1, -1)),
            (slice(1, -1), slice(2, None), slice(1, -1)),
            (slice(1, -1), slice(0, -2), slice(1, -1)),
            (slice(1, -1), slice(1, -1), slice(2, None)),
            (slice(1, -1), slice(1, -1), slice(0, -2)),
        ]
        for sx, sy, sz in shifts:
            face = 0.5 * (ccen + cpad[sx, sy, sz])
            total = total + face[None] * (centre - padded[:, sx, sy, sz])
        return (total, None)

    own = mixed_ext.shape[1]
    shape = (own, mixed_ext.shape[2] - 2) + mixed_ext.shape[3:]
    start = jnp.zeros(shape, jnp.float32)
    total, unused = lax.scan(step, start, (mixed_ext, coef_ext[:, 0]))
    return total.astype(jnp.bfloat16)


def body(field, coupling, coefs):
    coef_five = coefs[:, None]
    field_ext, coef_ext = (
        padded_2(field[None], (("grid", 2),), 1),
        padded_2(coef_five, (("grid", 2),), 1),
    )
    whole = lax.all_gather(field_ext[0], "mode", axis=0, tiled=True)
    mixed_ext = mix_modes(coupling, whole)
    return stencil_sum(mixed_ext, coef_ext)


def solution(mesh):
    in_specs = (P("mode", "grid", None, None), P(None, "mode", None), P(None, "grid", None, None))
    out_specs = P("mode", "grid", None, None)
    return jax.shard_map(body, mesh=mesh, in_specs=in_specs, out_specs=out_specs, check_vma=False)
```

profile of v0, /device:TPU:27, one launch (start us, length us, event | category | flops | bytes accessed | tf_op | source)
XLA Modules:
  0.0 340.9 jit_solution(9144782742739697266)
XLA Ops:
  7.6 3.1 collective-permute-start.2
  10.8 2.2 collective-permute-start.3
  12.9 4.5 %collective-permute-done.2 = bf16[1,144,1,8,128]{4,3,2,0,1:T(8,128)(2,1)S(1)} collective-permute-done((bf16[1,144,1,8,128]{4,3,2,0,1:T(8,128)(2,1)S(1)}, bf16[1,144,1,8,128]{4,3,2,0,1:T(8,128)(2,1)S(1)}, u32[]{:S(2)}, u32[]{:S(2)}) %collective-permute-start.2) | collective-permute-done | bytes 294944 | tf_op jit(solution)/shard_map/ppermute | solution.py:12
  17.4 7.3 %collective-permute-done.3 = bf16[1,144,1,8,128]{4,3,2,0,1:T(8,128)(2,1)S(1)} collective-permute-done((bf16[1,144,1,8,128]{4,3,2,0,1:T(8,128)(2,1)S(1)}, bf16[1,144,1,8,128]{4,3,2,0,1:T(8,128)(2,1)S(1)}, u32[]{:S(2)}, u32[]{:S(2)}) %collective-permute-start.3) | collective-permute-done | bytes 294944 | tf_op jit(solution)/shard_map/ppermute | solution.py:15
  24.7 3.2 pad_maximum_fusion
  29.3 4.0 %collective-permute-start = (bf16[11,1,1,8,128]{4,3,2,0,1:T(8,128)(2,1)}, bf16[11,1,1,8,128]{4,3,2,0,1:T(8,128)(2,1)}, u32[]{:S(2)}, u32[]{:S(2)}) collective-permute-start(bf16[11,1,1,8,128]{4,3,2,0,1:T(8,128)(2,1)} %get-tuple-element.127), channel_id=1, source_target_pairs={{0,2},{2,4},{4,6},{6,8},{8,10},{10,12},{12,14},{14,16},{16,18},{18... | collective-permute-start | bytes 67592 | tf_op jit(solution)/shard_map/ppermute | solution.py:12
  33.3 1.9 collective-permute-start.1
  35.3 3.8 %collective-permute-done.1 = bf16[11,1,1,8,128]{4,3,2,0,1:T(8,128)(2,1)} collective-permute-done((bf16[11,1,1,8,128]{4,3,2,0,1:T(8,128)(2,1)}, bf16[11,1,1,8,128]{4,3,2,0,1:T(8,128)(2,1)}, u32[]{:S(2)}, u32[]{:S(2)}) %collective-permute-start.1) | collective-permute-done | bytes 22560 | tf_op jit(solution)/shard_map/ppermute | solution.py:15
  39.1 1.6 maximum_bitcast_fusion
  40.8 3.4 all-gather.3.cloned.1.call-done
  44.1 13.7 %copy.7 = bf16[36,8,64,128]{3,1,2,0:T(8,128)(2,1)} copy(bf16[36,8,64,128]{3,2,1,0:T(8,128)(2,1)} %bitcast.68) | data formatting | bytes 9437184
  57.8 57.4 %while.23 = (s32[]{:T(128)}, bf16[11,144,8192]{2,1,0:T(8,128)(2,1)}, bf16[11,144,288]{2,1,0:T(8,128)(2,1)}, bf16[288,8192]{1,0:T(8,128)(2,1)}, s32[]{:T(128)}) while((s32[]{:T(128)}, bf16[11,144,8192]{2,1,0:T(8,128)(2,1)}, bf16[11,144,288]{2,1,0:T(8,128)(2,1)}, bf16[288,8192]{1,0:T(8,128)(2,1)}, s32[]{:T(128)}) %tuple.66), condition=%wide.region_1.2_spmd, body=%wide.region_0.1_spmd.sunk | while | flops 680656896 | bytes 7189565 | solution.py:27
  57.8 5.2 %fusion.44 = bf16[11,144,8192]{2,1,0:T(8,128)(2,1)} fusion(bf16[11,144,8192]{2,1,0:T(8,128)(2,1)} %get-tuple-element.201, s32[]{:T(128)} %get-tuple-element.200, bf16[288,8192]{1,0:T(8,128)(2,1)} %get-tuple-element.208, bf16[11,144,288]{2,1,0:T(8,128)(2,1)} %get-tuple-element.207), kind=kOutput, calls=%fused_computation.2.clone.1 | convolution fusion | flops 680656896 | bytes 7189504 | tf_op jit(solution)/shard_map/while/body/eval_jaxpr/dot_general | solution.py:25
  63.0 5.3 %fusion.44 = bf16[11,144,8192]{2,1,0:T(8,128)(2,1)} fusion(bf16[11,144,8192]{2,1,0:T(8,128)(2,1)} %get-tuple-element.201, s32[]{:T(128)} %get-tuple-element.200, bf16[288,8192]{1,0:T(8,128)(2,1)} %get-tuple-element.208, bf16[11,144,288]{2,1,0:T(8,128)(2,1)} %get-tuple-element.207), kind=kOutput, calls=%fused_computation.2.clone.1 | convolution fusion | flops 680656896 | bytes 7189504 | tf_op jit(solution)/shard_map/while/body/eval_jaxpr/dot_general | solution.py:25
  68.3 5.2 %fusion.44 = bf16[11,144,8192]{2,1,0:T(8,128)(2,1)} fusion(bf16[11,144,8192]{2,1,0:T(8,128)(2,1)} %get-tuple-element.201, s32[]{:T(128)} %get-tuple-element.200, bf16[288,8192]{1,0:T(8,128)(2,1)} %get-tuple-element.208, bf16[11,144,288]{2,1,0:T(8,128)(2,1)} %get-tuple-element.207), kind=kOutput, calls=%fused_computation.2.clone.1 | convolution fusion | flops 680656896 | bytes 7189504 | tf_op jit(solution)/shard_map/while/body/eval_jaxpr/dot_general | solution.py:25
  73.5 5.2 %fusion.44 = bf16[11,144,8192]{2,1,0:T(8,128)(2,1)} fusion(bf16[11,144,8192]{2,1,0:T(8,128)(2,1)} %get-tuple-element.201, s32[]{:T(128)} %get-tuple-element.200, bf16[288,8192]{1,0:T(8,128)(2,1)} %get-tuple-element.208, bf16[11,144,288]{2,1,0:T(8,128)(2,1)} %get-tuple-element.207), kind=kOutput, calls=%fused_computation.2.clone.1 | convolution fusion | flops 680656896 | bytes 7189504 | tf_op jit(solution)/shard_map/while/body/eval_jaxpr/dot_general | solution.py:25
  78.7 5.3 %fusion.44 = bf16[11,144,8192]{2,1,0:T(8,128)(2,1)} fusion(bf16[11,144,8192]{2,1,0:T(8,128)(2,1)} %get-tuple-element.201, s32[]{:T(128)} %get-tuple-element.200, bf16[288,8192]{1,0:T(8,128)(2,1)} %get-tuple-element.208, bf16[11,144,288]{2,1,0:T(8,128)(2,1)} %get-tuple-element.207), kind=kOutput, calls=%fused_computation.2.clone.1 | convolution fusion | flops 680656896 | bytes 7189504 | tf_op jit(solution)/shard_map/while/body/eval_jaxpr/dot_general | solution.py:25
  83.9 5.2 %fusion.44 = bf16[11,144,8192]{2,1,0:T(8,128)(2,1)} fusion(bf16[11,144,8192]{2,1,0:T(8,128)(2,1)} %get-tuple-element.201, s32[]{:T(128)} %get-tuple-element.200, bf16[288,8192]{1,0:T(8,128)(2,1)} %get-tuple-element.208, bf16[11,144,288]{2,1,0:T(8,128)(2,1)} %get-tuple-element.207), kind=kOutput, calls=%fused_computation.2.clone.1 | convolution fusion | flops 680656896 | bytes 7189504 | tf_op jit(solution)/shard_map/while/body/eval_jaxpr/dot_general | solution.py:25
  89.1 5.2 %fusion.44 = bf16[11,144,8192]{2,1,0:T(8,128)(2,1)} fusion(bf16[11,144,8192]{2,1,0:T(8,128)(2,1)} %get-tuple-element.201, s32[]{:T(128)} %get-tuple-element.200, bf16[288,8192]{1,0:T(8,128)(2,1)} %get-tuple-element.208, bf16[11,144,288]{2,1,0:T(8,128)(2,1)} %get-tuple-element.207), kind=kOutput, calls=%fused_computation.2.clone.1 | convolution fusion | flops 680656896 | bytes 7189504 | tf_op jit(solution)/shard_map/while/body/eval_jaxpr/dot_general | solution.py:25
  94.4 5.2 %fusion.44 = bf16[11,144,8192]{2,1,0:T(8,128)(2,1)} fusion(bf16[11,144,8192]{2,1,0:T(8,128)(2,1)} %get-tuple-element.201, s32[]{:T(128)} %get-tuple-element.200, bf16[288,8192]{1,0:T(8,128)(2,1)} %get-tuple-element.208, bf16[11,144,288]{2,1,0:T(8,128)(2,1)} %get-tuple-element.207), kind=kOutput, calls=%fused_computation.2.clone.1 | convolution fusion | flops 680656896 | bytes 7189504 | tf_op jit(solution)/shard_map/while/body/eval_jaxpr/dot_general | solution.py:25
  99.6 5.3 %fusion.44 = bf16[11,144,8192]{2,1,0:T(8,128)(2,1)} fusion(bf16[11,144,8192]{2,1,0:T(8,128)(2,1)} %get-tuple-element.201, s32[]{:T(128)} %get-tuple-element.200, bf16[288,8192]{1,0:T(8,128)(2,1)} %get-tuple-element.208, bf16[11,144,288]{2,1,0:T(8,128)(2,1)} %get-tuple-element.207), kind=kOutput, calls=%fused_computation.2.clone.1 | convolution fusion | flops 680656896 | bytes 7189504 | tf_op jit(solution)/shard_map/while/body/eval_jaxpr/dot_general | solution.py:25
  104.9 5.2 %fusion.44 = bf16[11,144,8192]{2,1,0:T(8,128)(2,1)} fusion(bf16[11,144,8192]{2,1,0:T(8,128)(2,1)} %get-tuple-element.201, s32[]{:T(128)} %get-tuple-element.200, bf16[288,8192]{1,0:T(8,128)(2,1)} %get-tuple-element.208, bf16[11,144,288]{2,1,0:T(8,128)(2,1)} %get-tuple-element.207), kind=kOutput, calls=%fused_computation.2.clone.1 | convolution fusion | flops 680656896 | bytes 7189504 | tf_op jit(solution)/shard_map/while/body/eval_jaxpr/dot_general | solution.py:25
  110.0 5.2 %fusion.44 = bf16[11,144,8192]{2,1,0:T(8,128)(2,1)} fusion(bf16[11,144,8192]{2,1,0:T(8,128)(2,1)} %get-tuple-element.201, s32[]{:T(128)} %get-tuple-element.200, bf16[288,8192]{1,0:T(8,128)(2,1)} %get-tuple-element.208, bf16[11,144,288]{2,1,0:T(8,128)(2,1)} %get-tuple-element.207), kind=kOutput, calls=%fused_computation.2.clone.1 | convolution fusion | flops 680656896 | bytes 7189504 | tf_op jit(solution)/shard_map/while/body/eval_jaxpr/dot_general | solution.py:25
  115.2 23.1 %copy.5 = bf16[198,8,64,128]{3,2,1,0:T(8,128)(2,1)} copy(bf16[198,8,64,128]{3,1,2,0:T(8,128)(2,1)} %bitcast.67) | data formatting | bytes 51904512
  138.3 194.4 %while.24 = (s32[]{:T(128)}, f32[144,6,8,128]{3,2,1,0:T(8,128)S(1)}, bf16[11,8,8,128]{3,2,1,0:T(8,128)(2,1)}, bf16[11,144,8,8,128]{4,3,2,1,0:T(8,128)(2,1)}, s32[]{:T(128)}, /*index=5*/s32[]{:T(128)}) while((s32[]{:T(128)}, f32[144,6,8,128]{3,2,1,0:T(8,128)S(1)}, bf16[11,8,8,128]{3,2,1,0:T(8,128)(2,1)}, ...), condition=%wide.region_3.4_spmd.clone, body=%wide.region_2.3_spmd.clone.sunk | while | flops 18071556 | bytes 29974612 | solution.py:57
  139.7 4.4 %bitcast_convert_fusion.2 = f32[144,8,8,128]{3,2,1,0:T(8,128)} fusion(bf16[11,144,8,8,128]{4,3,2,1,0:T(8,128)(2,1)} %get-tuple-element.225, s32[]{:T(128)} %get-tuple-element.216), kind=kLoop, calls=%fused_computation.28.clone.1 | loop fusion | flops 1179648 | bytes 7077892 | tf_op jit(solution)/shard_map/while/body/eval_jaxpr/convert_element_type | solution.py:35
  144.2 11.8 %fusion.46 = f32[144,6,8,128]{3,2,1,0:T(8,128)S(1)} fusion(f32[144,8,8,128]{3,2,1,0:T(8,128)} %bitcast_convert_fusion.2, f32[144,6,8,128]{3,2,1,0:T(8,128)S(1)} %get-tuple-element.217, f32[6,8,128]{2,1,0:T(8,128)} %get-tuple-element.189, f32[6,8,128]{2,1,0:T(8,128)} %get-tuple-element.190, f32[6,8,128]{2,1,0:T(8,128)} %get-tuple-element.191, ...), kind=kLoop, calls=%fused_computation.15.clone.1 | loop fusion | flops 16809984 | bytes 22560768 | tf_op jit(solution)/shard_map/while/body/eval_jaxpr/add | solution.py:51
  157.4 4.4 %bitcast_convert_fusion.2 = f32[144,8,8,128]{3,2,1,0:T(8,128)} fusion(bf16[11,144,8,8,128]{4,3,2,1,0:T(8,128)(2,1)} %get-tuple-element.225, s32[]{:T(128)} %get-tuple-element.216), kind=kLoop, calls=%fused_computation.28.clone.1 | loop fusion | flops 1179648 | bytes 7077892 | tf_op jit(solution)/shard_map/while/body/eval_jaxpr/convert_element_type | solution.py:35
  161.8 11.8 %fusion.46 = f32[144,6,8,128]{3,2,1,0:T(8,128)S(1)} fusion(f32[144,8,8,128]{3,2,1,0:T(8,128)} %bitcast_convert_fusion.2, f32[144,6,8,128]{3,2,1,0:T(8,128)S(1)} %get-tuple-element.217, f32[6,8,128]{2,1,0:T(8,128)} %get-tuple-element.189, f32[6,8,128]{2,1,0:T(8,128)} %get-tuple-element.190, f32[6,8,128]{2,1,0:T(8,128)} %get-tuple-element.191, ...), kind=kLoop, calls=%fused_computation.15.clone.1 | loop fusion | flops 16809984 | bytes 22560768 | tf_op jit(solution)/shard_map/while/body/eval_jaxpr/add | solution.py:51
  175.1 4.4 %bitcast_convert_fusion.2 = f32[144,8,8,128]{3,2,1,0:T(8,128)} fusion(bf16[11,144,8,8,128]{4,3,2,1,0:T(8,128)(2,1)} %get-tuple-element.225, s32[]{:T(128)} %get-tuple-element.216), kind=kLoop, calls=%fused_computation.28.clone.1 | loop fusion | flops 1179648 | bytes 7077892 | tf_op jit(solution)/shard_map/while/body/eval_jaxpr/convert_element_type | solution.py:35
  179.5 11.8 %fusion.46 = f32[144,6,8,128]{3,2,1,0:T(8,128)S(1)} fusion(f32[144,8,8,128]{3,2,1,0:T(8,128)} %bitcast_convert_fusion.2, f32[144,6,8,128]{3,2,1,0:T(8,128)S(1)} %get-tuple-element.217, f32[6,8,128]{2,1,0:T(8,128)} %get-tuple-element.189, f32[6,8,128]{2,1,0:T(8,128)} %get-tuple-element.190, f32[6,8,128]{2,1,0:T(8,128)} %get-tuple-element.191, ...), kind=kLoop, calls=%fused_computation.15.clone.1 | loop fusion | flops 16809984 | bytes 22560768 | tf_op jit(solution)/shard_map/while/body/eval_jaxpr/add | solution.py:51
  192.7 4.4 %bitcast_convert_fusion.2 = f32[144,8,8,128]{3,2,1,0:T(8,128)} fusion(bf16[11,144,8,8,128]{4,3,2,1,0:T(8,128)(2,1)} %get-tuple-element.225, s32[]{:T(128)} %get-tuple-element.216), kind=kLoop, calls=%fused_computation.28.clone.1 | loop fusion | flops 1179648 | bytes 7077892 | tf_op jit(solution)/shard_map/while/body/eval_jaxpr/convert_element_type | solution.py:35
  197.2 11.8 %fusion.46 = f32[144,6,8,128]{3,2,1,0:T(8,128)S(1)} fusion(f32[144,8,8,128]{3,2,1,0:T(8,128)} %bitcast_convert_fusion.2, f32[144,6,8,128]{3,2,1,0:T(8,128)S(1)} %get-tuple-element.217, f32[6,8,128]{2,1,0:T(8,128)} %get-tuple-element.189, f32[6,8,128]{2,1,0:T(8,128)} %get-tuple-element.190, f32[6,8,128]{2,1,0:T(8,128)} %get-tuple-element.191, ...), kind=kLoop, calls=%fused_computation.15.clone.1 | loop fusion | flops 16809984 | bytes 22560768 | tf_op jit(solution)/shard_map/while/body/eval_jaxpr/add | solution.py:51
  210.4 4.4 %bitcast_convert_fusion.2 = f32[144,8,8,128]{3,2,1,0:T(8,128)} fusion(bf16[11,144,8,8,128]{4,3,2,1,0:T(8,128)(2,1)} %get-tuple-element.225, s32[]{:T(128)} %get-tuple-element.216), kind=kLoop, calls=%fused_computation.28.clone.1 | loop fusion | flops 1179648 | bytes 7077892 | tf_op jit(solution)/shard_map/while/body/eval_jaxpr/convert_element_type | solution.py:35
  214.9 11.8 %fusion.46 = f32[144,6,8,128]{3,2,1,0:T(8,128)S(1)} fusion(f32[144,8,8,128]{3,2,1,0:T(8,128)} %bitcast_convert_fusion.2, f32[144,6,8,128]{3,2,1,0:T(8,128)S(1)} %get-tuple-element.217, f32[6,8,128]{2,1,0:T(8,128)} %get-tuple-element.189, f32[6,8,128]{2,1,0:T(8,128)} %get-tuple-element.190, f32[6,8,128]{2,1,0:T(8,128)} %get-tuple-element.191, ...), kind=kLoop, calls=%fused_computation.15.clone.1 | loop fusion | flops 16809984 | bytes 22560768 | tf_op jit(solution)/shard_map/while/body/eval_jaxpr/add | solution.py:51
  228.1 4.4 %bitcast_convert_fusion.2 = f32[144,8,8,128]{3,2,1,0:T(8,128)} fusion(bf16[11,144,8,8,128]{4,3,2,1,0:T(8,128)(2,1)} %get-tuple-element.225, s32[]{:T(128)} %get-tuple-element.216), kind=kLoop, calls=%fused_computation.28.clone.1 | loop fusion | flops 1179648 | bytes 7077892 | tf_op jit(solution)/shard_map/while/body/eval_jaxpr/convert_element_type | solution.py:35
  232.5 11.8 %fusion.46 = f32[144,6,8,128]{3,2,1,0:T(8,128)S(1)} fusion(f32[144,8,8,128]{3,2,1,0:T(8,128)} %bitcast_convert_fusion.2, f32[144,6,8,128]{3,2,1,0:T(8,128)S(1)} %get-tuple-element.217, f32[6,8,128]{2,1,0:T(8,128)} %get-tuple-element.189, f32[6,8,128]{2,1,0:T(8,128)} %get-tuple-element.190, f32[6,8,128]{2,1,0:T(8,128)} %get-tuple-element.191, ...), kind=kLoop, calls=%fused_computation.15.clone.1 | loop fusion | flops 16809984 | bytes 22560768 | tf_op jit(solution)/shard_map/while/body/eval_jaxpr/add | solution.py:51
  245.7 4.4 %bitcast_convert_fusion.2 = f32[144,8,8,128]{3,2,1,0:T(8,128)} fusion(bf16[11,144,8,8,128]{4,3,2,1,0:T(8,128)(2,1)} %get-tuple-element.225, s32[]{:T(128)} %get-tuple-element.216), kind=kLoop, calls=%fused_computation.28.clone.1 | loop fusion | flops 1179648 | bytes 7077892 | tf_op jit(solution)/shard_map/while/body/eval_jaxpr/convert_element_type | solution.py:35
  250.2 11.8 %fusion.46 = f32[144,6,8,128]{3,2,1,0:T(8,128)S(1)} fusion(f32[144,8,8,128]{3,2,1,0:T(8,128)} %bitcast_convert_fusion.2, f32[144,6,8,128]{3,2,1,0:T(8,128)S(1)} %get-tuple-element.217, f32[6,8,128]{2,1,0:T(8,128)} %get-tuple-element.189, f32[6,8,128]{2,1,0:T(8,128)} %get-tuple-element.190, f32[6,8,128]{2,1,0:T(8,128)} %get-tuple-element.191, ...), kind=kLoop, calls=%fused_computation.15.clone.1 | loop fusion | flops 16809984 | bytes 22560768 | tf_op jit(solution)/shard_map/while/body/eval_jaxpr/add | solution.py:51
  263.4 4.4 %bitcast_convert_fusion.2 = f32[144,8,8,128]{3,2,1,0:T(8,128)} fusion(bf16[11,144,8,8,128]{4,3,2,1,0:T(8,128)(2,1)} %get-tuple-element.225, s32[]{:T(128)} %get-tuple-element.216), kind=kLoop, calls=%fused_computation.28.clone.1 | loop fusion | flops 1179648 | bytes 7077892 | tf_op jit(solution)/shard_map/while/body/eval_jaxpr/convert_element_type | solution.py:35
  267.9 11.8 %fusion.46 = f32[144,6,8,128]{3,2,1,0:T(8,128)S(1)} fusion(f32[144,8,8,128]{3,2,1,0:T(8,128)} %bitcast_convert_fusion.2, f32[144,6,8,128]{3,2,1,0:T(8,128)S(1)} %get-tuple-element.217, f32[6,8,128]{2,1,0:T(8,128)} %get-tuple-element.189, f32[6,8,128]{2,1,0:T(8,128)} %get-tuple-element.190, f32[6,8,128]{2,1,0:T(8,128)} %get-tuple-element.191, ...), kind=kLoop, calls=%fused_computation.15.clone.1 | loop fusion | flops 16809984 | bytes 22560768 | tf_op jit(solution)/shard_map/while/body/eval_jaxpr/add | solution.py:51
  281.1 4.4 %bitcast_convert_fusion.2 = f32[144,8,8,128]{3,2,1,0:T(8,128)} fusion(bf16[11,144,8,8,128]{4,3,2,1,0:T(8,128)(2,1)} %get-tuple-element.225, s32[]{:T(128)} %get-tuple-element.216), kind=kLoop, calls=%fused_computation.28.clone.1 | loop fusion | flops 1179648 | bytes 7077892 | tf_op jit(solution)/shard_map/while/body/eval_jaxpr/convert_element_type | solution.py:35
  285.5 11.8 %fusion.46 = f32[144,6,8,128]{3,2,1,0:T(8,128)S(1)} fusion(f32[144,8,8,128]{3,2,1,0:T(8,128)} %bitcast_convert_fusion.2, f32[144,6,8,128]{3,2,1,0:T(8,128)S(1)} %get-tuple-element.217, f32[6,8,128]{2,1,0:T(8,128)} %get-tuple-element.189, f32[6,8,128]{2,1,0:T(8,128)} %get-tuple-element.190, f32[6,8,128]{2,1,0:T(8,128)} %get-tuple-element.191, ...), kind=kLoop, calls=%fused_computation.15.clone.1 | loop fusion | flops 16809984 | bytes 22560768 | tf_op jit(solution)/shard_map/while/body/eval_jaxpr/add | solution.py:51
  298.8 4.4 %bitcast_convert_fusion.2 = f32[144,8,8,128]{3,2,1,0:T(8,128)} fusion(bf16[11,144,8,8,128]{4,3,2,1,0:T(8,128)(2,1)} %get-tuple-element.225, s32[]{:T(128)} %get-tuple-element.216), kind=kLoop, calls=%fused_computation.28.clone.1 | loop fusion | flops 1179648 | bytes 7077892 | tf_op jit(solution)/shard_map/while/body/eval_jaxpr/convert_element_type | solution.py:35
  303.2 11.8 %fusion.46 = f32[144,6,8,128]{3,2,1,0:T(8,128)S(1)} fusion(f32[144,8,8,128]{3,2,1,0:T(8,128)} %bitcast_convert_fusion.2, f32[144,6,8,128]{3,2,1,0:T(8,128)S(1)} %get-tuple-element.217, f32[6,8,128]{2,1,0:T(8,128)} %get-tuple-element.189, f32[6,8,128]{2,1,0:T(8,128)} %get-tuple-element.190, f32[6,8,128]{2,1,0:T(8,128)} %get-tuple-element.191, ...), kind=kLoop, calls=%fused_computation.15.clone.1 | loop fusion | flops 16809984 | bytes 22560768 | tf_op jit(solution)/shard_map/while/body/eval_jaxpr/add | solution.py:51
  316.4 4.4 %bitcast_convert_fusion.2 = f32[144,8,8,128]{3,2,1,0:T(8,128)} fusion(bf16[11,144,8,8,128]{4,3,2,1,0:T(8,128)(2,1)} %get-tuple-element.225, s32[]{:T(128)} %get-tuple-element.216), kind=kLoop, calls=%fused_computation.28.clone.1 | loop fusion | flops 1179648 | bytes 7077892 | tf_op jit(solution)/shard_map/while/body/eval_jaxpr/convert_element_type | solution.py:35
  320.9 11.8 %fusion.46 = f32[144,6,8,128]{3,2,1,0:T(8,128)S(1)} fusion(f32[144,8,8,128]{3,2,1,0:T(8,128)} %bitcast_convert_fusion.2, f32[144,6,8,128]{3,2,1,0:T(8,128)S(1)} %get-tuple-element.217, f32[6,8,128]{2,1,0:T(8,128)} %get-tuple-element.189, f32[6,8,128]{2,1,0:T(8,128)} %get-tuple-element.190, f32[6,8,128]{2,1,0:T(8,128)} %get-tuple-element.191, ...), kind=kLoop, calls=%fused_computation.15.clone.1 | loop fusion | flops 16809984 | bytes 22560768 | tf_op jit(solution)/shard_map/while/body/eval_jaxpr/add | solution.py:51
  332.7 1.4 convert_element_type.30
  (29 shorter events, 18.3 us)
Async XLA Ops:
  6.5 37.6 %all-gather.3.cloned.1.call-start = ((), (), s32[]{:S(2)}) async-start(), calls=%async_computation | async-start | bytes 7077888 | tf_op jit(solution)/shard_map/all_gather | solution.py:67
  7.6 9.8 %collective-permute-start.2 = (bf16[1,144,1,8,128]{4,3,2,0,1:T(8,128)(2,1)S(1)}, bf16[1,144,1,8,128]{4,3,2,0,1:T(8,128)(2,1)S(1)}, u32[]{:S(2)}, u32[]{:S(2)}) collective-permute-start(bf16[1,144,1,8,128]{4,3,2,0,1:T(8,128)(2,1)S(1)} %get-tuple-element.125), channel_id=1, source_target_pairs={{0,2},{2,4},{4,6},{6,8},{8,10},{10,12},{12,14},{14,16},{16,18},{18... | collective-permute-start | bytes 884744 | tf_op jit(solution)/shard_map/ppermute | solution.py:12
  10.8 13.9 %collective-permute-start.3 = (bf16[1,144,1,8,128]{4,3,2,0,1:T(8,128)(2,1)S(1)}, bf16[1,144,1,8,128]{4,3,2,0,1:T(8,128)(2,1)S(1)}, u32[]{:S(2)}, u32[]{:S(2)}) collective-permute-start(bf16[1,144,1,8,128]{4,3,2,0,1:T(8,128)(2,1)S(1)} %get-tuple-element.126), channel_id=1, source_target_pairs={{2,0},{4,2},{6,4},{8,6},{10,8},{12,10},{14,12},{16,14},{18,16},{20... | collective-permute-start | bytes 884744 | tf_op jit(solution)/shard_map/ppermute | solution.py:15
  29.3 6.0 %collective-permute-start = (bf16[11,1,1,8,128]{4,3,2,0,1:T(8,128)(2,1)}, bf16[11,1,1,8,128]{4,3,2,0,1:T(8,128)(2,1)}, u32[]{:S(2)}, u32[]{:S(2)}) collective-permute-start(bf16[11,1,1,8,128]{4,3,2,0,1:T(8,128)(2,1)} %get-tuple-element.127), channel_id=1, source_target_pairs={{0,2},{2,4},{4,6},{6,8},{8,10},{10,12},{12,14},{14,16},{16,18},{18... | collective-permute-start | bytes 67592 | tf_op jit(solution)/shard_map/ppermute | solution.py:12
  33.3 5.8 %collective-permute-start.1 = (bf16[11,1,1,8,128]{4,3,2,0,1:T(8,128)(2,1)}, bf16[11,1,1,8,128]{4,3,2,0,1:T(8,128)(2,1)}, u32[]{:S(2)}, u32[]{:S(2)}) collective-permute-start(bf16[11,1,1,8,128]{4,3,2,0,1:T(8,128)(2,1)} %get-tuple-element.128), channel_id=1, source_target_pairs={{2,0},{4,2},{6,4},{8,6},{10,8},{12,10},{14,12},{16,14},{18,16},{20... | collective-permute-start | bytes 67592 | tf_op jit(solution)/shard_map/ppermute | solution.py:15
Sparse Core Ops, SparseCore 0:
  28.1 16.0 all-gather.2
where the time goes:
time: 344 us; the launch traced here: 341 us
  other arithmetic  200 us (58%)
  matrix products  57.4 us (17%)
  local copies, waits for them, and re-layouts  39.3 us (11%)
  waiting for transfers between devices  18.9 us (5%)
  between operations  13.5 us (4%)
  starting transfers between devices  11.2 us (3%)
    add x11, other arithmetic, step(): total = total + face[None] * (centre - padded[:, sx, sy, sz])  129 us
    dot_general x11, matrix products, one_term(): jnp.dot(weights, flat, preferred_element_type=jnp.float32)  57.4 us
    convert_element_type x11, other arithmetic, step(): values = values.astype(jnp.float32)  48.9 us
    unnamed x2, local copies, waits for them, and re-layouts  36.8 us
    ppermute x2, waiting for transfers between devices, padded_2(): lax.ppermute(lax.slice_in_dim(block, 0, width, axis=dim), axis, backward)  11.1 us
    convert_element_type x11, other arithmetic, step(): coef = coef.astype(jnp.float32)  8 us
    mul x11, other arithmetic, step(): face = 0.5 * (ccen + cpad[sx, sy, sz])  7.78 us
    ppermute x2, starting transfers between devices, padded_2(): lax.ppermute(lax.slice_in_dim(block, block.shape[dim] - width, None, axis...  7.15 us
  transfers between devices with their start and end apart: 5, of which 4 were waited for; matrix products, arithmetic and copies ran while one was open for 1% of the time, Pallas kernels for 0%

commit v1 on v0

v1 whole, which is shorter than its diff:
```python
import functools

import jax
import jax.numpy as jnp
from jax import lax
from jax.experimental import pallas as pl
from jax.experimental.pallas import tpu as pltpu
from jax.sharding import PartitionSpec as P

BF16 = jnp.bfloat16
F32 = jnp.float32
SIDES = 6
VMEM_LIMIT = 60 * 2**20


def up(n, m):
    return -(-n // m) * m


def chunk_of(blocks):
    return next(c for c in (3, 2, 1) if blocks % c == 0)


def turn_kernel(f_ref, o_ref, lo_ref, hi_ref, s_ref):
    x = pl.program_id(0)
    modes, _, ny, nz = f_ref.shape
    padded = o_ref.shape[2]
    s_ref[...] = f_ref[:, 0].astype(F32).reshape(modes * ny, nz)
    for y in range(ny):
        rows = s_ref[pl.ds(y, modes, stride=ny), :].astype(BF16)
        if padded > modes:
            rows = jnp.concatenate([rows, jnp.zeros((padded - modes, nz), BF16)], axis=0)
        o_ref[0, y] = rows

    @pl.when(x == 0)
    def _():
        lo_ref[...] = o_ref[0]

    @pl.when(x == pl.num_programs(0) - 1)
    def _():
        hi_ref[...] = o_ref[0]


def turn(field):
    modes, nx, ny, nz = field.shape
    padded = up(modes, 16)
    layer = jax.ShapeDtypeStruct((ny, padded, nz), BF16)
    return pl.pallas_call(
        turn_kernel,
        grid=(nx,),
        in_specs=[pl.BlockSpec((modes, 1, ny, nz), lambda x: (0, x, 0, 0))],
        out_specs=[
            pl.BlockSpec((1, ny, padded, nz), lambda x: (x, 0, 0, 0)),
            pl.BlockSpec((ny, padded, nz), lambda x: (0, 0, 0)),
            pl.BlockSpec((ny, padded, nz), lambda x: (0, 0, 0)),
        ],
        out_shape=[jax.ShapeDtypeStruct((nx, ny, padded, nz), BF16), layer, layer],
        scratch_shapes=[pltpu.VMEM((modes * ny, nz), F32)],
        compiler_params=pltpu.CompilerParams(vmem_limit_bytes=VMEM_LIMIT),
        name="turn",
    )(field)


def main_kernel(sources, *refs):
    w_ref, a_ref = refs[:2]
    f_hbm = refs[2:2 + sources]
    out_hbm, base_hbm = refs[2 + sources:4 + sources]
    f_ref, ta, tb, face, rep, acc, obuf, fsem, osem, bsem = refs[4 + sources:]
    terms, nx, ny, nz = a_ref.shape
    padded = f_ref.shape[3]
    outs = obuf.shape[1]
    step = 16 * chunk_of(padded // 16)
    zero = jnp.zeros((ny, padded, nz), BF16)
    for s in range(sources):
        f_ref[s, 0] = zero
        f_ref[s, nx + 1] = zero

    def load(s, x):
        return pltpu.make_async_copy(f_hbm[s].at[x], f_ref.at[s, x + 1], fsem.at[s, x])

    for x in range(nx):
        for s in range(sources):
            load(s, x).start()
    for s in range(sources):
        load(s, 0).wait()

    def write(x, slot):
        return pltpu.make_async_copy(obuf.at[slot], out_hbm.at[:, x], osem.at[slot])

    def write_base(side):
        return pltpu.make_async_copy(acc.at[side], base_hbm.at[side], bsem.at[side])

    lane = lax.broadcasted_iota(jnp.int32, (ny, nz), 1)
    row = lax.broadcasted_iota(jnp.int32, (ny, nz), 0)

    def faces(x):
        for k in range(terms):
            a = a_ref[k, x].astype(F32)
            before = a_ref[k, jnp.maximum(x - 1, 0)].astype(F32)
            after = a_ref[k, jnp.minimum(x + 1, nx - 1)].astype(F32)
            face[0 * terms + k] = jnp.where(x > 0, 0.5 * (a + before), 0.0)
            face[1 * terms + k] = jnp.where(x < nx - 1, 0.5 * (a + after), 0.0)
            face[2 * terms + k] = 0.5 * (a + jnp.where(row > 0, pltpu.roll(a, 1, 0), 0.0))
            face[3 * terms + k] = 0.5 * (a + jnp.where(row < ny - 1, pltpu.roll(a, ny - 1, 0), 0.0))
            face[4 * terms + k] = 0.5 * (a + jnp.where(lane > 0, pltpu.roll(a, 1, 1), 0.0))
            face[5 * terms + k] = 0.5 * (a + jnp.where(lane < nz - 1, pltpu.roll(a, nz - 1, 1), 0.0))

    def differences(s, x, y, q):
        def at(x, y):
            return f_ref[s, x, y, pl.ds(q, step), :]

        here = at(x + 1, y)
        wide = here.astype(F32)
        lanes = lax.broadcasted_iota(jnp.int32, wide.shape, 1)
        zm = jnp.where(lanes > 0, pltpu.roll(wide, 1, 1), 0.0)
        zp = jnp.where(lanes < nz - 1, pltpu.roll(wide, nz - 1, 1), 0.0)
        return (
            here - at(x, y),
            here - at(x + 2, y),
            here - at(x + 1, y - 1) if y > 0 else here,
            here - at(x + 1, y + 1) if y < ny - 1 else here,
            (wide - zm).astype(BF16),
            (wide - zp).astype(BF16),
        )

    def fill(t_ref, x, y, column):
        for r in range(SIDES * terms):
            rep[r] = jnp.broadcast_to(face[r, pl.ds(y, 1), :], (16, nz)).astype(BF16)
        for s in range(sources):
            for q in range(0, padded, step):
                d = [v.reshape(step // 16, 16, nz) for v in differences(s, x, y, q)]
                for k in range(terms):
                    p = [d[h] * rep[h * terms + k][None] for h in range(SIDES)]
                    t = (p[0] + p[1]) + (p[2] + p[3]) + (p[4] + p[5])
                    at = (s * terms + k) * padded + q
                    t_ref[at:at + step, column * nz:(column + 1) * nz] = t.reshape(step, nz)

    pairs = ny // 2

    def mix(t_ref, side, pair):
        r = jnp.dot(w_ref[...], t_ref[...], preferred_element_type=F32)
        acc[side, pl.ds(2 * pair, outs, stride=ny), :] = r[:, :nz]
        acc[side, pl.ds(2 * pair + 1, outs, stride=ny), :] = r[:, nz:]

    def finish(x, slot):
        obuf[slot] = acc[slot].reshape(outs, ny, nz).astype(BF16)

    bufs = (ta, tb)

    @pl.loop(0, nx)
    def _(x):
        slot = x & 1
        last = jnp.maximum(x - 1, 0)

        @pl.when(x + 1 < nx)
        def _():
            for s in range(sources):
                load(s, x + 1).wait()

        faces(x)
        for pair in range(pairs):
            t_ref, done = bufs[pair % 2], bufs[(pair + 1) % 2]
            if pair == 0:
                mix(done, last & 1, pairs - 1)
            else:
                mix(done, slot, pair - 1)
            for column in range(2):
                fill(t_ref, x, 2 * pair + column, column)
            if pair == 0:
                @pl.when(x > 0)
                def _():
                    @pl.when(x > 2)
                    def _():
                        write(x - 3, 1 - slot).wait()
                    finish(x - 1, 1 - slot)
                    write(x - 1, 1 - slot).start()

                    @pl.when(x == 1)
                    def _():
                        write_base(0).start()
                        write_base(0).wait()

    final = (nx - 1) & 1
    mix(bufs[(pairs - 1) % 2], final, pairs - 1)
    pltpu.make_async_copy(acc.at[final], base_hbm.at[1], bsem.at[1]).start()
    write(nx - 3, final).wait()
    finish(nx - 1, final)
    write(nx - 1, final).start()
    write(nx - 2, 1 - final).wait()
    write(nx - 1, final).wait()
    pltpu.make_async_copy(acc.at[final], base_hbm.at[1], bsem.at[1]).wait()


def main(weights, coefs, fields):
    terms, nx, ny, nz = coefs.shape
    outs = weights.shape[0]
    padded = fields[0].shape[2]
    sources = len(fields)
    depth = sources * terms * padded
    vmem = pl.BlockSpec(memory_space=pltpu.VMEM)
    hbm = pl.BlockSpec(memory_space=pl.ANY)
    return pl.pallas_call(
        functools.partial(main_kernel, sources),
        in_specs=[vmem, vmem] + [hbm] * sources,
        out_specs=[hbm, hbm],
        out_shape=[
            jax.ShapeDtypeStruct((outs, nx, ny, nz), BF16),
            jax.ShapeDtypeStruct((2, outs * ny, nz), F32),
        ],
        scratch_shapes=[
            pltpu.VMEM((sources, nx + 2, ny, padded, nz), BF16),
            pltpu.VMEM((depth, 2 * nz), BF16),
            pltpu.VMEM((depth, 2 * nz), BF16),
            pltpu.VMEM((SIDES * terms, ny, nz), F32),
            pltpu.VMEM((SIDES * terms, 16, nz), BF16),
            pltpu.VMEM((2, outs * ny, nz), F32),
            pltpu.VMEM((2, outs, ny, nz), BF16),
            pltpu.SemaphoreType.DMA((sources, nx)),
            pltpu.SemaphoreType.DMA((2,)),
            pltpu.SemaphoreType.DMA((2,)),
        ],
        compiler_params=pltpu.CompilerParams(vmem_limit_bytes=VMEM_LIMIT),
        cost_estimate=pl.CostEstimate(
            flops=2 * outs * depth * nx * ny * nz, bytes_accessed=8 * 2**20, transcendentals=0
        ),
        name="faces",
    )(weights, coefs, *fields)


def tail_kernel(sources, w_ref, a_ref, ah_ref, base_ref, *refs):
    f_refs = refs[:sources]
    h_refs = refs[sources:2 * sources]
    _, o_ref, t_ref, face, rep, acc = refs[2 * sources:]
    terms, _, ny, nz = a_ref.shape
    padded = t_ref.shape[0] // (sources * terms)
    outs = w_ref.shape[0]
    step = 16 * chunk_of(padded // 16)
    for k in range(terms):
        face[k] = 0.5 * (a_ref[k, 0].astype(F32) + ah_ref[0, k].astype(F32))
    for pair in range(ny // 2):
        for column in range(2):
            y = 2 * pair + column
            for k in range(terms):
                rep[k] = jnp.broadcast_to(face[k, pl.ds(y, 1), :], (16, nz)).astype(BF16)
            for s in range(sources):
                for q in range(0, padded, step):
                    d = f_refs[s][0, y, pl.ds(q, step), :] - h_refs[s][0, y, pl.ds(q, step), :]
                    d = d.reshape(step // 16, 16, nz)
                    for k in range(terms):
                        at = (s * terms + k) * padded + q
                        t_ref[at:at + step, column * nz:(column + 1) * nz] = (d * rep[k][None]).reshape(step, nz)
        r = jnp.dot(w_ref[...], t_ref[...], preferred_element_type=F32)
        acc[pl.ds(2 * pair, outs, stride=ny), :] = r[:, :nz]
        acc[pl.ds(2 * pair + 1, outs, stride=ny), :] = r[:, nz:]
    o_ref[:, 0] = (acc[...] + base_ref[0]).reshape(outs, ny, nz).astype(BF16)


def tail(weights, coefs, coef_halo, base, fields, halos, out):
    terms, nx, ny, nz = coefs.shape
    outs = weights.shape[0]
    padded = fields[0].shape[2]
    sources = len(fields)
    depth = sources * terms * padded
    return pl.pallas_call(
        functools.partial(tail_kernel, sources),
        grid=(2,),
        in_specs=[
            pl.BlockSpec((outs, depth), lambda i: (0, 0)),
            pl.BlockSpec((terms, 1, ny, nz), lambda i: (0, i * (nx - 1), 0, 0)),
            pl.BlockSpec((1, terms, ny, nz), lambda i: (i, 0, 0, 0)),
            pl.BlockSpec((1, outs * ny, nz), lambda i: (i, 0, 0)),
        ]
        + [pl.BlockSpec((1, ny, padded, nz), lambda i: (i * (nx - 1), 0, 0, 0))] * sources
        + [pl.BlockSpec((1, ny, padded, nz), lambda i: (i, 0, 0, 0))] * sources
        + [pl.BlockSpec(memory_space=pl.ANY)],
        out_specs=pl.BlockSpec((outs, 1, ny, nz), lambda i: (0, i * (nx - 1), 0, 0)),
        out_shape=jax.ShapeDtypeStruct(out.shape, BF16),
        input_output_aliases={4 + 2 * sources: 0},
        scratch_shapes=[
            pltpu.VMEM((depth, 2 * nz), BF16),
            pltpu.VMEM((terms, ny, nz), F32),
            pltpu.VMEM((terms, 16, nz), BF16),
            pltpu.VMEM((outs * ny, nz), F32),
        ],
        compiler_params=pltpu.CompilerParams(vmem_limit_bytes=VMEM_LIMIT),
        name="tail",
    )(weights, coefs, coef_halo, base, *fields, *halos, out)


def solution(mesh):
    modes_axis, grid_axis = "mode", "grid"
    sources, bricks = mesh.shape[modes_axis], mesh.shape[grid_axis]

    def around(block):
        found = [block]
        for r in range(1, sources):
            found.append(lax.ppermute(block, modes_axis, [((i + r) % sources, i) for i in range(sources)]))
        return found

    def body(field, coupling, coefs):
        modes = field.shape[0]
        terms, outs, total = coupling.shape
        padded = up(modes, 16)
        forward = [(i, i + 1) for i in range(bricks - 1)]
        backward = [(b, a) for a, b in forward]
        turned, first, last = turn(field)
        below = lax.ppermute(last, grid_axis, forward)
        above = lax.ppermute(first, grid_axis, backward)
        coef_below = lax.ppermute(coefs[:, -1], grid_axis, forward)
        coef_above = lax.ppermute(coefs[:, 0], grid_axis, backward)
        fields = around(turned)

        me = lax.axis_index(modes_axis)
        parts = []
        for r in range(sources):
            part = lax.dynamic_slice_in_dim(coupling, (me + r) % sources * modes, modes, 2)
            parts.append(jnp.pad(part, ((0, 0), (0, 0), (0, padded - modes))))
        weights = jnp.stack(parts).transpose(2, 0, 1, 3).reshape(outs, sources * terms * padded)

        out, base = main(weights, coefs, fields)
        halos = around(jnp.stack([below, above]))
        return tail(weights, coefs, jnp.stack([coef_below, coef_above]), base, fields, halos, out)

    spec = P(modes_axis, grid_axis, None, None)
    return jax.shard_map(
        body,
        mesh=mesh,
        in_specs=(spec, P(None, modes_axis, None), P(None, grid_axis, None, None)),
        out_specs=spec,
        check_vma=False,
    )
```

time: 344 us -> 88.5 us (0.26)
  other arithmetic: 200 us -> 2.73 us
  matrix products: 57.4 us -> 0 us
  Pallas kernels: 0 us -> 56.6 us
  local copies, waits for them, and re-layouts: 39.3 us -> 6.56 us
  between operations: 13.5 us -> 0.13 us
  waiting for transfers between devices: 18.9 us -> 7.36 us
    add x11 -> x0, other arithmetic: 129 us -> none  [step(): total = total + face[None] * (centre - padded[:, sx, sy, sz])]
    convert_element_type x23 -> x0, other arithmetic: 58.4 us -> none  [the longest x11 48.9 us: step(): values = values.astype(jnp.float32)]
    dot_general x11 -> x0, matrix products: 57.4 us -> none  [one_term(): jnp.dot(weights, flat, preferred_element_type=jnp.float32)]
    pallas_call x0 -> x3, Pallas kernels: none -> 56.6 us  [the longest x1 44.6 us: main(): pl.pallas_call(functools.partial(main_kernel, sources), in_specs=[vmem, v...]
    unnamed x2 -> x6, local copies, waits for them, and re-layouts: 36.8 us -> 0.82 us
    ppermute x4 -> x6, waiting for transfers between devices: 15.6 us -> 7.36 us  [the longest x1 7.09 us: body(): above = lax.ppermute(first, grid_axis, backward)]
    mul x11 -> x0, other arithmetic: 7.78 us -> none  [step(): face = 0.5 * (ccen + cpad[sx, sy, sz])]
    ppermute x4 -> x6, starting transfers between devices: 11.2 us -> 13.4 us  [the longest x1 4.02 us: body(): below = lax.ppermute(last, grid_axis, forward)]
  transfers between devices with their start and end apart: 5 -> 6, of which waited for: 4 -> 2; matrix products, arithmetic and copies ran while one was open for 1% -> 10% of each run, Pallas kernels for 0% -> 51%
where the time goes in v1:
time: 88.5 us; the launch traced here: 86.7 us
  Pallas kernels  56.6 us (64%)
  starting transfers between devices  13.4 us (15%)
  waiting for transfers between devices  7.36 us (8%)
  local copies, waits for them, and re-layouts  6.56 us (7%)
  other arithmetic  2.73 us (3%)
    pallas_call x1, Pallas kernels, main(): pl.pallas_call(functools.partial(main_kernel, sources), in_specs=[vmem, v...  44.6 us
    ppermute x1, waiting for transfers between devices, body(): above = lax.ppermute(first, grid_axis, backward)  7.09 us
    pallas_call x1, Pallas kernels, tail(): pl.pallas_call(functools.partial(tail_kernel, sources), grid=(2,), in_spe...  6.71 us
    pallas_call x1, Pallas kernels, turn(): pl.pallas_call(turn_kernel, grid=(nx,), in_specs=[pl.BlockSpec((modes, 1,...  5.28 us
    ppermute x1, starting transfers between devices, body(): below = lax.ppermute(last, grid_axis, forward)  4.02 us
    ppermute x1, starting transfers between devices, body(): coef_below = lax.ppermute(coefs[:, -1], grid_axis, forward)  3.11 us
    ppermute x1, starting transfers between devices, body(): coef_above = lax.ppermute(coefs[:, 0], grid_axis, backward)  2.16 us
    ppermute x2, starting transfers between devices, around(): lax.ppermute(block, modes_axis, [((i + r) % sources, i) for i in range(so...  2.16 us
  transfers between devices with their start and end apart: 6, of which 2 were waited for; matrix products, arithmetic and copies ran while one was open for 10% of the time, Pallas kernels for 51%

profile of v1, /device:TPU:27, one launch (start us, length us, event | category | flops | bytes accessed | tf_op | source)
XLA Modules:
  0.0 86.7 jit_solution(8199235682368444844)
XLA Ops:
  0.0 0.0 copy-start.1
  0.0 5.3 %turn.1 = (bf16[6,8,144,128]{3,2,1,0:T(8,128)(2,1)}, bf16[8,144,128]{2,1,0:T(8,128)(2,1)}, bf16[8,144,128]{2,1,0:T(8,128)(2,1)}) custom-call(bf16[144,6,8,128]{3,2,1,0:T(8,128)(2,1)} %f_ref.1), custom_call_target="tpu_custom_call" | custom-call | tf_op jit(solution)/shard_map/turn/pallas_call | solution.py:48
  5.3 0.7 collective-permute-start.2
  6.0 1.4 %slice_bitcast_fusion.1 = (bf16[11,8,128]{2,1,0:T(8,128)(2,1)}, bf16[11,8,128]{2,1,0:T(8,128)(2,1)}) fusion(bf16[11,6,8,128]{3,2,1,0:T(8,128)(2,1)} %a_ref.1), kind=kLoop, calls=%fused_computation.6 | loop fusion | bytes 90112 | tf_op jit(solution)/shard_map/squeeze | solution.py:309
  7.3 3.1 %collective-permute-start = (bf16[11,8,128]{2,1,0:T(8,128)(2,1)}, bf16[11,8,128]{2,1,0:T(8,128)(2,1)}, u32[]{:S(2)}, u32[]{:S(2)}) collective-permute-start(bf16[11,8,128]{2,1,0:T(8,128)(2,1)} %get-tuple-element.17), channel_id=1, source_target_pairs={{0,2},{2,4},{4,6},{6,8},{8,10},{10,12},{12,14},{14,16},{16,18},{18... | collective-permute-start | bytes 67592 | tf_op jit(solution)/shard_map/ppermute | solution.py:309
  10.4 2.2 %collective-permute-start.1 = (bf16[11,8,128]{2,1,0:T(8,128)(2,1)}, bf16[11,8,128]{2,1,0:T(8,128)(2,1)}, u32[]{:S(2)}, u32[]{:S(2)}) collective-permute-start(bf16[11,8,128]{2,1,0:T(8,128)(2,1)} %get-tuple-element.18), channel_id=1, source_target_pairs={{2,0},{4,2},{6,4},{8,6},{10,8},{12,10},{14,12},{16,14},{18,16},{20... | collective-permute-start | bytes 67592 | tf_op jit(solution)/shard_map/ppermute | solution.py:310
  12.6 4.0 %collective-permute-start.3 = (bf16[8,144,128]{2,1,0:T(8,128)(2,1)}, bf16[8,144,128]{2,1,0:T(8,128)(2,1)S(1)}, u32[]{:S(2)}, u32[]{:S(2)}) collective-permute-start(bf16[8,144,128]{2,1,0:T(8,128)(2,1)} %get-tuple-element.12), channel_id=1, source_target_pairs={{0,2},{2,4},{4,6},{6,8},{8,10},{10,12},{12,14},{14,16},{16,18},{18... | collective-permute-start | bytes 884744 | tf_op jit(solution)/shard_map/ppermute | solution.py:307
  16.6 1.9 %collective-permute-start.4 = (bf16[8,144,128]{2,1,0:T(8,128)(2,1)}, bf16[8,144,128]{2,1,0:T(8,128)(2,1)}, u32[]{:S(2)}, u32[]{:S(2)}) collective-permute-start(bf16[8,144,128]{2,1,0:T(8,128)(2,1)} %get-tuple-element.13), channel_id=1, source_target_pairs={{2,0},{4,2},{6,4},{8,6},{10,8},{12,10},{14,12},{16,14},{18,16},{20... | collective-permute-start | bytes 884744 | tf_op jit(solution)/shard_map/ppermute | solution.py:308
  18.6 0.0 copy-done.1
  18.6 0.8 dynamic-slice_bitcast_fusion.1
  19.4 0.3 maximum_bitcast_fusion
  19.7 1.7 %copy.7 = bf16[144,2,11,144]{0,3,2,1:T(8,128)(2,1)S(1)} copy(bf16[144,2,11,144]{3,0,2,1:T(8,128)(2,1)S(1)} %maximum_bitcast_fusion) | data formatting | bytes 1824768 | tf_op jit(solution)/shard_map/transpose | solution.py:318
  21.5 1.9 %copy.11.refs_0_.w_ref = bf16[144,3168]{1,0:T(8,128)(2,1)} copy(bf16[144,3168]{0,1:T(8,128)(2,1)S(1)} %bitcast.19) | data formatting | bytes 1824768 | tf_op jit(solution)/shard_map/reshape | solution.py:318
  23.3 0.3 collective-permute-done.3
  23.6 7.1 %collective-permute-done.4 = bf16[8,144,128]{2,1,0:T(8,128)(2,1)} collective-permute-done((bf16[8,144,128]{2,1,0:T(8,128)(2,1)}, bf16[8,144,128]{2,1,0:T(8,128)(2,1)}, u32[]{:S(2)}, u32[]{:S(2)}) %collective-permute-start.4) | collective-permute-done | bytes 294944 | tf_op jit(solution)/shard_map/ppermute | solution.py:308
  30.7 1.0 %pad_maximum_fusion.refs_2_ = bf16[2,8,144,128]{3,2,1,0:T(8,128)(2,1)S(1)} fusion(bf16[1,8,144,128]{3,2,1,0:T(8,128)(2,1)} %bitcast.9, bf16[1,8,144,128]{3,2,1,0:T(8,128)(2,1)S(1)} %bitcast.20), kind=kLoop, calls=%fused_computation.3 | loop fusion | flops 294912 | bytes 1179648 | tf_op jit(solution)/shard_map/stack | solution.py:321
  31.7 0.0 copy-start
  31.7 1.5 %collective-permute-start.5 = (bf16[2,8,144,128]{3,2,1,0:T(8,128)(2,1)S(1)}, bf16[2,8,144,128]{3,2,1,0:T(8,128)(2,1)S(1)}, u32[]{:S(2)}, u32[]{:S(2)}) collective-permute-start(bf16[2,8,144,128]{3,2,1,0:T(8,128)(2,1)S(1)} %pad_maximum_fusion.refs_2_), channel_id=1, source_target_pairs={{1,0},{0,1},{3,2},{2,3},{5,4},{4,5},{7,6},{6,7},{9,8},{8,9},{11,10... | collective-permute-start | bytes 1769480 | tf_op jit(solution)/shard_map/ppermute | solution.py:297
  33.2 0.0 collective-permute-done
  33.2 0.0 collective-permute-done.1
  33.2 1.4 %pad_maximum_fusion.1.ah_ref = bf16[2,11,8,128]{3,2,1,0:T(8,128)(2,1)} fusion(bf16[1,11,8,128]{3,2,1,0:T(8,128)(2,1)} %bitcast.7, bf16[1,11,8,128]{3,2,1,0:T(8,128)(2,1)} %bitcast.5), kind=kLoop, calls=%fused_computation.4 | loop fusion | flops 22528 | bytes 90112 | tf_op jit(solution)/shard_map/stack | solution.py:322
  34.6 0.0 collective-permute-done.2.refs_3_.refs_1_
  34.6 44.6 %faces.1 = (bf16[144,6,8,128]{3,2,1,0:T(8,128)(2,1)}, f32[2,1152,128]{2,1,0:T(8,128)}) custom-call(bf16[144,3168]{1,0:T(8,128)(2,1)} %copy.11.refs_0_.w_ref, bf16[11,6,8,128]{3,2,1,0:T(8,128)(2,1)} %a_ref.1, bf16[6,8,144,128]{3,2,1,0:T(8,128)(2,1)} %get-tuple-element.10.refs_2_.refs_0_, bf16[6,8,144,128]{3,2,1,0:T(8,128)(2,1)} %collective-permute-done.2.refs_3_.refs_1_), custom_call_target="tpu_custom_call" | custom-call | flops 5605687296 | bytes 8388608 | tf_op jit(solution)/shard_map/faces/pallas_call | solution.py:202
  79.2 0.0 copy-done
  79.2 0.0 collective-permute-done.5.refs_3_
  79.2 0.0 copy-start.2
  79.2 0.8 copy-done.2
  80.0 6.7 %tail.1 = bf16[144,6,8,128]{3,2,1,0:T(8,128)(2,1)} custom-call(bf16[144,3168]{1,0:T(8,128)(2,1)} %copy.11.refs_0_.w_ref, bf16[11,6,8,128]{3,2,1,0:T(8,128)(2,1)} %a_ref.1, bf16[2,11,8,128]{3,2,1,0:T(8,128)(2,1)} %pad_maximum_fusion.1.ah_ref, f32[2,1152,128]{2,1,0:T(8,128)} %get-tuple-element.11.base_ref, ...), custom_call_target="tpu_custom_call", output_to_operand_aliasing={{}: (8, {})} | custom-call | tf_op jit(solution)/shard_map/tail/pallas_call | solution.py:264
Async XLA Ops:
  0.0 18.6 %copy-start.1 = (bf16[11,144,288]{2,1,0:T(8,128)(2,1)S(1)}, bf16[11,144,288]{2,1,0:T(8,128)(2,1)}, u32[]{:S(2)}) copy-start(bf16[11,144,288]{2,1,0:T(8,128)(2,1)} %param.4) | copy-start | bytes 2737156
  5.3 29.3 %collective-permute-start.2 = (bf16[6,8,144,128]{3,2,1,0:T(8,128)(2,1)}, bf16[6,8,144,128]{3,2,1,0:T(8,128)(2,1)}, u32[]{:S(2)}, u32[]{:S(2)}) collective-permute-start(bf16[6,8,144,128]{3,2,1,0:T(8,128)(2,1)} %get-tuple-element.10.refs_2_.refs_0_), channel_id=1, source_target_pairs={{1,0},{0,1},{3,2},{2,3},{5,4},{4,5},{7,6},{6,7},{9,8},{8,9},{11,10... | collective-permute-start | bytes 5308424 | tf_op jit(solution)/shard_map/ppermute | solution.py:297
  7.3 25.9 %collective-permute-start = (bf16[11,8,128]{2,1,0:T(8,128)(2,1)}, bf16[11,8,128]{2,1,0:T(8,128)(2,1)}, u32[]{:S(2)}, u32[]{:S(2)}) collective-permute-start(bf16[11,8,128]{2,1,0:T(8,128)(2,1)} %get-tuple-element.17), channel_id=1, source_target_pairs={{0,2},{2,4},{4,6},{6,8},{8,10},{10,12},{12,14},{14,16},{16,18},{18... | collective-permute-start | bytes 67592 | tf_op jit(solution)/shard_map/ppermute | solution.py:309
  10.4 22.8 %collective-permute-start.1 = (bf16[11,8,128]{2,1,0:T(8,128)(2,1)}, bf16[11,8,128]{2,1,0:T(8,128)(2,1)}, u32[]{:S(2)}, u32[]{:S(2)}) collective-permute-start(bf16[11,8,128]{2,1,0:T(8,128)(2,1)} %get-tuple-element.18), channel_id=1, source_target_pairs={{2,0},{4,2},{6,4},{8,6},{10,8},{12,10},{14,12},{16,14},{18,16},{20... | collective-permute-start | bytes 67592 | tf_op jit(solution)/shard_map/ppermute | solution.py:310
  12.6 11.0 %collective-permute-start.3 = (bf16[8,144,128]{2,1,0:T(8,128)(2,1)}, bf16[8,144,128]{2,1,0:T(8,128)(2,1)S(1)}, u32[]{:S(2)}, u32[]{:S(2)}) collective-permute-start(bf16[8,144,128]{2,1,0:T(8,128)(2,1)} %get-tuple-element.12), channel_id=1, source_target_pairs={{0,2},{2,4},{4,6},{6,8},{8,10},{10,12},{12,14},{14,16},{16,18},{18... | collective-permute-start | bytes 884744 | tf_op jit(solution)/shard_map/ppermute | solution.py:307
  16.6 14.0 %collective-permute-start.4 = (bf16[8,144,128]{2,1,0:T(8,128)(2,1)}, bf16[8,144,128]{2,1,0:T(8,128)(2,1)}, u32[]{:S(2)}, u32[]{:S(2)}) collective-permute-start(bf16[8,144,128]{2,1,0:T(8,128)(2,1)} %get-tuple-element.13), channel_id=1, source_target_pairs={{2,0},{4,2},{6,4},{8,6},{10,8},{12,10},{14,12},{16,14},{18,16},{20... | collective-permute-start | bytes 884744 | tf_op jit(solution)/shard_map/ppermute | solution.py:308
  31.7 47.5 %copy-start = (bf16[2,8,144,128]{3,2,1,0:T(8,128)(2,1)}, bf16[2,8,144,128]{3,2,1,0:T(8,128)(2,1)S(1)}, u32[]{:S(2)}) copy-start(bf16[2,8,144,128]{3,2,1,0:T(8,128)(2,1)S(1)} %pad_maximum_fusion.refs_2_) | copy-start | bytes 1769476
  31.7 47.5 %collective-permute-start.5 = (bf16[2,8,144,128]{3,2,1,0:T(8,128)(2,1)S(1)}, bf16[2,8,144,128]{3,2,1,0:T(8,128)(2,1)S(1)}, u32[]{:S(2)}, u32[]{:S(2)}) collective-permute-start(bf16[2,8,144,128]{3,2,1,0:T(8,128)(2,1)S(1)} %pad_maximum_fusion.refs_2_), channel_id=1, source_target_pairs={{1,0},{0,1},{3,2},{2,3},{5,4},{4,5},{7,6},{6,7},{9,8},{8,9},{11,10... | collective-permute-start | bytes 1769480 | tf_op jit(solution)/shard_map/ppermute | solution.py:297
  79.2 0.8 copy-start.2

commit v2 on v0

v2 whole, which is shorter than its diff:
```python
import functools

import jax
import jax.numpy as jnp
from jax import lax
from jax.experimental import pallas as pl
from jax.experimental.pallas import tpu as pltpu
from jax.sharding import PartitionSpec as P

BF16 = jnp.bfloat16
F32 = jnp.float32
VMEM_LIMIT = 60 * 2**20
MODE, GRID = "mode", "grid"
PARAMS = pltpu.CompilerParams(vmem_limit_bytes=VMEM_LIMIT)
VMEM = pl.BlockSpec(memory_space=pltpu.VMEM)
HBM = pl.BlockSpec(memory_space=pl.ANY)


def block_of(rows):
    return 16 if rows % 16 == 0 else 8


def divisor(n, candidates):
    return next(c for c in candidates if n % c == 0)


def one_hot(count, inner):
    size = count * inner
    r = lax.broadcasted_iota(jnp.int32, (size, size), 0)
    c = lax.broadcasted_iota(jnp.int32, (size, size), 1)
    return (c == lax.rem(r, count) * inner + lax.div(r, count)).astype(F32).astype(BF16)


def permuted(perm, rows):
    return jnp.dot(perm, rows, preferred_element_type=F32).astype(BF16)


def extra_of(terms, ny):
    return ny * -(-terms // ny)


def coef_rows(ref, k, modes, ny):
    return ref.at[k % ny, pl.ds(modes + ny * (k // ny), ny), :]


def turn_kernel(modes, f_ref, a_ref, o_ref, e_ref, d_ref, perm):
    step = pl.program_id(0)
    chunk, nx, ny, nz = f_ref.shape
    terms = a_ref.shape[0]
    block = block_of(chunk)
    odd = lax.rem(lax.axis_index(GRID), 2)
    outer = ((e_ref, (1 - odd) * (nx - 1)), (d_ref, odd * (nx - 1)))

    @pl.when(step == 0)
    def _():
        perm[...] = one_hot(block, ny)
        for out, x in outer:
            for k in range(terms):
                coef_rows(out, k, modes, ny)[...] = a_ref[k, x]

    layers = 2 if nx % 2 == 0 else 1
    for x in range(0, nx, layers):
        for q in range(0, chunk, block):
            wide = jnp.concatenate(
                [f_ref[pl.ds(q, block), x + j].reshape(block * ny, nz) for j in range(layers)], axis=1
            )
            wide = permuted(perm[...], wide)
            for j in range(layers):
                o_ref[x + j, :, pl.ds(q, block), :] = wide[:, j * nz:(j + 1) * nz].reshape(ny, block, nz)
    rows = pl.ds(pl.multiple_of(step * chunk, 8), chunk)
    for out, x in outer:
        out[:, rows, :] = o_ref[x]


def turn(field, coefs):
    modes, nx, ny, nz = field.shape
    chunk = divisor(modes, (48, 72, 64, 32, 16, 8))
    outer = (ny, modes + extra_of(coefs.shape[0], ny), nz)
    block = block_of(chunk)
    whole = pl.BlockSpec(outer, lambda i: (0, 0, 0))
    return pl.pallas_call(
        functools.partial(turn_kernel, modes),
        grid=(modes // chunk,),
        in_specs=[
            pl.BlockSpec((chunk, nx, ny, nz), lambda i: (i, 0, 0, 0)),
            pl.BlockSpec(coefs.shape, lambda i: (0, 0, 0, 0)),
        ],
        out_specs=[pl.BlockSpec((nx, ny, chunk, nz), lambda i: (0, 0, i, 0)), whole, whole],
        scratch_shapes=[pltpu.VMEM((block * ny, block * ny), BF16)],
        out_shape=[
            jax.ShapeDtypeStruct((nx, ny, modes, nz), BF16),
            jax.ShapeDtypeStruct(outer, BF16),
            jax.ShapeDtypeStruct(outer, BF16),
        ],
        compiler_params=PARAMS,
        name="turn",
    )(field, coefs)


def chunk_of(total):
    return divisor(total, (32, 16))


def weights_kernel(c_ref, o_ref):
    terms, _, total = c_ref.shape
    chunk = chunk_of(total)
    pieces = [(k, q) for q in range(0, total, chunk) for k in range(terms)]
    per = 128 // chunk
    for i in range(0, len(pieces), per):
        group = pieces[i:i + per]
        wide = jnp.concatenate([c_ref[k, :, q:q + chunk] for k, q in group], axis=1)
        o_ref[:, i * chunk:i * chunk + len(group) * chunk] = wide


def weights_of(coupling):
    terms, outs, total = coupling.shape
    return pl.pallas_call(
        weights_kernel,
        in_specs=[VMEM],
        out_specs=VMEM,
        out_shape=jax.ShapeDtypeStruct((outs, terms * total), BF16),
        compiler_params=PARAMS,
        name="weights",
    )(coupling)


def layers_kernel(sources, outer, w_ref, a_ref, *refs):
    terms, nx, ny, nz = a_ref.shape
    outs, total = w_ref.shape[0], w_ref.shape[1] // terms
    modes = total // sources
    f_hbm, refs = refs[:sources], refs[sources:]
    if outer:
        even, odd, refs = refs[:sources], refs[sources:2 * sources], refs[2 * sources + 1:]
    out_hbm, f_ref, stage, coef, face, repx, repy, repz, acc, obuf, perm, fsem, osem, *more = refs
    slots = f_ref.shape[0]
    items = repx.shape[0]
    stride = 3 if outer else 1
    block = block_of(outs)
    pairs = ny // 2
    me = lax.axis_index(MODE)
    is_even = lax.rem(lax.axis_index(GRID), 2) == 0

    def place(s):
        return pl.ds(pl.multiple_of(lax.rem(me + s, sources) * modes, 8), modes)

    def load(s, slot, ref):
        return pltpu.make_async_copy(ref, stage.at[slot, :, place(s), :], fsem.at[s, slot])

    layer_of = (None, 0, 1, nx - 2, nx - 1, None) if outer else range(nx)
    if outer:
        ends, csem = more
        copies = []
        for s in range(sources):
            for test, lo, hi in ((is_even, odd[s], even[s]), (~is_even, even[s], odd[s])):
                @pl.when(test)
                def _():
                    load(s, 0, lo.at[:, pl.ds(0, modes), :]).start()
                    load(s, slots - 1, hi.at[:, pl.ds(0, modes), :]).start()
                    if s == 0:
                        for i, ref in ((0, lo), (1, hi)):
                            pltpu.make_async_copy(
                                ref.at[:, pl.ds(modes, ends.shape[2]), :], ends.at[i], csem.at[i]
                            ).start()
    for slot in range(slots):
        if layer_of[slot] is not None:
            for s in range(sources):
                load(s, slot, f_hbm[s].at[layer_of[slot]]).start()

    perm[...] = one_hot(ny, block)
    lane = lax.broadcasted_iota(jnp.int32, (ny, nz), 1)
    row = lax.broadcasted_iota(jnp.int32, (ny, nz), 0)
    for slot in range(slots):
        for y in (0, ny + 1):
            f_ref[slot, y] = jnp.zeros((total, nz), F32)
    if outer:
        for i in range(2):
            pltpu.make_async_copy(even[0].at[:, pl.ds(modes, ends.shape[2]), :], ends.at[i], csem.at[i]).wait()
    for slot in range(slots):
        for k in range(terms):
            if layer_of[slot] is None:
                tile = coef_rows(ends.at[0 if slot == 0 else 1], k, 0, ny)[...]
            else:
                tile = a_ref[k, layer_of[slot]]
            coef[slot, k] = 0.5 * tile.astype(F32)

    def spread(values, y):
        return jnp.broadcast_to(values[pl.ds(y, 1), :], (16, nz)).astype(BF16)

    @pl.loop(0, items)
    def _(i):
        c = 1 + stride * i
        for k in range(terms):
            a = coef[c, k]
            face[0, k] = a + coef[c - 1, k]
            face[1, k] = a + coef[c + 1, k]
            face[2, k] = a + jnp.where(row > 0, pltpu.roll(a, 1, 0), 0.0)
            face[3, k] = a + jnp.where(lane > 0, pltpu.roll(a, 1, 1), 0.0)
            face[4, k] = a + jnp.where(lane < nz - 1, pltpu.roll(a, nz - 1, 1), 0.0)
            face[5, k] = a
        for k in range(terms):
            for y in range(ny):
                repx[i, 0, y, k] = spread(face.at[0, k], y)
                repx[i, 1, y, k] = spread(face.at[1, k], y)
                repy[i, y, k] = spread(face.at[2, k], y)
                repz[i, 0, y, k] = spread(face.at[3, k], y)
                repz[i, 1, y, k] = spread(face.at[4, k], y)
            repy[i, ny, k] = spread(face.at[5, k], ny - 1)

    lanes = lax.broadcasted_iota(jnp.int32, (16, nz), 1)

    def arrive(slot):
        for s in range(sources):
            load(s, slot, f_hbm[s].at[0]).wait()

        @pl.loop(0, ny)
        def _(y):
            f_ref[slot, y + 1] = stage[slot, y].astype(F32)

    def differences(c, y, q):
        def at(c, y):
            return f_ref[c, y + 1, pl.ds(q, 16), :]

        here = at(c, y)
        zm = jnp.where(lanes > 0, pltpu.roll(here, 1, 1), 0.0)
        zp = jnp.where(lanes < nz - 1, pltpu.roll(here, nz - 1, 1), 0.0)
        others = (at(c - 1, y), at(c + 1, y), at(c, y - 1), at(c, y + 1), zm, zp)
        return [(here - v).astype(BF16) for v in others]

    def rows_of(i, c, y, q):
        ds = [differences(c, y, q + g) for g in range(0, chunk_of(total), 16)]
        rows = []
        for k in range(terms):
            w = (repx[i, 0, y, k], repx[i, 1, y, k], repy[i, y, k], repy[i, y + 1, k], repz[i, 0, y, k], repz[i, 1, y, k])
            for d in ds:
                p = [u * v for u, v in zip(d, w)]
                rows.append((p[0] + p[1]) + (p[2] + p[3]) + (p[4] + p[5]))
        return rows

    def mix(i, c, slot, pair):
        sides = ([], [])
        for q in range(0, total, chunk_of(total)):
            for column in range(2):
                sides[column].extend(rows_of(i, c, 2 * pair + column, q))
        t = jnp.concatenate([jnp.concatenate(side, axis=0) for side in sides], axis=1)
        r = jnp.dot(w_ref[...], t, preferred_element_type=F32).astype(BF16)
        acc[2 * pair] = r[:, :nz]
        acc[2 * pair + 1] = r[:, nz:]

    def finish(slot):
        for p in range(0, outs, block):
            rows = acc[:, pl.ds(p, block), :].reshape(ny * block, nz)
            obuf[slot, pl.ds(p, block)] = permuted(perm[...], rows).reshape(block, ny, nz)

    def write(i, slot):
        x = i * (nx - 1) if outer else i + 1
        return pltpu.make_async_copy(obuf.at[slot], out_hbm.at[:, x], osem.at[slot])

    unroll = 2 if pairs % 2 == 0 else 1

    @pl.loop(0, items)
    def _(i):
        slot = i & 1
        c = 1 + stride * i
        if outer:
            for j in range(3):
                arrive(3 * i + j)
        else:
            @pl.when(i == 0)
            def _():
                arrive(0)
                arrive(1)
            arrive(i + 2)

        @pl.loop(0, pairs // unroll)
        def _(n):
            for j in range(unroll):
                mix(i, c, slot, unroll * n + j)

        @pl.when(i > 1)
        def _():
            write(i - 2, slot).wait()

        finish(slot)
        write(i, slot).start()

    for i in range(max(items - 2, 0), items):
        write(i, i & 1).wait()


def layers(weights, coefs, fields, halos=None, out=None):
    outer = halos is not None
    terms, nx, ny, nz = coefs.shape
    outs, depth = weights.shape
    total = depth // terms
    sources = len(fields)
    block = block_of(outs)
    items = 2 if outer else nx - 2
    slots = 6 if outer else nx
    shape = jax.ShapeDtypeStruct((outs, nx, ny, nz), BF16)
    operands = [weights, coefs, *fields] + ([*halos[0], *halos[1], out] if outer else [])
    more = []
    if outer:
        more = [pltpu.VMEM((2, ny, extra_of(terms, ny), nz), BF16), pltpu.SemaphoreType.DMA((2,))]
    return pl.pallas_call(
        functools.partial(layers_kernel, sources, outer),
        in_specs=[VMEM, VMEM] + [HBM] * (len(operands) - 2),
        out_specs=HBM,
        out_shape=shape,
        input_output_aliases={len(operands) - 1: 0} if outer else {},
        scratch_shapes=[
            pltpu.VMEM((slots, ny + 2, total, nz), F32),
            pltpu.VMEM((slots, ny, total, nz), BF16),
            pltpu.VMEM((slots, terms, ny, nz), F32),
            pltpu.VMEM((6, terms, ny, nz), F32),
            pltpu.VMEM((items, 2, ny, terms, 16, nz), BF16),
            pltpu.VMEM((items, ny + 1, terms, 16, nz), BF16),
            pltpu.VMEM((items, 2, ny, terms, 16, nz), BF16),
            pltpu.VMEM((ny, outs, nz), BF16),
            pltpu.VMEM((2, outs, ny, nz), BF16),
            pltpu.VMEM((block * ny, block * ny), BF16),
            pltpu.SemaphoreType.DMA((sources, slots)),
            pltpu.SemaphoreType.DMA((2,)),
            *more,
        ],
        compiler_params=PARAMS,
        cost_estimate=pl.CostEstimate(
            flops=2 * outs * depth * items * ny * nz, bytes_accessed=6 * 2**20, transcendentals=0
        ),
        name="outer" if outer else "inner",
    )(*operands)


def solution(mesh):
    sources, bricks = mesh.shape[MODE], mesh.shape[GRID]

    def around(block):
        found = [block]
        for r in range(1, sources):
            found.append(lax.ppermute(block, MODE, [((i + r) % sources, i) for i in range(sources)]))
        return found

    def exchange(block, offset):
        pairs = [(i, i + 1) for i in range(offset, bricks - 1, 2)]
        return lax.ppermute(block, GRID, pairs + [(b, a) for a, b in pairs])

    def body(field, coupling, coefs):
        turned, even_out, odd_out = turn(field, coefs)
        even_in, odd_in = exchange(even_out, 0), exchange(odd_out, 1)
        fields = around(turned)
        weights = weights_of(coupling)
        out = layers(weights, coefs, fields)
        even_in, odd_in, out = lax.optimization_barrier((even_in, odd_in, out))
        return layers(weights, coefs, fields, (around(even_in), around(odd_in)), out)

    spec = P(MODE, GRID, None, None)
    return jax.shard_map(
        body,
        mesh=mesh,
        in_specs=(spec, P(None, MODE, None), P(None, GRID, None, None)),
        out_specs=spec,
        check_vma=False,
    )
```

time: 344 us -> 50.6 us (0.15)
  other arithmetic: 200 us -> 0 us
  matrix products: 57.4 us -> 0 us
  Pallas kernels: 0 us -> 40.6 us
  local copies, waits for them, and re-layouts: 39.3 us -> 2.21 us
  waiting for transfers between devices: 18.9 us -> 1.65 us
  between operations: 13.5 us -> 0.06 us
  starting transfers between devices: 11.2 us -> 5.77 us
    add x11 -> x0, other arithmetic: 129 us -> none  [step(): total = total + face[None] * (centre - padded[:, sx, sy, sz])]
    convert_element_type x23 -> x0, other arithmetic: 58.4 us -> none  [the longest x11 48.9 us: step(): values = values.astype(jnp.float32)]
    dot_general x11 -> x0, matrix products: 57.4 us -> none  [one_term(): jnp.dot(weights, flat, preferred_element_type=jnp.float32)]
    pallas_call x0 -> x4, Pallas kernels: none -> 40.6 us  [the longest x2 33.4 us: layers(): pl.pallas_call(functools.partial(layers_kernel, sources, outer), in_specs...]
    unnamed x2 -> x10, local copies, waits for them, and re-layouts: 36.8 us -> 2.21 us
    ppermute x4 -> x5, waiting for transfers between devices: 15.6 us -> 1.65 us  [the longest x3 1.65 us: around(): lax.ppermute(block, MODE, [((i + r) % sources, i) for i in range(sources)])]
    mul x11 -> x0, other arithmetic: 7.78 us -> none  [step(): face = 0.5 * (ccen + cpad[sx, sy, sz])]
    ppermute x4 -> x5, starting transfers between devices: 11.2 us -> 5.77 us  [the longest x2 4.31 us: exchange(): return lax.ppermute(block, GRID, pairs + [(b, a) for a, b in pairs])]
  transfers between devices with their start and end apart: 5 -> 5, of which waited for: 4 -> 2; matrix products, arithmetic and copies ran while one was open for 1% -> 0% of each run, Pallas kernels for 0% -> 46%
where the time goes in v2:
time: 50.6 us; the launch traced here: 50.3 us
  Pallas kernels  40.6 us (80%)
  starting transfers between devices  5.77 us (11%)
  local copies, waits for them, and re-layouts  2.21 us (4%)
  waiting for transfers between devices  1.65 us (3%)
    pallas_call x2, Pallas kernels, layers(): pl.pallas_call(functools.partial(layers_kernel, sources, outer), in_specs...  33.4 us
    ppermute x2, starting transfers between devices, exchange(): return lax.ppermute(block, GRID, pairs + [(b, a) for a, b in pairs])  4.31 us
    pallas_call x1, Pallas kernels, turn(): pl.pallas_call(functools.partial(turn_kernel, modes), grid=(modes // chun...  4.26 us
    pallas_call x1, Pallas kernels, weights_of(): pl.pallas_call(weights_kernel, in_specs=[VMEM], out_specs=VMEM, out_shape...  2.95 us
    unnamed x10, local copies, waits for them, and re-layouts  2.21 us
    ppermute x3, waiting for transfers between devices, around(): lax.ppermute(block, MODE, [((i + r) % sources, i) for i in range(sources)])  1.65 us
    ppermute x3, starting transfers between devices, around(): lax.ppermute(block, MODE, [((i + r) % sources, i) for i in range(sources)])  1.45 us
  transfers between devices with their start and end apart: 5, of which 2 were waited for; matrix products, arithmetic and copies ran while one was open for 0% of the time, Pallas kernels for 46%

profile of v2, /device:TPU:27, one launch (start us, length us, event | category | flops | bytes accessed | tf_op | source)
XLA Modules:
  0.0 50.3 jit_solution(8577480245945827181)
XLA Ops:
  0.0 4.3 %turn.1 = (bf16[6,8,144,128]{3,2,1,0:T(8,128)(2,1)}, bf16[8,160,128]{2,1,0:T(8,128)(2,1)}, bf16[8,160,128]{2,1,0:T(8,128)(2,1)}) custom-call(bf16[144,6,8,128]{3,2,1,0:T(8,128)(2,1)} %f_ref.1, bf16[11,6,8,128]{3,2,1,0:T(8,128)(2,1)} %a_ref.5), custom_call_target="tpu_custom_call" | custom-call | tf_op jit(solution)/shard_map/turn/pallas_call | solution.py:81
  4.3 0.7 %collective-permute-start = (bf16[6,8,144,128]{3,2,1,0:T(8,128)(2,1)}, bf16[6,8,144,128]{3,2,1,0:T(8,128)(2,1)S(1)}, u32[]{:S(2)}, u32[]{:S(2)}) collective-permute-start(bf16[6,8,144,128]{3,2,1,0:T(8,128)(2,1)} %get-tuple-element.11.refs_0_), channel_id=1, source_target_pairs={{1,0},{0,1},{3,2},{2,3},{5,4},{4,5},{7,6},{6,7},{9,8},{8,9},{11,10... | collective-permute-start | bytes 5308424 | tf_op jit(solution)/shard_map/ppermute | solution.py:339
  4.9 0.3 collective-permute-start.1
  5.2 4.1 %collective-permute-start.2 = (bf16[8,160,128]{2,1,0:T(8,128)(2,1)}, bf16[8,160,128]{2,1,0:T(8,128)(2,1)S(1)}, u32[]{:S(2)}, u32[]{:S(2)}) collective-permute-start(bf16[8,160,128]{2,1,0:T(8,128)(2,1)} %get-tuple-element.13), channel_id=1, source_target_pairs={{2,4},{6,8},{10,12},{14,16},{18,20},{22,24},{26,28},{4,2},{8,6},{1... | collective-permute-start | bytes 983048 | tf_op jit(solution)/shard_map/ppermute | solution.py:344
  9.3 3.0 %weights.1.w_ref = bf16[144,3168]{1,0:T(8,128)(2,1)} custom-call(bf16[11,144,288]{2,1,0:T(8,128)(2,1)} %c_ref.1), custom_call_target="tpu_custom_call" | custom-call | tf_op jit(solution)/shard_map/weights/pallas_call | solution.py:117
  12.2 0.0 collective-permute-done.refs_1_
  12.2 0.0 copy-start
  12.2 1.2 %copy-done = bf16[6,8,144,128]{3,2,1,0:T(8,128)(2,1)} copy-done((bf16[6,8,144,128]{3,2,1,0:T(8,128)(2,1)}, bf16[6,8,144,128]{3,2,1,0:T(8,128)(2,1)S(1)}, u32[]{:S(2)}) %copy-start) | copy-done | bytes 1769496
  13.4 20.0 %inner.1.refs_6_ = bf16[144,6,8,128]{3,2,1,0:T(8,128)(2,1)} custom-call(bf16[144,3168]{1,0:T(8,128)(2,1)} %weights.1.w_ref, bf16[11,6,8,128]{3,2,1,0:T(8,128)(2,1)} %a_ref.5, bf16[6,8,144,128]{3,2,1,0:T(8,128)(2,1)} %get-tuple-element.11.refs_0_, bf16[6,8,144,128]{3,2,1,0:T(8,128)(2,1)} %copy-done), custom_call_target="tpu_custom_call" | custom-call | flops 3737124864 | bytes 6291456 | tf_op jit(solution)/shard_map/inner/pallas_call | solution.py:304
  33.5 0.0 collective-permute-done.1.refs_2_
  33.5 0.0 copy-start.1
  33.5 0.0 collective-permute-done.2.refs_4_
  33.5 0.0 copy-start.2
  33.5 0.7 %collective-permute-start.3 = (bf16[8,160,128]{2,1,0:T(8,128)(2,1)S(1)}, bf16[8,160,128]{2,1,0:T(8,128)(2,1)S(1)}, u32[]{:S(2)}, u32[]{:S(2)}) collective-permute-start(bf16[8,160,128]{2,1,0:T(8,128)(2,1)S(1)} %collective-permute-done.1.refs_2_), channel_id=1, source_target_pairs={{1,0},{0,1},{3,2},{2,3},{5,4},{4,5},{7,6},{6,7},{9,8},{8,9},{11,10... | collective-permute-start | bytes 983048 | tf_op jit(solution)/shard_map/ppermute | solution.py:339
  34.2 0.1 collective-permute-start.4
  34.3 1.2 %collective-permute-done.3.refs_3_ = bf16[8,160,128]{2,1,0:T(8,128)(2,1)S(1)} collective-permute-done((bf16[8,160,128]{2,1,0:T(8,128)(2,1)S(1)}, bf16[8,160,128]{2,1,0:T(8,128)(2,1)S(1)}, u32[]{:S(2)}, u32[]{:S(2)}) %collective-permute-start.3) | collective-permute-done | bytes 327712 | tf_op jit(solution)/shard_map/ppermute | solution.py:339
  35.5 0.0 copy-start.3
  35.5 0.5 collective-permute-done.4.refs_5_
  35.9 0.0 copy-done.1
  35.9 0.0 copy-done.2
  35.9 0.3 copy-done.3
  36.2 0.0 copy-start.4
  36.2 0.7 %copy-done.4 = bf16[8,160,128]{2,1,0:T(8,128)(2,1)} copy-done((bf16[8,160,128]{2,1,0:T(8,128)(2,1)}, bf16[8,160,128]{2,1,0:T(8,128)(2,1)S(1)}, u32[]{:S(2)}) %copy-start.4) | copy-done | bytes 327704
  36.9 13.4 %outer.1 = bf16[144,6,8,128]{3,2,1,0:T(8,128)(2,1)} custom-call(bf16[144,3168]{1,0:T(8,128)(2,1)} %weights.1.w_ref, bf16[11,6,8,128]{3,2,1,0:T(8,128)(2,1)} %a_ref.5, bf16[6,8,144,128]{3,2,1,0:T(8,128)(2,1)} %get-tuple-element.11.refs_0_, bf16[6,8,144,128]{3,2,1,0:T(8,128)(2,1)} %copy-done, ...), custom_call_target="tpu_custom_call", output_to_operand_aliasing={{}: (8, {})} | custom-call | flops 1868562432 | bytes 6291456 | tf_op jit(solution)/shard_map/outer/pallas_call | solution.py:304
Async XLA Ops:
  4.3 8.0 %collective-permute-start = (bf16[6,8,144,128]{3,2,1,0:T(8,128)(2,1)}, bf16[6,8,144,128]{3,2,1,0:T(8,128)(2,1)S(1)}, u32[]{:S(2)}, u32[]{:S(2)}) collective-permute-start(bf16[6,8,144,128]{3,2,1,0:T(8,128)(2,1)} %get-tuple-element.11.refs_0_), channel_id=1, source_target_pairs={{1,0},{0,1},{3,2},{2,3},{5,4},{4,5},{7,6},{6,7},{9,8},{8,9},{11,10... | collective-permute-start | bytes 5308424 | tf_op jit(solution)/shard_map/ppermute | solution.py:339
  4.9 28.5 %collective-permute-start.1 = (bf16[8,160,128]{2,1,0:T(8,128)(2,1)}, bf16[8,160,128]{2,1,0:T(8,128)(2,1)S(1)}, u32[]{:S(2)}, u32[]{:S(2)}) collective-permute-start(bf16[8,160,128]{2,1,0:T(8,128)(2,1)} %get-tuple-element.12), channel_id=1, source_target_pairs={{0,2},{4,6},{8,10},{12,14},{16,18},{20,22},{24,26},{28,30},{2,0},{... | collective-permute-start | bytes 983048 | tf_op jit(solution)/shard_map/ppermute | solution.py:344
  5.2 28.3 %collective-permute-start.2 = (bf16[8,160,128]{2,1,0:T(8,128)(2,1)}, bf16[8,160,128]{2,1,0:T(8,128)(2,1)S(1)}, u32[]{:S(2)}, u32[]{:S(2)}) collective-permute-start(bf16[8,160,128]{2,1,0:T(8,128)(2,1)} %get-tuple-element.13), channel_id=1, source_target_pairs={{2,4},{6,8},{10,12},{14,16},{18,20},{22,24},{26,28},{4,2},{8,6},{1... | collective-permute-start | bytes 983048 | tf_op jit(solution)/shard_map/ppermute | solution.py:344
  12.2 1.2 %copy-start = (bf16[6,8,144,128]{3,2,1,0:T(8,128)(2,1)}, bf16[6,8,144,128]{3,2,1,0:T(8,128)(2,1)S(1)}, u32[]{:S(2)}) copy-start(bf16[6,8,144,128]{3,2,1,0:T(8,128)(2,1)S(1)} %collective-permute-done.refs_1_) | copy-start | bytes 5308420
  33.5 2.5 %copy-start.1 = (bf16[8,160,128]{2,1,0:T(8,128)(2,1)}, bf16[8,160,128]{2,1,0:T(8,128)(2,1)S(1)}, u32[]{:S(2)}) copy-start(bf16[8,160,128]{2,1,0:T(8,128)(2,1)S(1)} %collective-permute-done.1.refs_2_) | copy-start | bytes 983044
  33.5 2.4 %copy-start.2 = (bf16[8,160,128]{2,1,0:T(8,128)(2,1)}, bf16[8,160,128]{2,1,0:T(8,128)(2,1)S(1)}, u32[]{:S(2)}) copy-start(bf16[8,160,128]{2,1,0:T(8,128)(2,1)S(1)} %collective-permute-done.2.refs_4_) | copy-start | bytes 983044
  33.5 2.0 %collective-permute-start.3 = (bf16[8,160,128]{2,1,0:T(8,128)(2,1)S(1)}, bf16[8,160,128]{2,1,0:T(8,128)(2,1)S(1)}, u32[]{:S(2)}, u32[]{:S(2)}) collective-permute-start(bf16[8,160,128]{2,1,0:T(8,128)(2,1)S(1)} %collective-permute-done.1.refs_2_), channel_id=1, source_target_pairs={{1,0},{0,1},{3,2},{2,3},{5,4},{4,5},{7,6},{6,7},{9,8},{8,9},{11,10... | collective-permute-start | bytes 983048 | tf_op jit(solution)/shard_map/ppermute | solution.py:339
  34.2 1.7 %collective-permute-start.4 = (bf16[8,160,128]{2,1,0:T(8,128)(2,1)S(1)}, bf16[8,160,128]{2,1,0:T(8,128)(2,1)S(1)}, u32[]{:S(2)}, u32[]{:S(2)}) collective-permute-start(bf16[8,160,128]{2,1,0:T(8,128)(2,1)S(1)} %collective-permute-done.2.refs_4_), channel_id=1, source_target_pairs={{1,0},{0,1},{3,2},{2,3},{5,4},{4,5},{7,6},{6,7},{9,8},{8,9},{11,10... | collective-permute-start | bytes 983048 | tf_op jit(solution)/shard_map/ppermute | solution.py:339
  35.5 0.7 %copy-start.3 = (bf16[8,160,128]{2,1,0:T(8,128)(2,1)}, bf16[8,160,128]{2,1,0:T(8,128)(2,1)S(1)}, u32[]{:S(2)}) copy-start(bf16[8,160,128]{2,1,0:T(8,128)(2,1)S(1)} %collective-permute-done.3.refs_3_) | copy-start | bytes 983044
  36.2 0.7 %copy-start.4 = (bf16[8,160,128]{2,1,0:T(8,128)(2,1)}, bf16[8,160,128]{2,1,0:T(8,128)(2,1)S(1)}, u32[]{:S(2)}) copy-start(bf16[8,160,128]{2,1,0:T(8,128)(2,1)S(1)} %collective-permute-done.4.refs_5_) | copy-start | bytes 983044

commit v3 on v2

--- a/solution.py
+++ b/solution.py
@@ -43,7 +43,8 @@
     return ref.at[k % ny, pl.ds(modes + ny * (k // ny), ny), :]
 
 
-def turn_kernel(modes, f_ref, a_ref, o_ref, e_ref, d_ref, perm):
+def turn_kernel(modes, f_ref, a_ref, o_ref, e_ref, d_ref, *more):
+    send, perm = more[:-1], more[-1]
     step = pl.program_id(0)
     chunk, nx, ny, nz = f_ref.shape
     terms = a_ref.shape[0]
@@ -70,9 +71,12 @@
     rows = pl.ds(pl.multiple_of(step * chunk, 8), chunk)
     for out, x in outer:
         out[:, rows, :] = o_ref[x]
-
-
-def turn(field, coefs):
+    for out in send:
+        count = out.shape[0]
+        out[...] = o_ref[pl.ds((1 - lax.axis_index(MODE)) * (nx - count), count)]
+
+
+def turn(field, coefs, sent=0):
     modes, nx, ny, nz = field.shape
     chunk = divisor(modes, (48, 72, 64, 32, 16, 8))
     outer = (ny, modes + extra_of(coefs.shape[0], ny), nz)
@@ -85,13 +89,15 @@
             pl.BlockSpec((chunk, nx, ny, nz), lambda i: (i, 0, 0, 0)),
             pl.BlockSpec(coefs.shape, lambda i: (0, 0, 0, 0)),
         ],
-        out_specs=[pl.BlockSpec((nx, ny, chunk, nz), lambda i: (0, 0, i, 0)), whole, whole],
+        out_specs=[pl.BlockSpec((nx, ny, chunk, nz), lambda i: (0, 0, i, 0)), whole, whole]
+        + [pl.BlockSpec((sent, ny, chunk, nz), lambda i: (0, 0, i, 0))] * (sent > 0),
         scratch_shapes=[pltpu.VMEM((block * ny, block * ny), BF16)],
         out_shape=[
             jax.ShapeDtypeStruct((nx, ny, modes, nz), BF16),
             jax.ShapeDtypeStruct(outer, BF16),
             jax.ShapeDtypeStruct(outer, BF16),
-        ],
+        ]
+        + [jax.ShapeDtypeStruct((sent, ny, modes, nz), BF16)] * (sent > 0),
         compiler_params=PARAMS,
         name="turn",
     )(field, coefs)
@@ -124,6 +130,262 @@
     )(coupling)
 
 
+class Engine:
+    def __init__(self, w_refs, terms, f_ref, stage, coef, face, repx, repy, repz, acc, obuf, perm):
+        self.w_refs, self.terms = w_refs, terms
+        self.f_ref, self.stage, self.coef, self.face = f_ref, stage, coef, face
+        self.repx, self.repy, self.repz = repx, repy, repz
+        self.acc, self.obuf, self.perm = acc, obuf, perm
+        _, self.ny, self.total, self.nz = stage.shape
+        self.outs = acc.shape[1]
+        self.block = block_of(self.outs // len(w_refs))
+
+    def prepare(self):
+        self.perm[...] = one_hot(self.ny, self.block)
+        for slot in range(self.f_ref.shape[0]):
+            for y in (0, self.ny + 1):
+                self.f_ref[slot, y] = jnp.zeros((self.total, self.nz), F32)
+
+    def spread(self, at, y):
+        return jnp.broadcast_to(self.face[at + (pl.ds(y, 1), slice(None))], (16, self.nz)).astype(BF16)
+
+    def faces(self, i, c):
+        ny, nz, terms, face = self.ny, self.nz, self.terms, self.face
+        lane = lax.broadcasted_iota(jnp.int32, (ny, nz), 1)
+        row = lax.broadcasted_iota(jnp.int32, (ny, nz), 0)
+        for k in range(terms):
+            a = self.coef[c, k]
+            face[0, k] = a + self.coef[c - 1, k]
+            face[1, k] = a + self.coef[c + 1, k]
+            face[2, k] = a + jnp.where(row > 0, pltpu.roll(a, 1, 0), 0.0)
+            face[3, k] = a + jnp.where(lane > 0, pltpu.roll(a, 1, 1), 0.0)
+            face[4, k] = a + jnp.where(lane < nz - 1, pltpu.roll(a, nz - 1, 1), 0.0)
+            face[5, k] = a
+        for k in range(terms):
+            for y in range(ny):
+                self.repx[i, 0, y, k] = self.spread((0, k), y)
+                self.repx[i, 1, y, k] = self.spread((1, k), y)
+                self.repy[i, y, k] = self.spread((2, k), y)
+                self.repz[i, 0, y, k] = self.spread((3, k), y)
+                self.repz[i, 1, y, k] = self.spread((4, k), y)
+            self.repy[i, ny, k] = self.spread((5, k), ny - 1)
+
+    def widen(self, slot):
+        @pl.loop(0, self.ny)
+        def _(y):
+            self.f_ref[slot, y + 1] = self.stage[slot, y].astype(F32)
+
+    def differences(self, c, y, q):
+        lanes = lax.broadcasted_iota(jnp.int32, (16, self.nz), 1)
+
+        def at(c, y):
+            return self.f_ref[c, y + 1, pl.ds(q, 16), :]
+
+        here = at(c, y)
+        zm = jnp.where(lanes > 0, pltpu.roll(here, 1, 1), 0.0)
+        zp = jnp.where(lanes < self.nz - 1, pltpu.roll(here, self.nz - 1, 1), 0.0)
+        others = (at(c - 1, y), at(c + 1, y), at(c, y - 1), at(c, y + 1), zm, zp)
+        return [(here - v).astype(BF16) for v in others]
+
+    def rows_of(self, i, c, y, q):
+        ds = [self.differences(c, y, q + g) for g in range(0, chunk_of(self.total), 16)]
+        x, z = self.repx, self.repz
+        rows = []
+        for k in range(self.terms):
+            w = (x[i, 0, y, k], x[i, 1, y, k], self.repy[i, y, k], self.repy[i, y + 1, k], z[i, 0, y, k], z[i, 1, y, k])
+            for d in ds:
+                p = [u * v for u, v in zip(d, w)]
+                rows.append((p[0] + p[1]) + (p[2] + p[3]) + (p[4] + p[5]))
+        return rows
+
+    def pair(self, i, c, n):
+        sides = ([], [])
+        for q in range(0, self.total, chunk_of(self.total)):
+            for column in range(2):
+                sides[column].extend(self.rows_of(i, c, 2 * n + column, q))
+        t = jnp.concatenate([jnp.concatenate(side, axis=0) for side in sides], axis=1)
+        w = jnp.concatenate([w_ref[...] for w_ref in self.w_refs], axis=0)
+        r = jnp.dot(w, t, preferred_element_type=F32).astype(BF16)
+        self.acc[2 * n] = r[:, :self.nz]
+        self.acc[2 * n + 1] = r[:, self.nz:]
+
+    def layer(self, i, c):
+        pairs = self.ny // 2
+        unroll = 2 if pairs % 2 == 0 else 1
+
+        @pl.loop(0, pairs // unroll)
+        def _(n):
+            for j in range(unroll):
+                self.pair(i, c, unroll * n + j)
+
+    def finish(self, slot):
+        for p in range(0, self.outs, self.block):
+            rows = self.acc[:, pl.ds(p, self.block), :].reshape(self.ny * self.block, self.nz)
+            rows = permuted(self.perm[...], rows)
+            self.obuf[slot, pl.ds(p, self.block)] = rows.reshape(self.block, self.ny, self.nz)
+
+
+def engine_scratch(slots, items, terms, ny, nz, total, outs, block):
+    return [
+        pltpu.VMEM((slots, ny + 2, total, nz), F32),
+        pltpu.VMEM((slots, ny, total, nz), BF16),
+        pltpu.VMEM((slots, terms, ny, nz), F32),
+        pltpu.VMEM((6, terms, ny, nz), F32),
+        pltpu.VMEM((items, 2, ny, terms, 16, nz), BF16),
+        pltpu.VMEM((items, ny + 1, terms, 16, nz), BF16),
+        pltpu.VMEM((items, 2, ny, terms, 16, nz), BF16),
+        pltpu.VMEM((ny, outs, nz), BF16),
+        pltpu.VMEM((2, outs, ny, nz), BF16),
+        pltpu.VMEM((block * ny, block * ny), BF16),
+    ]
+
+
+def half_kernel(outer, w_ref, w2_ref, a_ref, own, other, *refs):
+    terms, nx, ny, nz = a_ref.shape
+    total = w_ref.shape[1] // terms
+    modes, outs = total // 2, w_ref.shape[0]
+    half = nx // 2
+    me = lax.axis_index(MODE)
+    if outer:
+        halos, refs = refs[:4], refs[5:]
+    out_hbm, give_hbm, *refs = refs
+    engine = Engine((w_ref, w2_ref), terms, *refs[:10])
+    fsem, osem, *more = refs[10:]
+    stage, coef = engine.stage, engine.coef
+    slots, items = coef.shape[0], engine.repx.shape[0]
+    first = me * (half - 1)
+
+    def load(s, slot, ref):
+        rows = pl.ds(pl.multiple_of(lax.rem(me + s, 2) * modes, 8), modes)
+        return pltpu.make_async_copy(ref, stage.at[slot, :, rows, :], fsem.at[s, slot])
+
+    if outer:
+        ends, csem = more
+        even, odd = halos[:2], halos[2:]
+        takes_odd = (me == 0) == (lax.rem(lax.axis_index(GRID), 2) == 0)
+        layer_of = [(1 - me + j, me * (nx - 2) + j) for j in range(2)]
+        end = 2 * me
+        for test, halo in ((takes_odd, odd), (jnp.logical_not(takes_odd), even)):
+            @pl.when(test)
+            def _():
+                for s in range(2):
+                    load(s, end, halo[s].at[:, pl.ds(0, modes), :]).start()
+                pltpu.make_async_copy(halo[0].at[:, pl.ds(modes, ends.shape[1]), :], ends, csem).start()
+    else:
+        layer_of = [(slot, first + slot) for slot in range(slots)]
+    for slot, x in layer_of:
+        load(0, slot, own.at[x]).start()
+        load(1, slot, other.at[x - first]).start()
+    engine.prepare()
+    for slot, x in layer_of:
+        for k in range(terms):
+            coef[slot, k] = 0.5 * a_ref[k, x].astype(F32)
+    if outer:
+        pltpu.make_async_copy(even[0].at[:, pl.ds(modes, ends.shape[1]), :], ends, csem).wait()
+        for k in range(terms):
+            coef[end, k] = 0.5 * coef_rows(ends, k, 0, ny)[...].astype(F32)
+
+    @pl.loop(0, items)
+    def _(i):
+        engine.faces(i, i + 1)
+
+    def arrive(slot):
+        for s in range(2):
+            load(s, slot, own.at[0]).wait()
+        engine.widen(slot)
+
+    def writes(i, slot):
+        x = me * (nx - 1) if outer else first + i + 1
+        return (
+            pltpu.make_async_copy(engine.obuf.at[slot, pl.ds(0, outs)], out_hbm.at[:, x], osem.at[0, slot]),
+            pltpu.make_async_copy(engine.obuf.at[slot, pl.ds(outs, outs)], give_hbm.at[:, i], osem.at[1, slot]),
+        )
+
+    arrive(0)
+    arrive(1)
+
+    @pl.loop(0, items)
+    def _(i):
+        slot = i & 1
+        arrive(i + 2)
+        engine.layer(i, i + 1)
+
+        @pl.when(i > 1)
+        def _():
+            for copy in writes(i - 2, slot):
+                copy.wait()
+
+        engine.finish(slot)
+        for copy in writes(i, slot):
+            copy.start()
+
+    for i in range(max(items - 2, 0), items):
+        for copy in writes(i, i & 1):
+            copy.wait()
+
+
+def half_layers(weights, coefs, own, other, halos=(), out=()):
+    outer = len(halos) > 0
+    terms, nx, ny, nz = coefs.shape
+    outs, depth = weights[0].shape
+    total = depth // terms
+    items = 1 if outer else nx // 2 - 1
+    slots = items + 2
+    block = block_of(outs)
+    operands = [*weights, coefs, own, other, *halos, *out]
+    more = []
+    if outer:
+        more = [pltpu.VMEM((ny, extra_of(terms, ny), nz), BF16), pltpu.SemaphoreType.DMA]
+    return pl.pallas_call(
+        functools.partial(half_kernel, outer),
+        in_specs=[VMEM, VMEM, VMEM] + [HBM] * (len(operands) - 3),
+        out_specs=[HBM, HBM],
+        out_shape=[
+            jax.ShapeDtypeStruct((outs, nx, ny, nz), BF16),
+            jax.ShapeDtypeStruct((outs, items, ny, nz), BF16),
+        ],
+        input_output_aliases={len(operands) - 1: 0} if outer else {},
+        scratch_shapes=[
+            *engine_scratch(slots, items, terms, ny, nz, total, 2 * outs, block),
+            pltpu.SemaphoreType.DMA((2, slots)),
+            pltpu.SemaphoreType.DMA((2, 2)),
+            *more,
+        ],
+        compiler_params=PARAMS,
+        cost_estimate=pl.CostEstimate(
+            flops=4 * outs * depth * items * ny * nz, bytes_accessed=5 * 2**20, transcendentals=0
+        ),
+        name="outer" if outer else "inner",
+    )(*operands)
+
+
+def join_kernel(a_ref, b_ref, _, out_hbm, sem):
+    nx, inner = out_hbm.shape[1], a_ref.shape[1]
+    partner = 1 - lax.axis_index(MODE)
+    first = 1 + partner * inner
+    copies = [
+        pltpu.make_async_copy(a_ref, out_hbm.at[:, pl.ds(first, inner)], sem.at[0]),
+        pltpu.make_async_copy(b_ref, out_hbm.at[:, pl.ds(partner * (nx - 1), 1)], sem.at[1]),
+    ]
+    for copy in copies:
+        copy.start()
+    for copy in copies:
+        copy.wait()
+
+
+def join(inner, outer, out):
+    return pl.pallas_call(
+        join_kernel,
+        in_specs=[VMEM, VMEM, HBM],
+        out_specs=HBM,
+        out_shape=jax.ShapeDtypeStruct(out.shape, BF16),
+        input_output_aliases={2: 0},
+        scratch_shapes=[pltpu.SemaphoreType.DMA((2,))],
+        compiler_params=PARAMS,
+        name="join",
+    )(inner, outer, out)
+
+
 def layers_kernel(sources, outer, w_ref, a_ref, *refs):
     terms, nx, ny, nz = a_ref.shape
     outs, total = w_ref.shape[0], w_ref.shape[1] // terms
@@ -131,12 +393,12 @@
     f_hbm, refs = refs[:sources], refs[sources:]
     if outer:
         even, odd, refs = refs[:sources], refs[sources:2 * sources], refs[2 * sources + 1:]
-    out_hbm, f_ref, stage, coef, face, repx, repy, repz, acc, obuf, perm, fsem, osem, *more = refs
-    slots = f_ref.shape[0]
-    items = repx.shape[0]
+    out_hbm, *refs = refs
+    engine = Engine((w_ref,), terms, *refs[:10])
+    fsem, osem, *more = refs[10:]
+    stage, coef, obuf = engine.stage, engine.coef, engine.obuf
+    slots, items = coef.shape[0], engine.repx.shape[0]
     stride = 3 if outer else 1
-    block = block_of(outs)
-    pairs = ny // 2
     me = lax.axis_index(MODE)
     is_even = lax.rem(lax.axis_index(GRID), 2) == 0
 
@@ -166,12 +428,7 @@
             for s in range(sources):
                 load(s, slot, f_hbm[s].at[layer_of[slot]]).start()
 
-    perm[...] = one_hot(ny, block)
-    lane = lax.broadcasted_iota(jnp.int32, (ny, nz), 1)
-    row = lax.broadcasted_iota(jnp.int32, (ny, nz), 0)
-    for slot in range(slots):
-        for y in (0, ny + 1):
-            f_ref[slot, y] = jnp.zeros((total, nz), F32)
+    engine.prepare()
     if outer:
         for i in range(2):
             pltpu.make_async_copy(even[0].at[:, pl.ds(modes, ends.shape[2]), :], ends.at[i], csem.at[i]).wait()
@@ -183,84 +440,22 @@
                 tile = a_ref[k, layer_of[slot]]
             coef[slot, k] = 0.5 * tile.astype(F32)
 
-    def spread(values, y):
-        return jnp.broadcast_to(values[pl.ds(y, 1), :], (16, nz)).astype(BF16)
-
     @pl.loop(0, items)
     def _(i):
-        c = 1 + stride * i
-        for k in range(terms):
-            a = coef[c, k]
-            face[0, k] = a + coef[c - 1, k]
-            face[1, k] = a + coef[c + 1, k]
-            face[2, k] = a + jnp.where(row > 0, pltpu.roll(a, 1, 0), 0.0)
-            face[3, k] = a + jnp.where(lane > 0, pltpu.roll(a, 1, 1), 0.0)
-            face[4, k] = a + jnp.where(lane < nz - 1, pltpu.roll(a, nz - 1, 1), 0.0)
-            face[5, k] = a
-        for k in range(terms):
-            for y in range(ny):
-                repx[i, 0, y, k] = spread(face.at[0, k], y)
-                repx[i, 1, y, k] = spread(face.at[1, k], y)
-                repy[i, y, k] = spread(face.at[2, k], y)
-                repz[i, 0, y, k] = spread(face.at[3, k], y)
-                repz[i, 1, y, k] = spread(face.at[4, k], y)
-            repy[i, ny, k] = spread(face.at[5, k], ny - 1)
-
-    lanes = lax.broadcasted_iota(jnp.int32, (16, nz), 1)
+        engine.faces(i, 1 + stride * i)
 
     def arrive(slot):
         for s in range(sources):
             load(s, slot, f_hbm[s].at[0]).wait()
-
-        @pl.loop(0, ny)
-        def _(y):
-            f_ref[slot, y + 1] = stage[slot, y].astype(F32)
-
-    def differences(c, y, q):
-        def at(c, y):
-            return f_ref[c, y + 1, pl.ds(q, 16), :]
-
-        here = at(c, y)
-        zm = jnp.where(lanes > 0, pltpu.roll(here, 1, 1), 0.0)
-        zp = jnp.where(lanes < nz - 1, pltpu.roll(here, nz - 1, 1), 0.0)
-        others = (at(c - 1, y), at(c + 1, y), at(c, y - 1), at(c, y + 1), zm, zp)
-        return [(here - v).astype(BF16) for v in others]
-
-    def rows_of(i, c, y, q):
-        ds = [differences(c, y, q + g) for g in range(0, chunk_of(total), 16)]
-        rows = []
-        for k in range(terms):
-            w = (repx[i, 0, y, k], repx[i, 1, y, k], repy[i, y, k], repy[i, y + 1, k], repz[i, 0, y, k], repz[i, 1, y, k])
-            for d in ds:
-                p = [u * v for u, v in zip(d, w)]
-                rows.append((p[0] + p[1]) + (p[2] + p[3]) + (p[4] + p[5]))
-        return rows
-
-    def mix(i, c, slot, pair):
-        sides = ([], [])
-        for q in range(0, total, chunk_of(total)):
-            for column in range(2):
-                sides[column].extend(rows_of(i, c, 2 * pair + column, q))
-        t = jnp.concatenate([jnp.concatenate(side, axis=0) for side in sides], axis=1)
-        r = jnp.dot(w_ref[...], t, preferred_element_type=F32).astype(BF16)
-        acc[2 * pair] = r[:, :nz]
-        acc[2 * pair + 1] = r[:, nz:]
-
-    def finish(slot):
-        for p in range(0, outs, block):
-            rows = acc[:, pl.ds(p, block), :].reshape(ny * block, nz)
-            obuf[slot, pl.ds(p, block)] = permuted(perm[...], rows).reshape(block, ny, nz)
+        engine.widen(slot)
 
     def write(i, slot):
         x = i * (nx - 1) if outer else i + 1
         return pltpu.make_async_copy(obuf.at[slot], out_hbm.at[:, x], osem.at[slot])
 
-    unroll = 2 if pairs % 2 == 0 else 1
-
     @pl.loop(0, items)
     def _(i):
         slot = i & 1
-        c = 1 + stride * i
         if outer:
             for j in range(3):
                 arrive(3 * i + j)
@@ -271,16 +466,13 @@
                 arrive(1)
             arrive(i + 2)
 
-        @pl.loop(0, pairs // unroll)
-        def _(n):
-            for j in range(unroll):
-                mix(i, c, slot, unroll * n + j)
+        engine.layer(i, 1 + stride * i)
 
         @pl.when(i > 1)
         def _():
             write(i - 2, slot).wait()
 
-        finish(slot)
+        engine.finish(slot)
         write(i, slot).start()
 
     for i in range(max(items - 2, 0), items):
@@ -308,16 +500,7 @@
         out_shape=shape,
         input_output_aliases={len(operands) - 1: 0} if outer else {},
         scratch_shapes=[
-            pltpu.VMEM((slots, ny + 2, total, nz), F32),
-            pltpu.VMEM((slots, ny, total, nz), BF16),
-            pltpu.VMEM((slots, terms, ny, nz), F32),
-            pltpu.VMEM((6, terms, ny, nz), F32),
-            pltpu.VMEM((items, 2, ny, terms, 16, nz), BF16),
-            pltpu.VMEM((items, ny + 1, terms, 16, nz), BF16),
-            pltpu.VMEM((items, 2, ny, terms, 16, nz), BF16),
-            pltpu.VMEM((ny, outs, nz), BF16),
-            pltpu.VMEM((2, outs, ny, nz), BF16),
-            pltpu.VMEM((block * ny, block * ny), BF16),
+            *engine_scratch(slots, items, terms, ny, nz, total, outs, block),
             pltpu.SemaphoreType.DMA((sources, slots)),
             pltpu.SemaphoreType.DMA((2,)),
             *more,
@@ -343,7 +526,26 @@
         pairs = [(i, i + 1) for i in range(offset, bricks - 1, 2)]
         return lax.ppermute(block, GRID, pairs + [(b, a) for a, b in pairs])
 
+    def halves(field, coupling, coefs):
+        def swap(block):
+            return lax.ppermute(block, MODE, [(0, 1), (1, 0)])
+
+        weights = weights_of(coupling)
+        weights, field = lax.optimization_barrier((weights, field))
+        weights = (weights, swap(weights))
+        turned, even_out, odd_out, send = turn(field, coefs, coefs.shape[1] // 2 + 1)
+        even_in, odd_in = exchange(even_out, 0), exchange(odd_out, 1)
+        other = swap(send)
+        out, give = half_layers(weights, coefs, turned, other)
+        even_in, odd_in, out, give = lax.optimization_barrier((even_in, odd_in, out, give))
+        inner = swap(give)
+        halos = (even_in, swap(even_in), odd_in, swap(odd_in))
+        out, give = half_layers(weights, coefs, turned, other, halos, (out,))
+        return join(inner, swap(give), out)
+
     def body(field, coupling, coefs):
+        if sources == 2 and coefs.shape[1] % 2 == 0 and coefs.shape[1] >= 4:
+            return halves(field, coupling, coefs)
         turned, even_out, odd_out = turn(field, coefs)
         even_in, odd_in = exchange(even_out, 0), exchange(odd_out, 1)
         fields = around(turned)

time: 50.6 us -> 45.8 us (0.905)
  Pallas kernels: 40.6 us -> 32.6 us
  starting transfers between devices: 5.77 us -> 7 us
  waiting for transfers between devices: 1.65 us -> 2.73 us
  local copies, waits for them, and re-layouts: 2.21 us -> 2.99 us
    pallas_call x2 -> x3, Pallas kernels: 33.4 us -> 25 us  [the longest x2 22.9 us: half_layers(): pl.pallas_call(functools.partial(half_kernel, outer), in_specs=[VMEM, VME...]
    ppermute x3 -> x6, starting transfers between devices: 1.45 us -> 2.68 us  [swap(): return lax.ppermute(block, MODE, [(0, 1), (1, 0)])]
    ppermute x3 -> x6, waiting for transfers between devices: 1.65 us -> 2.73 us  [swap(): return lax.ppermute(block, MODE, [(0, 1), (1, 0)])]
    unnamed x10 -> x18, local copies, waits for them, and re-layouts: 2.21 us -> 2.99 us
  transfers between devices with their start and end apart: 5 -> 8, of which waited for: 2 -> 3; matrix products, arithmetic and copies ran while one was open for 0% -> 0% of each run, Pallas kernels for 46% -> 50%
where the time goes in v3:
time: 45.8 us; the launch traced here: 45.5 us
  Pallas kernels  32.6 us (71%)
  starting transfers between devices  7 us (15%)
  local copies, waits for them, and re-layouts  2.99 us (7%)
  waiting for transfers between devices  2.73 us (6%)
    pallas_call x2, Pallas kernels, half_layers(): pl.pallas_call(functools.partial(half_kernel, outer), in_specs=[VMEM, VME...  22.9 us
    pallas_call x1, Pallas kernels, turn(): pl.pallas_call(functools.partial(turn_kernel, modes), grid=(modes // chun...  4.67 us
    ppermute x2, starting transfers between devices, exchange(): return lax.ppermute(block, GRID, pairs + [(b, a) for a, b in pairs])  4.32 us
    unnamed x18, local copies, waits for them, and re-layouts  2.99 us
    pallas_call x1, Pallas kernels, weights_of(): pl.pallas_call(weights_kernel, in_specs=[VMEM], out_specs=VMEM, out_shape...  2.97 us
    ppermute x6, waiting for transfers between devices, swap(): return lax.ppermute(block, MODE, [(0, 1), (1, 0)])  2.73 us
    ppermute x6, starting transfers between devices, swap(): return lax.ppermute(block, MODE, [(0, 1), (1, 0)])  2.68 us
    pallas_call x1, Pallas kernels, join(): pl.pallas_call(join_kernel, in_specs=[VMEM, VMEM, HBM], out_specs=HBM, ou...  2.06 us
  transfers between devices with their start and end apart: 8, of which 3 were waited for; matrix products, arithmetic and copies ran while one was open for 0% of the time, Pallas kernels for 50%

profile of v3, /device:TPU:27, one launch (start us, length us, event | category | flops | bytes accessed | tf_op | source)
XLA Modules:
  0.0 45.5 jit_solution(17388631875760591884)
XLA Ops:
  0.0 3.0 %weights.1.w_ref = bf16[144,3168]{1,0:T(8,128)(2,1)} custom-call(bf16[11,144,288]{2,1,0:T(8,128)(2,1)} %c_ref.1), custom_call_target="tpu_custom_call" | custom-call | tf_op jit(solution)/shard_map/weights/pallas_call | solution.py:123
  3.0 0.0 copy-start
  3.0 4.7 %turn.1 = (bf16[6,8,144,128]{3,2,1,0:T(8,128)(2,1)}, bf16[8,160,128]{2,1,0:T(8,128)(2,1)}, bf16[8,160,128]{2,1,0:T(8,128)(2,1)}, bf16[4,8,144,128]{3,2,1,0:T(8,128)(2,1)}) custom-call(bf16[144,6,8,128]{3,2,1,0:T(8,128)(2,1)} %f_ref, bf16[11,6,8,128]{3,2,1,0:T(8,128)(2,1)} %a_ref.5), custom_call_target="tpu_custom_call" | custom-call | tf_op jit(solution)/shard_map/turn/pallas_call | solution.py:85
  7.6 0.7 %collective-permute-start.3 = (bf16[4,8,144,128]{3,2,1,0:T(8,128)(2,1)}, bf16[4,8,144,128]{3,2,1,0:T(8,128)(2,1)S(1)}, u32[]{:S(2)}, u32[]{:S(2)}) collective-permute-start(bf16[4,8,144,128]{3,2,1,0:T(8,128)(2,1)} %get-tuple-element.24), channel_id=1, source_target_pairs={{0,1},{1,0},{2,3},{3,2},{4,5},{5,4},{6,7},{7,6},{8,9},{9,8},{10,11... | collective-permute-start | bytes 3538952 | tf_op jit(solution)/shard_map/ppermute | solution.py:531
  8.3 0.0 copy-done
  8.3 0.1 collective-permute-start.2
  8.4 0.3 collective-permute-start
  8.7 4.1 %collective-permute-start.1 = (bf16[8,160,128]{2,1,0:T(8,128)(2,1)}, bf16[8,160,128]{2,1,0:T(8,128)(2,1)S(1)}, u32[]{:S(2)}, u32[]{:S(2)}) collective-permute-start(bf16[8,160,128]{2,1,0:T(8,128)(2,1)} %get-tuple-element.21), channel_id=1, source_target_pairs={{2,4},{6,8},{10,12},{14,16},{18,20},{22,24},{26,28},{4,2},{8,6},{1... | collective-permute-start | bytes 983048 | tf_op jit(solution)/shard_map/ppermute | solution.py:527
  12.7 0.0 collective-permute-done.2.w2_ref
  12.7 0.0 copy-start.2
  12.8 0.0 collective-permute-done.3.other
  12.8 0.0 copy-start.1
  12.8 0.9 %copy-done.2 = bf16[144,3168]{1,0:T(8,128)(2,1)} copy-done((bf16[144,3168]{1,0:T(8,128)(2,1)}, bf16[144,3168]{1,0:T(8,128)(2,1)S(1)}, u32[]{:S(2)}) %copy-start.2) | copy-done | bytes 912408
  13.7 0.4 copy-done.1
  14.1 13.7 %inner.1 = (bf16[144,6,8,128]{3,2,1,0:T(8,128)(2,1)}, bf16[144,2,8,128]{3,2,1,0:T(8,128)(2,1)}) custom-call(bf16[144,3168]{1,0:T(8,128)(2,1)} %weights.1.w_ref, bf16[144,3168]{1,0:T(8,128)(2,1)} %copy-done.2, bf16[11,6,8,128]{3,2,1,0:T(8,128)(2,1)} %a_ref.5, bf16[6,8,144,128]{3,2,1,0:T(8,128)(2,1)} %get-tuple-element.23.own, bf16[4,8,144,128]{3,2,1,0:T(8,128)(2,1)} %copy-done.1), custom_call_target="tpu_custom_call" | custom-call | flops 3737124864 | bytes 5242880 | tf_op jit(solution)/shard_map/inner/pallas_call | solution.py:339
  27.8 0.0 collective-permute-done.refs_0_
  27.8 0.0 copy-start.4
  27.8 0.0 collective-permute-done.1.refs_2_
  27.8 0.0 copy-start.5
  27.8 1.1 %collective-permute-start.5 = (bf16[8,160,128]{2,1,0:T(8,128)(2,1)S(1)}, bf16[8,160,128]{2,1,0:T(8,128)(2,1)S(1)}, u32[]{:S(2)}, u32[]{:S(2)}) collective-permute-start(bf16[8,160,128]{2,1,0:T(8,128)(2,1)S(1)} %collective-permute-done.refs_0_), channel_id=1, source_target_pairs={{0,1},{1,0},{2,3},{3,2},{4,5},{5,4},{6,7},{7,6},{8,9},{9,8},{10,11... | collective-permute-start | bytes 983048 | tf_op jit(solution)/shard_map/ppermute | solution.py:531
  28.9 0.1 collective-permute-start.6
  29.0 0.4 collective-permute-start.4
  29.4 0.7 %collective-permute-done.5.refs_1_ = bf16[8,160,128]{2,1,0:T(8,128)(2,1)S(1)} collective-permute-done((bf16[8,160,128]{2,1,0:T(8,128)(2,1)S(1)}, bf16[8,160,128]{2,1,0:T(8,128)(2,1)S(1)}, u32[]{:S(2)}, u32[]{:S(2)}) %collective-permute-start.5) | collective-permute-done | bytes 327712 | tf_op jit(solution)/shard_map/ppermute | solution.py:531
  30.2 0.0 copy-start.6
  30.2 0.5 %collective-permute-done.6.refs_3_ = bf16[8,160,128]{2,1,0:T(8,128)(2,1)S(1)} collective-permute-done((bf16[8,160,128]{2,1,0:T(8,128)(2,1)S(1)}, bf16[8,160,128]{2,1,0:T(8,128)(2,1)S(1)}, u32[]{:S(2)}, u32[]{:S(2)}) %collective-permute-start.6) | collective-permute-done | bytes 327712 | tf_op jit(solution)/shard_map/ppermute | solution.py:531
  30.6 0.0 copy-done.4
  30.6 0.0 copy-done.5
  30.6 0.2 copy-done.6
  30.9 0.0 copy-start.7
  30.9 0.7 %copy-done.7 = bf16[8,160,128]{2,1,0:T(8,128)(2,1)} copy-done((bf16[8,160,128]{2,1,0:T(8,128)(2,1)}, bf16[8,160,128]{2,1,0:T(8,128)(2,1)S(1)}, u32[]{:S(2)}) %copy-start.7) | copy-done | bytes 327704
  31.6 9.2 %outer.1 = (bf16[144,6,8,128]{3,2,1,0:T(8,128)(2,1)}, bf16[144,1,8,128]{3,2,1,0:T(8,128)(2,1)}) custom-call(bf16[144,3168]{1,0:T(8,128)(2,1)} %weights.1.w_ref, bf16[144,3168]{1,0:T(8,128)(2,1)} %copy-done.2, bf16[11,6,8,128]{3,2,1,0:T(8,128)(2,1)} %a_ref.5, bf16[6,8,144,128]{3,2,1,0:T(8,128)(2,1)} %get-tuple-element.23.own, ...), custom_call_target="tpu_custom_call", output_to_operand_aliasing={{0}: (9, {})} | custom-call | flops 1868562432 | bytes 5242880 | tf_op jit(solution)/shard_map/outer/pallas_call | solution.py:339
  40.8 0.3 collective-permute-start.7
  41.2 0.0 collective-permute-done.4.a_ref
  41.2 0.0 copy-start.3
  41.2 1.5 %collective-permute-done.7.b_ref = bf16[144,1,8,128]{3,2,1,0:T(8,128)(2,1)S(1)} collective-permute-done((bf16[144,1,8,128]{3,2,1,0:T(8,128)(2,1)}, bf16[144,1,8,128]{3,2,1,0:T(8,128)(2,1)S(1)}, u32[]{:S(2)}, u32[]{:S(2)}) %collective-permute-start.7) | collective-permute-done | bytes 294944 | tf_op jit(solution)/shard_map/ppermute | solution.py:531
  42.7 0.0 copy-start.8
  42.7 0.0 copy-done.3
  42.7 0.7 %copy-done.8 = bf16[144,1,8,128]{3,2,1,0:T(8,128)(2,1)} copy-done((bf16[144,1,8,128]{3,2,1,0:T(8,128)(2,1)}, bf16[144,1,8,128]{3,2,1,0:T(8,128)(2,1)S(1)}, u32[]{:S(2)}) %copy-start.8) | copy-done | bytes 294936
  43.4 2.1 %join.1 = bf16[144,6,8,128]{3,2,1,0:T(8,128)(2,1)} custom-call(bf16[144,2,8,128]{3,2,1,0:T(8,128)(2,1)} %copy-done.3, bf16[144,1,8,128]{3,2,1,0:T(8,128)(2,1)} %copy-done.8, bf16[144,6,8,128]{3,2,1,0:T(8,128)(2,1)} %get-tuple-element.32._), custom_call_target="tpu_custom_call", output_to_operand_aliasing={{}: (2, {})} | custom-call | tf_op jit(solution)/shard_map/join/pallas_call | solution.py:377
Async XLA Ops:
  3.0 5.4 %copy-start = (bf16[144,3168]{1,0:T(8,128)(2,1)S(1)}, bf16[144,3168]{1,0:T(8,128)(2,1)}, u32[]{:S(2)}) copy-start(bf16[144,3168]{1,0:T(8,128)(2,1)} %weights.1.w_ref) | copy-start | bytes 2737156
  7.6 5.1 %collective-permute-start.3 = (bf16[4,8,144,128]{3,2,1,0:T(8,128)(2,1)}, bf16[4,8,144,128]{3,2,1,0:T(8,128)(2,1)S(1)}, u32[]{:S(2)}, u32[]{:S(2)}) collective-permute-start(bf16[4,8,144,128]{3,2,1,0:T(8,128)(2,1)} %get-tuple-element.24), channel_id=1, source_target_pairs={{0,1},{1,0},{2,3},{3,2},{4,5},{5,4},{6,7},{7,6},{8,9},{9,8},{10,11... | collective-permute-start | bytes 3538952 | tf_op jit(solution)/shard_map/ppermute | solution.py:531
  8.3 4.4 %collective-permute-start.2 = (bf16[144,3168]{1,0:T(8,128)(2,1)S(1)}, bf16[144,3168]{1,0:T(8,128)(2,1)S(1)}, u32[]{:S(2)}, u32[]{:S(2)}) collective-permute-start(bf16[144,3168]{1,0:T(8,128)(2,1)S(1)} %copy-done), channel_id=1, source_target_pairs={{0,1},{1,0},{2,3},{3,2},{4,5},{5,4},{6,7},{7,6},{8,9},{9,8},{10,11... | collective-permute-start | bytes 2737160 | tf_op jit(solution)/shard_map/ppermute | solution.py:531
  8.4 19.4 %collective-permute-start = (bf16[8,160,128]{2,1,0:T(8,128)(2,1)}, bf16[8,160,128]{2,1,0:T(8,128)(2,1)S(1)}, u32[]{:S(2)}, u32[]{:S(2)}) collective-permute-start(bf16[8,160,128]{2,1,0:T(8,128)(2,1)} %get-tuple-element.20), channel_id=1, source_target_pairs={{0,2},{4,6},{8,10},{12,14},{16,18},{20,22},{24,26},{28,30},{2,0},{... | collective-permute-start | bytes 983048 | tf_op jit(solution)/shard_map/ppermute | solution.py:527
  8.7 19.2 %collective-permute-start.1 = (bf16[8,160,128]{2,1,0:T(8,128)(2,1)}, bf16[8,160,128]{2,1,0:T(8,128)(2,1)S(1)}, u32[]{:S(2)}, u32[]{:S(2)}) collective-permute-start(bf16[8,160,128]{2,1,0:T(8,128)(2,1)} %get-tuple-element.21), channel_id=1, source_target_pairs={{2,4},{6,8},{10,12},{14,16},{18,20},{22,24},{26,28},{4,2},{8,6},{1... | collective-permute-start | bytes 983048 | tf_op jit(solution)/shard_map/ppermute | solution.py:527
  12.7 0.9 %copy-start.2 = (bf16[144,3168]{1,0:T(8,128)(2,1)}, bf16[144,3168]{1,0:T(8,128)(2,1)S(1)}, u32[]{:S(2)}) copy-start(bf16[144,3168]{1,0:T(8,128)(2,1)S(1)} %collective-permute-done.2.w2_ref) | copy-start | bytes 2737156
  12.8 1.3 %copy-start.1 = (bf16[4,8,144,128]{3,2,1,0:T(8,128)(2,1)}, bf16[4,8,144,128]{3,2,1,0:T(8,128)(2,1)S(1)}, u32[]{:S(2)}) copy-start(bf16[4,8,144,128]{3,2,1,0:T(8,128)(2,1)S(1)} %collective-permute-done.3.other) | copy-start | bytes 3538948
  27.8 2.8 %copy-start.4 = (bf16[8,160,128]{2,1,0:T(8,128)(2,1)}, bf16[8,160,128]{2,1,0:T(8,128)(2,1)S(1)}, u32[]{:S(2)}) copy-start(bf16[8,160,128]{2,1,0:T(8,128)(2,1)S(1)} %collective-permute-done.refs_0_) | copy-start | bytes 983044
  27.8 2.8 %copy-start.5 = (bf16[8,160,128]{2,1,0:T(8,128)(2,1)}, bf16[8,160,128]{2,1,0:T(8,128)(2,1)S(1)}, u32[]{:S(2)}) copy-start(bf16[8,160,128]{2,1,0:T(8,128)(2,1)S(1)} %collective-permute-done.1.refs_2_) | copy-start | bytes 983044
  27.8 2.3 %collective-permute-start.5 = (bf16[8,160,128]{2,1,0:T(8,128)(2,1)S(1)}, bf16[8,160,128]{2,1,0:T(8,128)(2,1)S(1)}, u32[]{:S(2)}, u32[]{:S(2)}) collective-permute-start(bf16[8,160,128]{2,1,0:T(8,128)(2,1)S(1)} %collective-permute-done.refs_0_), channel_id=1, source_target_pairs={{0,1},{1,0},{2,3},{3,2},{4,5},{5,4},{6,7},{7,6},{8,9},{9,8},{10,11... | collective-permute-start | bytes 983048 | tf_op jit(solution)/shard_map/ppermute | solution.py:531
  28.9 1.7 %collective-permute-start.6 = (bf16[8,160,128]{2,1,0:T(8,128)(2,1)S(1)}, bf16[8,160,128]{2,1,0:T(8,128)(2,1)S(1)}, u32[]{:S(2)}, u32[]{:S(2)}) collective-permute-start(bf16[8,160,128]{2,1,0:T(8,128)(2,1)S(1)} %collective-permute-done.1.refs_2_), channel_id=1, source_target_pairs={{0,1},{1,0},{2,3},{3,2},{4,5},{5,4},{6,7},{7,6},{8,9},{9,8},{10,11... | collective-permute-start | bytes 983048 | tf_op jit(solution)/shard_map/ppermute | solution.py:531
  29.0 12.2 %collective-permute-start.4 = (bf16[144,2,8,128]{3,2,1,0:T(8,128)(2,1)}, bf16[144,2,8,128]{3,2,1,0:T(8,128)(2,1)S(1)}, u32[]{:S(2)}, u32[]{:S(2)}) collective-permute-start(bf16[144,2,8,128]{3,2,1,0:T(8,128)(2,1)} %get-tuple-element.27), channel_id=1, source_target_pairs={{0,1},{1,0},{2,3},{3,2},{4,5},{5,4},{6,7},{7,6},{8,9},{9,8},{10,11... | collective-permute-start | bytes 1769480 | tf_op jit(solution)/shard_map/ppermute | solution.py:531
  30.2 0.7 %copy-start.6 = (bf16[8,160,128]{2,1,0:T(8,128)(2,1)}, bf16[8,160,128]{2,1,0:T(8,128)(2,1)S(1)}, u32[]{:S(2)}) copy-start(bf16[8,160,128]{2,1,0:T(8,128)(2,1)S(1)} %collective-permute-done.5.refs_1_) | copy-start | bytes 983044
  30.9 0.7 %copy-start.7 = (bf16[8,160,128]{2,1,0:T(8,128)(2,1)}, bf16[8,160,128]{2,1,0:T(8,128)(2,1)S(1)}, u32[]{:S(2)}) copy-start(bf16[8,160,128]{2,1,0:T(8,128)(2,1)S(1)} %collective-permute-done.6.refs_3_) | copy-start | bytes 983044
  40.8 1.9 %collective-permute-start.7 = (bf16[144,1,8,128]{3,2,1,0:T(8,128)(2,1)}, bf16[144,1,8,128]{3,2,1,0:T(8,128)(2,1)S(1)}, u32[]{:S(2)}, u32[]{:S(2)}) collective-permute-start(bf16[144,1,8,128]{3,2,1,0:T(8,128)(2,1)} %get-tuple-element.31), channel_id=1, source_target_pairs={{0,1},{1,0},{2,3},{3,2},{4,5},{5,4},{6,7},{7,6},{8,9},{9,8},{10,11... | collective-permute-start | bytes 884744 | tf_op jit(solution)/shard_map/ppermute | solution.py:531
  41.2 1.5 %copy-start.3 = (bf16[144,2,8,128]{3,2,1,0:T(8,128)(2,1)}, bf16[144,2,8,128]{3,2,1,0:T(8,128)(2,1)S(1)}, u32[]{:S(2)}) copy-start(bf16[144,2,8,128]{3,2,1,0:T(8,128)(2,1)S(1)} %collective-permute-done.4.a_ref) | copy-start | bytes 1769476
  42.7 0.7 %copy-start.8 = (bf16[144,1,8,128]{3,2,1,0:T(8,128)(2,1)}, bf16[144,1,8,128]{3,2,1,0:T(8,128)(2,1)S(1)}, u32[]{:S(2)}) copy-start(bf16[144,1,8,128]{3,2,1,0:T(8,128)(2,1)S(1)} %collective-permute-done.7.b_ref) | copy-start | bytes 884740

commit v4 on v3

--- a/solution.py
+++ b/solution.py
@@ -1,4 +1,5 @@
 import functools
+import math
 
 import jax
 import jax.numpy as jnp
@@ -9,9 +10,14 @@
 
 BF16 = jnp.bfloat16
 F32 = jnp.float32
-VMEM_LIMIT = 60 * 2**20
 MODE, GRID = "mode", "grid"
-PARAMS = pltpu.CompilerParams(vmem_limit_bytes=VMEM_LIMIT)
+
+
+def grant(*parts):
+    size = sum(math.prod(p.shape) * jnp.dtype(p.dtype).itemsize for p in parts)
+    return pltpu.CompilerParams(vmem_limit_bytes=min(size + 10 * 2**20, 60 * 2**20))
+
+
 VMEM = pl.BlockSpec(memory_space=pltpu.VMEM)
 HBM = pl.BlockSpec(memory_space=pl.ANY)
 
@@ -43,7 +49,7 @@
     return ref.at[k % ny, pl.ds(modes + ny * (k // ny), ny), :]
 
 
-def turn_kernel(modes, f_ref, a_ref, o_ref, e_ref, d_ref, *more):
+def turn_kernel(modes, f_ref, a_ref, c_ref, o_ref, e_ref, d_ref, w_ref, *more):
     send, perm = more[:-1], more[-1]
     step = pl.program_id(0)
     chunk, nx, ny, nz = f_ref.shape
@@ -58,6 +64,7 @@
         for out, x in outer:
             for k in range(terms):
                 coef_rows(out, k, modes, ny)[...] = a_ref[k, x]
+        arrange(c_ref, w_ref)
 
     layers = 2 if nx % 2 == 0 else 1
     for x in range(0, nx, layers):
@@ -76,9 +83,10 @@
         out[...] = o_ref[pl.ds((1 - lax.axis_index(MODE)) * (nx - count), count)]
 
 
-def turn(field, coefs, sent=0):
+def turn(field, coefs, coupling, sent=0):
     modes, nx, ny, nz = field.shape
-    chunk = divisor(modes, (48, 72, 64, 32, 16, 8))
+    terms, outs, total = coupling.shape
+    chunk = divisor(modes, (72, 48, 64, 32, 16, 8))
     outer = (ny, modes + extra_of(coefs.shape[0], ny), nz)
     block = block_of(chunk)
     whole = pl.BlockSpec(outer, lambda i: (0, 0, 0))
@@ -88,26 +96,29 @@
         in_specs=[
             pl.BlockSpec((chunk, nx, ny, nz), lambda i: (i, 0, 0, 0)),
             pl.BlockSpec(coefs.shape, lambda i: (0, 0, 0, 0)),
+            pl.BlockSpec(coupling.shape, lambda i: (0, 0, 0)),
         ],
         out_specs=[pl.BlockSpec((nx, ny, chunk, nz), lambda i: (0, 0, i, 0)), whole, whole]
+        + [pl.BlockSpec((outs, terms * total), lambda i: (0, 0))]
         + [pl.BlockSpec((sent, ny, chunk, nz), lambda i: (0, 0, i, 0))] * (sent > 0),
         scratch_shapes=[pltpu.VMEM((block * ny, block * ny), BF16)],
         out_shape=[
             jax.ShapeDtypeStruct((nx, ny, modes, nz), BF16),
             jax.ShapeDtypeStruct(outer, BF16),
             jax.ShapeDtypeStruct(outer, BF16),
+            jax.ShapeDtypeStruct((outs, terms * total), BF16),
         ]
         + [jax.ShapeDtypeStruct((sent, ny, modes, nz), BF16)] * (sent > 0),
-        compiler_params=PARAMS,
+        compiler_params=grant(field, field, field, field, coefs, coupling, coupling, coupling, coupling),
         name="turn",
-    )(field, coefs)
+    )(field, coefs, coupling)
 
 
 def chunk_of(total):
     return divisor(total, (32, 16))
 
 
-def weights_kernel(c_ref, o_ref):
+def arrange(c_ref, o_ref):
     terms, _, total = c_ref.shape
     chunk = chunk_of(total)
     pieces = [(k, q) for q in range(0, total, chunk) for k in range(terms)]
@@ -116,18 +127,6 @@
         group = pieces[i:i + per]
         wide = jnp.concatenate([c_ref[k, :, q:q + chunk] for k, q in group], axis=1)
         o_ref[:, i * chunk:i * chunk + len(group) * chunk] = wide
-
-
-def weights_of(coupling):
-    terms, outs, total = coupling.shape
-    return pl.pallas_call(
-        weights_kernel,
-        in_specs=[VMEM],
-        out_specs=VMEM,
-        out_shape=jax.ShapeDtypeStruct((outs, terms * total), BF16),
-        compiler_params=PARAMS,
-        name="weights",
-    )(coupling)
 
 
 class Engine:
@@ -181,28 +180,33 @@
         def at(c, y):
             return self.f_ref[c, y + 1, pl.ds(q, 16), :]
 
-        here = at(c, y)
-        zm = jnp.where(lanes > 0, pltpu.roll(here, 1, 1), 0.0)
-        zp = jnp.where(lanes < self.nz - 1, pltpu.roll(here, self.nz - 1, 1), 0.0)
-        others = (at(c - 1, y), at(c + 1, y), at(c, y - 1), at(c, y + 1), zm, zp)
-        return [(here - v).astype(BF16) for v in others]
+        def shifted(v, by, edge):
+            return jnp.where(lanes != edge, pltpu.roll(v, by, 1), 0.0)
+
+        a, b = at(c, y), at(c, y + 1)
+        near = (at(c - 1, y), at(c + 1, y), at(c, y - 1), b, shifted(a, 1, 0), shifted(a, self.nz - 1, self.nz - 1))
+        far = (at(c - 1, y + 1), at(c + 1, y + 1), at(c, y + 2), shifted(b, 1, 0), shifted(b, self.nz - 1, self.nz - 1))
+        return [(a - v).astype(BF16) for v in near], [(b - v).astype(BF16) for v in far]
 
     def rows_of(self, i, c, y, q):
-        ds = [self.differences(c, y, q + g) for g in range(0, chunk_of(self.total), 16)]
-        x, z = self.repx, self.repz
-        rows = []
+        x, yf, z = self.repx, self.repy, self.repz
+        both = [self.differences(c, y, q + g) for g in range(0, chunk_of(self.total), 16)]
+        sides = ([], [])
         for k in range(self.terms):
-            w = (x[i, 0, y, k], x[i, 1, y, k], self.repy[i, y, k], self.repy[i, y + 1, k], z[i, 0, y, k], z[i, 1, y, k])
-            for d in ds:
-                p = [u * v for u, v in zip(d, w)]
-                rows.append((p[0] + p[1]) + (p[2] + p[3]) + (p[4] + p[5]))
-        return rows
+            for near, far in both:
+                shared = near[3] * yf[i, y + 1, k]
+                for j, d, own in ((0, near, near[2] * yf[i, y, k]), (1, far, far[2] * yf[i, y + 2, k])):
+                    along_x = d[0] * x[i, 0, y + j, k] + d[1] * x[i, 1, y + j, k]
+                    along_y = own + shared if j == 0 else own - shared
+                    along_z = d[-2] * z[i, 0, y + j, k] + d[-1] * z[i, 1, y + j, k]
+                    sides[j].append(along_x + along_y + along_z)
+        return sides
 
     def pair(self, i, c, n):
         sides = ([], [])
         for q in range(0, self.total, chunk_of(self.total)):
-            for column in range(2):
-                sides[column].extend(self.rows_of(i, c, 2 * n + column, q))
+            for side, rows in zip(sides, self.rows_of(i, c, 2 * n, q)):
+                side.extend(rows)
         t = jnp.concatenate([jnp.concatenate(side, axis=0) for side in sides], axis=1)
         w = jnp.concatenate([w_ref[...] for w_ref in self.w_refs], axis=0)
         r = jnp.dot(w, t, preferred_element_type=F32).astype(BF16)
@@ -333,6 +337,7 @@
     slots = items + 2
     block = block_of(outs)
     operands = [*weights, coefs, own, other, *halos, *out]
+    scratch = engine_scratch(slots, items, terms, ny, nz, total, 2 * outs, block)
     more = []
     if outer:
         more = [pltpu.VMEM((ny, extra_of(terms, ny), nz), BF16), pltpu.SemaphoreType.DMA]
@@ -346,12 +351,12 @@
         ],
         input_output_aliases={len(operands) - 1: 0} if outer else {},
         scratch_shapes=[
-            *engine_scratch(slots, items, terms, ny, nz, total, 2 * outs, block),
+            *scratch,
             pltpu.SemaphoreType.DMA((2, slots)),
             pltpu.SemaphoreType.DMA((2, 2)),
             *more,
         ],
-        compiler_params=PARAMS,
+        compiler_params=grant(*scratch, *weights, coefs),
         cost_estimate=pl.CostEstimate(
             flops=4 * outs * depth * items * ny * nz, bytes_accessed=5 * 2**20, transcendentals=0
         ),
@@ -381,7 +386,7 @@
         out_shape=jax.ShapeDtypeStruct(out.shape, BF16),
         input_output_aliases={2: 0},
         scratch_shapes=[pltpu.SemaphoreType.DMA((2,))],
-        compiler_params=PARAMS,
+        compiler_params=grant(inner, outer),
         name="join",
     )(inner, outer, out)
 
@@ -490,6 +495,7 @@
     slots = 6 if outer else nx
     shape = jax.ShapeDtypeStruct((outs, nx, ny, nz), BF16)
     operands = [weights, coefs, *fields] + ([*halos[0], *halos[1], out] if outer else [])
+    scratch = engine_scratch(slots, items, terms, ny, nz, total, outs, block)
     more = []
     if outer:
         more = [pltpu.VMEM((2, ny, extra_of(terms, ny), nz), BF16), pltpu.SemaphoreType.DMA((2,))]
@@ -500,12 +506,12 @@
         out_shape=shape,
         input_output_aliases={len(operands) - 1: 0} if outer else {},
         scratch_shapes=[
-            *engine_scratch(slots, items, terms, ny, nz, total, outs, block),
+            *scratch,
             pltpu.SemaphoreType.DMA((sources, slots)),
             pltpu.SemaphoreType.DMA((2,)),
             *more,
         ],
-        compiler_params=PARAMS,
+        compiler_params=grant(*scratch, weights, coefs),
         cost_estimate=pl.CostEstimate(
             flops=2 * outs * depth * items * ny * nz, bytes_accessed=6 * 2**20, transcendentals=0
         ),
@@ -530,10 +536,8 @@
         def swap(block):
             return lax.ppermute(block, MODE, [(0, 1), (1, 0)])
 
-        weights = weights_of(coupling)
-        weights, field = lax.optimization_barrier((weights, field))
+        turned, even_out, odd_out, weights, send = turn(field, coefs, coupling, coefs.shape[1] // 2 + 1)
         weights = (weights, swap(weights))
-        turned, even_out, odd_out, send = turn(field, coefs, coefs.shape[1] // 2 + 1)
         even_in, odd_in = exchange(even_out, 0), exchange(odd_out, 1)
         other = swap(send)
         out, give = half_layers(weights, coefs, turned, other)
@@ -546,10 +550,9 @@
     def body(field, coupling, coefs):
         if sources == 2 and coefs.shape[1] % 2 == 0 and coefs.shape[1] >= 4:
             return halves(field, coupling, coefs)
-        turned, even_out, odd_out = turn(field, coefs)
+        turned, even_out, odd_out, weights = turn(field, coefs, coupling)
         even_in, odd_in = exchange(even_out, 0), exchange(odd_out, 1)
         fields = around(turned)
-        weights = weights_of(coupling)
         out = layers(weights, coefs, fields)
         even_in, odd_in, out = lax.optimization_barrier((even_in, odd_in, out))
         return layers(weights, coefs, fields, (around(even_in), around(odd_in)), out)

time: 45.8 us -> 35.7 us (0.78)
  Pallas kernels: 32.6 us -> 21 us
  local copies, waits for them, and re-layouts: 2.99 us -> 3.67 us
  waiting for transfers between devices: 2.73 us -> 3.37 us
    pallas_call x2, Pallas kernels: 22.9 us -> 18 us  [half_layers(): pl.pallas_call(functools.partial(half_kernel, outer), in_specs=[VMEM, VME...]
    pallas_call x1 -> x0, Pallas kernels: 2.97 us -> none  [weights_of(): pl.pallas_call(weights_kernel, in_specs=[VMEM], out_specs=VMEM, out_shape...]
    pallas_call x1, Pallas kernels: 4.67 us -> 2.06 us  [turn(): pl.pallas_call(functools.partial(turn_kernel, modes), grid=(modes // chun...]
    pallas_call x1, Pallas kernels: 2.06 us -> 0.92 us  [join(): pl.pallas_call(join_kernel, in_specs=[VMEM, VMEM, HBM], out_specs=HBM, ou...]
    ppermute x2, waiting for transfers between devices: 0.01 us -> 0.95 us  [exchange(): return lax.ppermute(block, GRID, pairs + [(b, a) for a, b in pairs])]
    unnamed x18 -> x8, local copies, waits for them, and re-layouts: 2.99 us -> 3.67 us
  transfers between devices with their start and end apart: 8 -> 8, of which waited for: 3 -> 4; matrix products, arithmetic and copies ran while one was open for 0% -> 0% of each run, Pallas kernels for 50% -> 51%
where the time goes in v4:
time: 35.7 us; the launch traced here: 35.5 us
  Pallas kernels  21 us (59%)
  starting transfers between devices  7.39 us (21%)
  local copies, waits for them, and re-layouts  3.67 us (10%)
  waiting for transfers between devices  3.37 us (9%)
    pallas_call x2, Pallas kernels, half_layers(): pl.pallas_call(functools.partial(half_kernel, outer), in_specs=[VMEM, VME...  18 us
    ppermute x2, starting transfers between devices, exchange(): return lax.ppermute(block, GRID, pairs + [(b, a) for a, b in pairs])  4.32 us
    unnamed x8, local copies, waits for them, and re-layouts  3.67 us
    ppermute x6, starting transfers between devices, swap(): return lax.ppermute(block, MODE, [(0, 1), (1, 0)])  3.07 us
    ppermute x6, waiting for transfers between devices, swap(): return lax.ppermute(block, MODE, [(0, 1), (1, 0)])  2.43 us
    pallas_call x1, Pallas kernels, turn(): pl.pallas_call(functools.partial(turn_kernel, modes), grid=(modes // chun...  2.06 us
    ppermute x2, waiting for transfers between devices, exchange(): return lax.ppermute(block, GRID, pairs + [(b, a) for a, b in pairs])  0.95 us
    pallas_call x1, Pallas kernels, join(): pl.pallas_call(join_kernel, in_specs=[VMEM, VMEM, HBM], out_specs=HBM, ou...  0.92 us
  transfers between devices with their start and end apart: 8, of which 4 were waited for; matrix products, arithmetic and copies ran while one was open for 0% of the time, Pallas kernels for 51%

profile of v4, /device:TPU:27, one launch (start us, length us, event | category | flops | bytes accessed | tf_op | source)
XLA Modules:
  0.0 35.5 jit_solution(4703193390214865545)
XLA Ops:
  0.0 0.0 copy-start
  0.0 1.5 %copy-done = bf16[144,6,8,128]{3,2,1,0:T(8,128)(2,1)S(1)} copy-done((bf16[144,6,8,128]{3,2,1,0:T(8,128)(2,1)S(1)}, bf16[144,6,8,128]{3,2,1,0:T(8,128)(2,1)}, u32[]{:S(2)}) %copy-start) | copy-done | bytes 1769496
  1.5 0.0 copy-start.1
  1.5 1.3 %copy-done.1 = bf16[11,144,288]{2,1,0:T(8,128)(2,1)S(1)} copy-done((bf16[11,144,288]{2,1,0:T(8,128)(2,1)S(1)}, bf16[11,144,288]{2,1,0:T(8,128)(2,1)}, u32[]{:S(2)}) %copy-start.1) | copy-done | bytes 912408
  2.8 0.0 copy-start.2
  2.8 0.9 %copy-done.2 = bf16[11,6,8,128]{3,2,1,0:T(8,128)(2,1)S(1)} copy-done((bf16[11,6,8,128]{3,2,1,0:T(8,128)(2,1)S(1)}, bf16[11,6,8,128]{3,2,1,0:T(8,128)(2,1)}, u32[]{:S(2)}) %copy-start.2) | copy-done | bytes 135192
  3.7 0.0 copy-start.3
  3.7 2.1 %turn.1 = (bf16[6,8,144,128]{3,2,1,0:T(8,128)(2,1)S(1)}, bf16[8,160,128]{2,1,0:T(8,128)(2,1)S(1)}, bf16[8,160,128]{2,1,0:T(8,128)(2,1)S(1)}, bf16[144,3168]{1,0:T(8,128)(2,1)S(1)}, bf16[4,8,144,128]{3,2,1,0:T(8,128)(2,1)S(1)}) custom-call(bf16[144,6,8,128]{3,2,1,0:T(8,128)(2,1)S(1)} %copy-done, bf16[11,6,8,128]{3,2,1,0:T(8,128)(2,1)S(1)} %copy-done.2, ...), custom_call_target="tpu_custom_call" | custom-call | tf_op jit(solution)/shard_map/turn/pallas_call | solution.py:93
  5.7 0.8 %collective-permute-start.3 = (bf16[4,8,144,128]{3,2,1,0:T(8,128)(2,1)S(1)}, bf16[4,8,144,128]{3,2,1,0:T(8,128)(2,1)S(1)}, u32[]{:S(2)}, u32[]{:S(2)}) collective-permute-start(bf16[4,8,144,128]{3,2,1,0:T(8,128)(2,1)S(1)} %get-tuple-element.22), channel_id=1, source_target_pairs={{0,1},{1,0},{2,3},{3,2},{4,5},{5,4},{6,7},{7,6},{8,9},{9,8},{10,11... | collective-permute-start | bytes 3538952 | tf_op jit(solution)/shard_map/ppermute | solution.py:537
  6.5 0.1 collective-permute-start.2
  6.6 0.3 collective-permute-start
  6.8 4.1 %collective-permute-start.1 = (bf16[8,160,128]{2,1,0:T(8,128)(2,1)S(1)}, bf16[8,160,128]{2,1,0:T(8,128)(2,1)S(1)}, u32[]{:S(2)}, u32[]{:S(2)}) collective-permute-start(bf16[8,160,128]{2,1,0:T(8,128)(2,1)S(1)} %get-tuple-element.19), channel_id=1, source_target_pairs={{2,4},{6,8},{10,12},{14,16},{18,20},{22,24},{26,28},{4,2},{8,6},{1... | collective-permute-start | bytes 983048 | tf_op jit(solution)/shard_map/ppermute | solution.py:533
  10.9 0.0 collective-permute-done.2.w2_ref
  10.9 0.0 collective-permute-done.3.other
  10.9 0.0 copy-done.3
  10.9 11.5 %inner.1 = (bf16[144,6,8,128]{3,2,1,0:T(8,128)(2,1)}, bf16[144,2,8,128]{3,2,1,0:T(8,128)(2,1)S(1)}) custom-call(bf16[144,3168]{1,0:T(8,128)(2,1)S(1)} %get-tuple-element.20.w_ref, bf16[144,3168]{1,0:T(8,128)(2,1)S(1)} %collective-permute-done.2.w2_ref, bf16[11,6,8,128]{3,2,1,0:T(8,128)(2,1)S(1)} %copy-done.3, ...), custom_call_target="tpu_custom_call" | custom-call | flops 3737124864 | bytes 5242880 | tf_op jit(solution)/shard_map/inner/pallas_call | solution.py:344
  22.4 0.0 collective-permute-done.refs_0_
  22.4 0.9 %collective-permute-done.1.refs_2_ = bf16[8,160,128]{2,1,0:T(8,128)(2,1)S(1)} collective-permute-done((bf16[8,160,128]{2,1,0:T(8,128)(2,1)S(1)}, bf16[8,160,128]{2,1,0:T(8,128)(2,1)S(1)}, u32[]{:S(2)}, u32[]{:S(2)}) %collective-permute-start.1) | collective-permute-done | bytes 327712 | tf_op jit(solution)/shard_map/ppermute | solution.py:533
  23.4 1.3 %collective-permute-start.5 = (bf16[8,160,128]{2,1,0:T(8,128)(2,1)S(1)}, bf16[8,160,128]{2,1,0:T(8,128)(2,1)S(1)}, u32[]{:S(2)}, u32[]{:S(2)}) collective-permute-start(bf16[8,160,128]{2,1,0:T(8,128)(2,1)S(1)} %collective-permute-done.refs_0_), channel_id=1, source_target_pairs={{0,1},{1,0},{2,3},{3,2},{4,5},{5,4},{6,7},{7,6},{8,9},{9,8},{10,11... | collective-permute-start | bytes 983048 | tf_op jit(solution)/shard_map/ppermute | solution.py:537
  24.7 0.0 collective-permute-start.6
  24.7 0.5 %collective-permute-start.4 = (bf16[144,2,8,128]{3,2,1,0:T(8,128)(2,1)S(1)}, bf16[144,2,8,128]{3,2,1,0:T(8,128)(2,1)S(1)}, u32[]{:S(2)}, u32[]{:S(2)}) collective-permute-start(bf16[144,2,8,128]{3,2,1,0:T(8,128)(2,1)S(1)} %get-tuple-element.25), channel_id=1, source_target_pairs={{0,1},{1,0},{2,3},{3,2},{4,5},{5,4},{6,7},{7,6},{8,9},{9,8},{10,11... | collective-permute-start | bytes 1769480 | tf_op jit(solution)/shard_map/ppermute | solution.py:537
  25.2 0.7 %collective-permute-done.5.refs_1_ = bf16[8,160,128]{2,1,0:T(8,128)(2,1)S(1)} collective-permute-done((bf16[8,160,128]{2,1,0:T(8,128)(2,1)S(1)}, bf16[8,160,128]{2,1,0:T(8,128)(2,1)S(1)}, u32[]{:S(2)}, u32[]{:S(2)}) %collective-permute-start.5) | collective-permute-done | bytes 327712 | tf_op jit(solution)/shard_map/ppermute | solution.py:537
  25.9 0.5 %collective-permute-done.6.refs_3_ = bf16[8,160,128]{2,1,0:T(8,128)(2,1)S(1)} collective-permute-done((bf16[8,160,128]{2,1,0:T(8,128)(2,1)S(1)}, bf16[8,160,128]{2,1,0:T(8,128)(2,1)S(1)}, u32[]{:S(2)}, u32[]{:S(2)}) %collective-permute-start.6) | collective-permute-done | bytes 327712 | tf_op jit(solution)/shard_map/ppermute | solution.py:537
  26.4 6.5 %outer.1 = (bf16[144,6,8,128]{3,2,1,0:T(8,128)(2,1)}, bf16[144,1,8,128]{3,2,1,0:T(8,128)(2,1)S(1)}) custom-call(bf16[144,3168]{1,0:T(8,128)(2,1)S(1)} %get-tuple-element.20.w_ref, bf16[144,3168]{1,0:T(8,128)(2,1)S(1)} %collective-permute-done.2.w2_ref, bf16[11,6,8,128]{3,2,1,0:T(8,128)(2,1)S(1)} %copy-done.3, ...), custom_call_target="tpu_custom_call", output_to_operand_aliasing={{0}: (9, {})} | custom-call | flops 1868562432 | bytes 5242880 | tf_op jit(solution)/shard_map/outer/pallas_call | solution.py:344
  32.9 0.4 %collective-permute-start.7 = (bf16[144,1,8,128]{3,2,1,0:T(8,128)(2,1)S(1)}, bf16[144,1,8,128]{3,2,1,0:T(8,128)(2,1)S(1)}, u32[]{:S(2)}, u32[]{:S(2)}) collective-permute-start(bf16[144,1,8,128]{3,2,1,0:T(8,128)(2,1)S(1)} %get-tuple-element.29), channel_id=1, source_target_pairs={{0,1},{1,0},{2,3},{3,2},{4,5},{5,4},{6,7},{7,6},{8,9},{9,8},{10,11... | collective-permute-start | bytes 884744 | tf_op jit(solution)/shard_map/ppermute | solution.py:537
  33.4 0.0 collective-permute-done.4.a_ref
  33.4 1.2 %collective-permute-done.7.b_ref = bf16[144,1,8,128]{3,2,1,0:T(8,128)(2,1)S(1)} collective-permute-done((bf16[144,1,8,128]{3,2,1,0:T(8,128)(2,1)S(1)}, bf16[144,1,8,128]{3,2,1,0:T(8,128)(2,1)S(1)}, u32[]{:S(2)}, u32[]{:S(2)}) %collective-permute-start.7) | collective-permute-done | bytes 294944 | tf_op jit(solution)/shard_map/ppermute | solution.py:537
  34.6 0.9 %join.1 = bf16[144,6,8,128]{3,2,1,0:T(8,128)(2,1)} custom-call(bf16[144,2,8,128]{3,2,1,0:T(8,128)(2,1)S(1)} %collective-permute-done.4.a_ref, bf16[144,1,8,128]{3,2,1,0:T(8,128)(2,1)S(1)} %collective-permute-done.7.b_ref, bf16[144,6,8,128]{3,2,1,0:T(8,128)(2,1)} %get-tuple-element.30._), custom_call_target="tpu_custom_call", output_to_operand_aliasing={{}: (2, {})} | custom-call | tf_op jit(solution)/shard_map/join/pallas_call | solution.py:382
Async XLA Ops:
  0.0 1.5 %copy-start = (bf16[144,6,8,128]{3,2,1,0:T(8,128)(2,1)S(1)}, bf16[144,6,8,128]{3,2,1,0:T(8,128)(2,1)}, u32[]{:S(2)}) copy-start(bf16[144,6,8,128]{3,2,1,0:T(8,128)(2,1)} %f_ref.1) | copy-start | bytes 5308420
  1.5 1.3 %copy-start.1 = (bf16[11,144,288]{2,1,0:T(8,128)(2,1)S(1)}, bf16[11,144,288]{2,1,0:T(8,128)(2,1)}, u32[]{:S(2)}) copy-start(bf16[11,144,288]{2,1,0:T(8,128)(2,1)} %c_ref.1) | copy-start | bytes 2737156
  2.8 0.9 %copy-start.2 = (bf16[11,6,8,128]{3,2,1,0:T(8,128)(2,1)S(1)}, bf16[11,6,8,128]{3,2,1,0:T(8,128)(2,1)}, u32[]{:S(2)}) copy-start(bf16[11,6,8,128]{3,2,1,0:T(8,128)(2,1)} %a_ref.5) | copy-start | bytes 405508
  3.7 7.3 %copy-start.3 = (bf16[11,6,8,128]{3,2,1,0:T(8,128)(2,1)S(1)}, bf16[11,6,8,128]{3,2,1,0:T(8,128)(2,1)}, u32[]{:S(2)}) copy-start(bf16[11,6,8,128]{3,2,1,0:T(8,128)(2,1)} %a_ref.5) | copy-start | bytes 405508
  5.7 5.2 %collective-permute-start.3 = (bf16[4,8,144,128]{3,2,1,0:T(8,128)(2,1)S(1)}, bf16[4,8,144,128]{3,2,1,0:T(8,128)(2,1)S(1)}, u32[]{:S(2)}, u32[]{:S(2)}) collective-permute-start(bf16[4,8,144,128]{3,2,1,0:T(8,128)(2,1)S(1)} %get-tuple-element.22), channel_id=1, source_target_pairs={{0,1},{1,0},{2,3},{3,2},{4,5},{5,4},{6,7},{7,6},{8,9},{9,8},{10,11... | collective-permute-start | bytes 3538952 | tf_op jit(solution)/shard_map/ppermute | solution.py:537
  6.5 4.4 %collective-permute-start.2 = (bf16[144,3168]{1,0:T(8,128)(2,1)S(1)}, bf16[144,3168]{1,0:T(8,128)(2,1)S(1)}, u32[]{:S(2)}, u32[]{:S(2)}) collective-permute-start(bf16[144,3168]{1,0:T(8,128)(2,1)S(1)} %get-tuple-element.20.w_ref), channel_id=1, source_target_pairs={{0,1},{1,0},{2,3},{3,2},{4,5},{5,4},{6,7},{7,6},{8,9},{9,8},{10,11... | collective-permute-start | bytes 2737160 | tf_op jit(solution)/shard_map/ppermute | solution.py:537
  6.6 15.9 %collective-permute-start = (bf16[8,160,128]{2,1,0:T(8,128)(2,1)S(1)}, bf16[8,160,128]{2,1,0:T(8,128)(2,1)S(1)}, u32[]{:S(2)}, u32[]{:S(2)}) collective-permute-start(bf16[8,160,128]{2,1,0:T(8,128)(2,1)S(1)} %get-tuple-element.18), channel_id=1, source_target_pairs={{0,2},{4,6},{8,10},{12,14},{16,18},{20,22},{24,26},{28,30},{2,0},{... | collective-permute-start | bytes 983048 | tf_op jit(solution)/shard_map/ppermute | solution.py:533
  6.8 16.6 %collective-permute-start.1 = (bf16[8,160,128]{2,1,0:T(8,128)(2,1)S(1)}, bf16[8,160,128]{2,1,0:T(8,128)(2,1)S(1)}, u32[]{:S(2)}, u32[]{:S(2)}) collective-permute-start(bf16[8,160,128]{2,1,0:T(8,128)(2,1)S(1)} %get-tuple-element.19), channel_id=1, source_target_pairs={{2,4},{6,8},{10,12},{14,16},{18,20},{22,24},{26,28},{4,2},{8,6},{1... | collective-permute-start | bytes 983048 | tf_op jit(solution)/shard_map/ppermute | solution.py:533
  23.4 2.5 %collective-permute-start.5 = (bf16[8,160,128]{2,1,0:T(8,128)(2,1)S(1)}, bf16[8,160,128]{2,1,0:T(8,128)(2,1)S(1)}, u32[]{:S(2)}, u32[]{:S(2)}) collective-permute-start(bf16[8,160,128]{2,1,0:T(8,128)(2,1)S(1)} %collective-permute-done.refs_0_), channel_id=1, source_target_pairs={{0,1},{1,0},{2,3},{3,2},{4,5},{5,4},{6,7},{7,6},{8,9},{9,8},{10,11... | collective-permute-start | bytes 983048 | tf_op jit(solution)/shard_map/ppermute | solution.py:537
  24.7 1.7 %collective-permute-start.6 = (bf16[8,160,128]{2,1,0:T(8,128)(2,1)S(1)}, bf16[8,160,128]{2,1,0:T(8,128)(2,1)S(1)}, u32[]{:S(2)}, u32[]{:S(2)}) collective-permute-start(bf16[8,160,128]{2,1,0:T(8,128)(2,1)S(1)} %collective-permute-done.1.refs_2_), channel_id=1, source_target_pairs={{0,1},{1,0},{2,3},{3,2},{4,5},{5,4},{6,7},{7,6},{8,9},{9,8},{10,11... | collective-permute-start | bytes 983048 | tf_op jit(solution)/shard_map/ppermute | solution.py:537
  24.7 8.7 %collective-permute-start.4 = (bf16[144,2,8,128]{3,2,1,0:T(8,128)(2,1)S(1)}, bf16[144,2,8,128]{3,2,1,0:T(8,128)(2,1)S(1)}, u32[]{:S(2)}, u32[]{:S(2)}) collective-permute-start(bf16[144,2,8,128]{3,2,1,0:T(8,128)(2,1)S(1)} %get-tuple-element.25), channel_id=1, source_target_pairs={{0,1},{1,0},{2,3},{3,2},{4,5},{5,4},{6,7},{7,6},{8,9},{9,8},{10,11... | collective-permute-start | bytes 1769480 | tf_op jit(solution)/shard_map/ppermute | solution.py:537
  32.9 1.7 %collective-permute-start.7 = (bf16[144,1,8,128]{3,2,1,0:T(8,128)(2,1)S(1)}, bf16[144,1,8,128]{3,2,1,0:T(8,128)(2,1)S(1)}, u32[]{:S(2)}, u32[]{:S(2)}) collective-permute-start(bf16[144,1,8,128]{3,2,1,0:T(8,128)(2,1)S(1)} %get-tuple-element.29), channel_id=1, source_target_pairs={{0,1},{1,0},{2,3},{3,2},{4,5},{5,4},{6,7},{7,6},{8,9},{9,8},{10,11... | collective-permute-start | bytes 884744 | tf_op jit(solution)/shard_map/ppermute | solution.py:537

commit v5 on v4

--- a/solution.py
+++ b/solution.py
@@ -49,35 +49,44 @@
     return ref.at[k % ny, pl.ds(modes + ny * (k // ny), ny), :]
 
 
-def turn_kernel(modes, f_ref, a_ref, c_ref, o_ref, e_ref, d_ref, w_ref, *more):
-    send, perm = more[:-1], more[-1]
-    step = pl.program_id(0)
-    chunk, nx, ny, nz = f_ref.shape
+def turn_kernel(chunk, f_hbm, a_hbm, c_hbm, o_ref, e_ref, d_ref, w_ref, *more):
+    *send, f_ref, a_ref, c_ref, perm, fsem, sem = more
+    modes, nx, ny, nz = f_ref.shape
     terms = a_ref.shape[0]
     block = block_of(chunk)
+
+    def load(q):
+        part = pl.ds(q, chunk)
+        return pltpu.make_async_copy(f_hbm.at[part], f_ref.at[part], fsem.at[q // chunk])
+
+    others = (
+        pltpu.make_async_copy(a_hbm, a_ref, sem.at[0]),
+        pltpu.make_async_copy(c_hbm, c_ref, sem.at[1]),
+    )
+    for q in range(0, modes, chunk):
+        load(q).start()
+    for copy in others:
+        copy.start()
+    perm[...] = one_hot(block, ny)
+    layers = 2 if nx % 2 == 0 else 1
+    for start in range(0, modes, chunk):
+        load(start).wait()
+        for x in range(0, nx, layers):
+            for q in range(start, start + chunk, block):
+                wide = jnp.concatenate(
+                    [f_ref[pl.ds(q, block), x + j].reshape(block * ny, nz) for j in range(layers)], axis=1
+                )
+                wide = permuted(perm[...], wide)
+                for j in range(layers):
+                    o_ref[x + j, :, pl.ds(q, block), :] = wide[:, j * nz:(j + 1) * nz].reshape(ny, block, nz)
+    for copy in others:
+        copy.wait()
     odd = lax.rem(lax.axis_index(GRID), 2)
-    outer = ((e_ref, (1 - odd) * (nx - 1)), (d_ref, odd * (nx - 1)))
-
-    @pl.when(step == 0)
-    def _():
-        perm[...] = one_hot(block, ny)
-        for out, x in outer:
-            for k in range(terms):
-                coef_rows(out, k, modes, ny)[...] = a_ref[k, x]
-        arrange(c_ref, w_ref)
-
-    layers = 2 if nx % 2 == 0 else 1
-    for x in range(0, nx, layers):
-        for q in range(0, chunk, block):
-            wide = jnp.concatenate(
-                [f_ref[pl.ds(q, block), x + j].reshape(block * ny, nz) for j in range(layers)], axis=1
-            )
-            wide = permuted(perm[...], wide)
-            for j in range(layers):
-                o_ref[x + j, :, pl.ds(q, block), :] = wide[:, j * nz:(j + 1) * nz].reshape(ny, block, nz)
-    rows = pl.ds(pl.multiple_of(step * chunk, 8), chunk)
-    for out, x in outer:
-        out[:, rows, :] = o_ref[x]
+    for out, x in ((e_ref, (1 - odd) * (nx - 1)), (d_ref, odd * (nx - 1))):
+        out[:, :modes, :] = o_ref[x]
+        for k in range(terms):
+            coef_rows(out, k, modes, ny)[...] = a_ref[k, x]
+    arrange(c_ref, w_ref)
     for out in send:
         count = out.shape[0]
         out[...] = o_ref[pl.ds((1 - lax.axis_index(MODE)) * (nx - count), count)]
@@ -86,32 +95,26 @@
 def turn(field, coefs, coupling, sent=0):
     modes, nx, ny, nz = field.shape
     terms, outs, total = coupling.shape
-    chunk = divisor(modes, (72, 48, 64, 32, 16, 8))
-    outer = (ny, modes + extra_of(coefs.shape[0], ny), nz)
+    chunk = divisor(modes, (48, 72, 64, 32, 16, 8))
+    outer = (ny, modes + extra_of(terms, ny), nz)
     block = block_of(chunk)
-    whole = pl.BlockSpec(outer, lambda i: (0, 0, 0))
+    shapes = [(nx, ny, modes, nz), outer, outer, (outs, terms * total)] + [(sent, ny, modes, nz)] * (sent > 0)
+    shapes = [jax.ShapeDtypeStruct(shape, BF16) for shape in shapes]
+    inputs = [pltpu.with_memory_space_constraint(v, pltpu.HBM) for v in (field, coefs, coupling)]
     return pl.pallas_call(
-        functools.partial(turn_kernel, modes),
-        grid=(modes // chunk,),
-        in_specs=[
-            pl.BlockSpec((chunk, nx, ny, nz), lambda i: (i, 0, 0, 0)),
-            pl.BlockSpec(coefs.shape, lambda i: (0, 0, 0, 0)),
-            pl.BlockSpec(coupling.shape, lambda i: (0, 0, 0)),
+        functools.partial(turn_kernel, chunk),
+        in_specs=[pl.BlockSpec(memory_space=pltpu.HBM)] * 3,
+        out_specs=[VMEM] * len(shapes),
+        scratch_shapes=[pltpu.VMEM(v.shape, BF16) for v in inputs]
+        + [
+            pltpu.VMEM((block * ny, block * ny), BF16),
+            pltpu.SemaphoreType.DMA((modes // chunk,)),
+            pltpu.SemaphoreType.DMA((2,)),
         ],
-        out_specs=[pl.BlockSpec((nx, ny, chunk, nz), lambda i: (0, 0, i, 0)), whole, whole]
-        + [pl.BlockSpec((outs, terms * total), lambda i: (0, 0))]
-        + [pl.BlockSpec((sent, ny, chunk, nz), lambda i: (0, 0, i, 0))] * (sent > 0),
-        scratch_shapes=[pltpu.VMEM((block * ny, block * ny), BF16)],
-        out_shape=[
-            jax.ShapeDtypeStruct((nx, ny, modes, nz), BF16),
-            jax.ShapeDtypeStruct(outer, BF16),
-            jax.ShapeDtypeStruct(outer, BF16),
-            jax.ShapeDtypeStruct((outs, terms * total), BF16),
-        ]
-        + [jax.ShapeDtypeStruct((sent, ny, modes, nz), BF16)] * (sent > 0),
-        compiler_params=grant(field, field, field, field, coefs, coupling, coupling, coupling, coupling),
+        out_shape=shapes,
+        compiler_params=grant(*inputs, *shapes),
         name="turn",
-    )(field, coefs, coupling)
+    )(*inputs)
 
 
 def chunk_of(total):
@@ -130,12 +133,13 @@
 
 
 class Engine:
-    def __init__(self, w_refs, terms, f_ref, stage, coef, face, repx, repy, repz, acc, obuf, perm):
+    def __init__(self, w_refs, terms, f_ref, coef, face, repx, repy, repz, acc, obuf, perm):
         self.w_refs, self.terms = w_refs, terms
-        self.f_ref, self.stage, self.coef, self.face = f_ref, stage, coef, face
+        self.f_ref, self.coef, self.face = f_ref, coef, face
         self.repx, self.repy, self.repz = repx, repy, repz
         self.acc, self.obuf, self.perm = acc, obuf, perm
-        _, self.ny, self.total, self.nz = stage.shape
+        _, rows, self.total, self.nz = f_ref.shape
+        self.ny = rows - 2
         self.outs = acc.shape[1]
         self.block = block_of(self.outs // len(w_refs))
 
@@ -169,10 +173,11 @@
                 self.repz[i, 1, y, k] = self.spread((4, k), y)
             self.repy[i, ny, k] = self.spread((5, k), ny - 1)
 
-    def widen(self, slot):
+    def widen(self, slot, parts):
         @pl.loop(0, self.ny)
         def _(y):
-            self.f_ref[slot, y + 1] = self.stage[slot, y].astype(F32)
+            for rows, ref in parts:
+                self.f_ref[slot, y + 1, rows, :] = ref[y].astype(F32)
 
     def differences(self, c, y, q):
         lanes = lax.broadcasted_iota(jnp.int32, (16, self.nz), 1)
@@ -215,7 +220,7 @@
 
     def layer(self, i, c):
         pairs = self.ny // 2
-        unroll = 2 if pairs % 2 == 0 else 1
+        unroll = divisor(pairs, (4, 2, 1))
 
         @pl.loop(0, pairs // unroll)
         def _(n):
@@ -232,7 +237,6 @@
 def engine_scratch(slots, items, terms, ny, nz, total, outs, block):
     return [
         pltpu.VMEM((slots, ny + 2, total, nz), F32),
-        pltpu.VMEM((slots, ny, total, nz), BF16),
         pltpu.VMEM((slots, terms, ny, nz), F32),
         pltpu.VMEM((6, terms, ny, nz), F32),
         pltpu.VMEM((items, 2, ny, terms, 16, nz), BF16),
@@ -253,18 +257,15 @@
     if outer:
         halos, refs = refs[:4], refs[5:]
     out_hbm, give_hbm, *refs = refs
-    engine = Engine((w_ref, w2_ref), terms, *refs[:10])
-    fsem, osem, *more = refs[10:]
-    stage, coef = engine.stage, engine.coef
+    engine = Engine((w_ref, w2_ref), terms, *refs[:9])
+    osem = refs[9]
+    coef = engine.coef
     slots, items = coef.shape[0], engine.repx.shape[0]
     first = me * (half - 1)
-
-    def load(s, slot, ref):
-        rows = pl.ds(pl.multiple_of(lax.rem(me + s, 2) * modes, 8), modes)
-        return pltpu.make_async_copy(ref, stage.at[slot, :, rows, :], fsem.at[s, slot])
-
+    aligned = 16 if modes % 16 == 0 else 8
+    places = [pl.ds(pl.multiple_of(lax.rem(me + s, 2) * modes, aligned), modes) for s in range(2)]
+    engine.prepare()
     if outer:
-        ends, csem = more
         even, odd = halos[:2], halos[2:]
         takes_odd = (me == 0) == (lax.rem(lax.axis_index(GRID), 2) == 0)
         layer_of = [(1 - me + j, me * (nx - 2) + j) for j in range(2)]
@@ -272,31 +273,19 @@
         for test, halo in ((takes_odd, odd), (jnp.logical_not(takes_odd), even)):
             @pl.when(test)
             def _():
-                for s in range(2):
-                    load(s, end, halo[s].at[:, pl.ds(0, modes), :]).start()
-                pltpu.make_async_copy(halo[0].at[:, pl.ds(modes, ends.shape[1]), :], ends, csem).start()
+                engine.widen(end, [(rows, ref.at[:, :modes, :]) for rows, ref in zip(places, halo)])
+                for k in range(terms):
+                    coef[end, k] = 0.5 * coef_rows(halo[0], k, modes, ny)[...].astype(F32)
     else:
         layer_of = [(slot, first + slot) for slot in range(slots)]
     for slot, x in layer_of:
-        load(0, slot, own.at[x]).start()
-        load(1, slot, other.at[x - first]).start()
-    engine.prepare()
-    for slot, x in layer_of:
+        engine.widen(slot, ((places[0], own.at[x]), (places[1], other.at[x - first])))
         for k in range(terms):
             coef[slot, k] = 0.5 * a_ref[k, x].astype(F32)
-    if outer:
-        pltpu.make_async_copy(even[0].at[:, pl.ds(modes, ends.shape[1]), :], ends, csem).wait()
-        for k in range(terms):
-            coef[end, k] = 0.5 * coef_rows(ends, k, 0, ny)[...].astype(F32)
 
     @pl.loop(0, items)
     def _(i):
         engine.faces(i, i + 1)
-
-    def arrive(slot):
-        for s in range(2):
-            load(s, slot, own.at[0]).wait()
-        engine.widen(slot)
 
     def writes(i, slot):
         x = me * (nx - 1) if outer else first + i + 1
@@ -305,13 +294,9 @@
             pltpu.make_async_copy(engine.obuf.at[slot, pl.ds(outs, outs)], give_hbm.at[:, i], osem.at[1, slot]),
         )
 
-    arrive(0)
-    arrive(1)
-
     @pl.loop(0, items)
     def _(i):
         slot = i & 1
-        arrive(i + 2)
         engine.layer(i, i + 1)
 
         @pl.when(i > 1)
@@ -338,12 +323,9 @@
     block = block_of(outs)
     operands = [*weights, coefs, own, other, *halos, *out]
     scratch = engine_scratch(slots, items, terms, ny, nz, total, 2 * outs, block)
-    more = []
-    if outer:
-        more = [pltpu.VMEM((ny, extra_of(terms, ny), nz), BF16), pltpu.SemaphoreType.DMA]
     return pl.pallas_call(
         functools.partial(half_kernel, outer),
-        in_specs=[VMEM, VMEM, VMEM] + [HBM] * (len(operands) - 3),
+        in_specs=[VMEM] * (5 + len(halos)) + [HBM] * len(out),
         out_specs=[HBM, HBM],
         out_shape=[
             jax.ShapeDtypeStruct((outs, nx, ny, nz), BF16),
@@ -352,11 +334,9 @@
         input_output_aliases={len(operands) - 1: 0} if outer else {},
         scratch_shapes=[
             *scratch,
-            pltpu.SemaphoreType.DMA((2, slots)),
             pltpu.SemaphoreType.DMA((2, 2)),
-            *more,
         ],
-        compiler_params=grant(*scratch, *weights, coefs),
+        compiler_params=grant(*scratch),
         cost_estimate=pl.CostEstimate(
             flops=4 * outs * depth * items * ny * nz, bytes_accessed=5 * 2**20, transcendentals=0
         ),
@@ -399,9 +379,9 @@
     if outer:
         even, odd, refs = refs[:sources], refs[sources:2 * sources], refs[2 * sources + 1:]
     out_hbm, *refs = refs
-    engine = Engine((w_ref,), terms, *refs[:10])
-    fsem, osem, *more = refs[10:]
-    stage, coef, obuf = engine.stage, engine.coef, engine.obuf
+    engine = Engine((w_ref,), terms, *refs[:9])
+    stage, fsem, osem, *more = refs[9:]
+    coef, obuf = engine.coef, engine.obuf
     slots, items = coef.shape[0], engine.repx.shape[0]
     stride = 3 if outer else 1
     me = lax.axis_index(MODE)
@@ -452,7 +432,7 @@
     def arrive(slot):
         for s in range(sources):
             load(s, slot, f_hbm[s].at[0]).wait()
-        engine.widen(slot)
+        engine.widen(slot, ((slice(None), stage.at[slot]),))
 
     def write(i, slot):
         x = i * (nx - 1) if outer else i + 1
@@ -496,6 +476,7 @@
     shape = jax.ShapeDtypeStruct((outs, nx, ny, nz), BF16)
     operands = [weights, coefs, *fields] + ([*halos[0], *halos[1], out] if outer else [])
     scratch = engine_scratch(slots, items, terms, ny, nz, total, outs, block)
+    scratch.append(pltpu.VMEM((slots, ny, total, nz), BF16))
     more = []
     if outer:
         more = [pltpu.VMEM((2, ny, extra_of(terms, ny), nz), BF16), pltpu.SemaphoreType.DMA((2,))]

time: 35.7 us -> 31.6 us (0.89)
  local copies, waits for them, and re-layouts: 3.67 us -> 0.01 us
  Pallas kernels: 21 us -> 20.1 us
  waiting for transfers between devices: 3.37 us -> 3.9 us
    unnamed x8 -> x2, local copies, waits for them, and re-layouts: 3.67 us -> 0.01 us
    pallas_call x3, Pallas kernels: 20.1 us -> 19.2 us  [the longest x2 16.2 us: half_layers(): pl.pallas_call(functools.partial(half_kernel, outer), in_specs=[VMEM] * (...]
    ppermute x2, waiting for transfers between devices: 0.95 us -> 1.47 us  [exchange(): return lax.ppermute(block, GRID, pairs + [(b, a) for a, b in pairs])]
  transfers between devices with their start and end apart: 8 -> 8, of which waited for: 4 -> 4; matrix products, arithmetic and copies ran while one was open for 0% -> 0% of each run, Pallas kernels for 51% -> 52%
where the time goes in v5:
time: 31.6 us; the launch traced here: 31.4 us
  Pallas kernels  20.1 us (64%)
  starting transfers between devices  7.37 us (23%)
  waiting for transfers between devices  3.9 us (12%)
    pallas_call x2, Pallas kernels, half_layers(): pl.pallas_call(functools.partial(half_kernel, outer), in_specs=[VMEM] * (...  16.2 us
    ppermute x2, starting transfers between devices, exchange(): return lax.ppermute(block, GRID, pairs + [(b, a) for a, b in pairs])  4.32 us
    ppermute x6, starting transfers between devices, swap(): return lax.ppermute(block, MODE, [(0, 1), (1, 0)])  3.05 us
    pallas_call x1, Pallas kernels, turn(): pl.pallas_call(functools.partial(turn_kernel, chunk), in_specs=[pl.BlockS...  2.97 us
    ppermute x6, waiting for transfers between devices, swap(): return lax.ppermute(block, MODE, [(0, 1), (1, 0)])  2.43 us
    ppermute x2, waiting for transfers between devices, exchange(): return lax.ppermute(block, GRID, pairs + [(b, a) for a, b in pairs])  1.47 us
    pallas_call x1, Pallas kernels, join(): pl.pallas_call(join_kernel, in_specs=[VMEM, VMEM, HBM], out_specs=HBM, ou...  0.92 us
  transfers between devices with their start and end apart: 8, of which 4 were waited for; matrix products, arithmetic and copies ran while one was open for 0% of the time, Pallas kernels for 52%

profile of v5, /device:TPU:27, one launch (start us, length us, event | category | flops | bytes accessed | tf_op | source)
XLA Modules:
  0.0 31.4 jit_solution(758171204753452315)
XLA Ops:
  0.0 0.0 copy-start
  0.0 3.0 %turn.1 = (bf16[6,8,144,128]{3,2,1,0:T(8,128)(2,1)S(1)}, bf16[8,160,128]{2,1,0:T(8,128)(2,1)S(1)}, bf16[8,160,128]{2,1,0:T(8,128)(2,1)S(1)}, bf16[144,3168]{1,0:T(8,128)(2,1)S(1)}, bf16[4,8,144,128]{3,2,1,0:T(8,128)(2,1)S(1)}) custom-call(bf16[144,6,8,128]{3,2,1,0:T(8,128)(2,1)} %f_hbm.1, bf16[11,6,8,128]{3,2,1,0:T(8,128)(2,1)} %a_ref.3, ...), custom_call_target="tpu_custom_call" | custom-call | tf_op jit(solution)/shard_map/turn/pallas_call | solution.py:104
  3.0 0.7 %collective-permute-start.3 = (bf16[4,8,144,128]{3,2,1,0:T(8,128)(2,1)S(1)}, bf16[4,8,144,128]{3,2,1,0:T(8,128)(2,1)S(1)}, u32[]{:S(2)}, u32[]{:S(2)}) collective-permute-start(bf16[4,8,144,128]{3,2,1,0:T(8,128)(2,1)S(1)} %get-tuple-element.22), channel_id=1, source_target_pairs={{0,1},{1,0},{2,3},{3,2},{4,5},{5,4},{6,7},{7,6},{8,9},{9,8},{10,11... | collective-permute-start | bytes 3538952 | tf_op jit(solution)/shard_map/ppermute | solution.py:518
  3.7 0.1 collective-permute-start.2
  3.8 0.3 collective-permute-start
  4.1 4.1 %collective-permute-start.1 = (bf16[8,160,128]{2,1,0:T(8,128)(2,1)S(1)}, bf16[8,160,128]{2,1,0:T(8,128)(2,1)S(1)}, u32[]{:S(2)}, u32[]{:S(2)}) collective-permute-start(bf16[8,160,128]{2,1,0:T(8,128)(2,1)S(1)} %get-tuple-element.19), channel_id=1, source_target_pairs={{2,4},{6,8},{10,12},{14,16},{18,20},{22,24},{26,28},{4,2},{8,6},{1... | collective-permute-start | bytes 983048 | tf_op jit(solution)/shard_map/ppermute | solution.py:514
  8.1 0.0 collective-permute-done.2.w2_ref
  8.1 0.0 collective-permute-done.3.other
  8.2 0.0 copy-done
  8.2 11.0 %inner.1 = (bf16[144,6,8,128]{3,2,1,0:T(8,128)(2,1)}, bf16[144,2,8,128]{3,2,1,0:T(8,128)(2,1)S(1)}) custom-call(bf16[144,3168]{1,0:T(8,128)(2,1)S(1)} %get-tuple-element.20.w_ref, bf16[144,3168]{1,0:T(8,128)(2,1)S(1)} %collective-permute-done.2.w2_ref, bf16[11,6,8,128]{3,2,1,0:T(8,128)(2,1)S(1)} %copy-done, ...), custom_call_target="tpu_custom_call" | custom-call | flops 3737124864 | bytes 5242880 | tf_op jit(solution)/shard_map/inner/pallas_call | solution.py:326
  19.1 0.0 collective-permute-done.refs_0_
  19.1 1.5 %collective-permute-done.1.refs_2_ = bf16[8,160,128]{2,1,0:T(8,128)(2,1)S(1)} collective-permute-done((bf16[8,160,128]{2,1,0:T(8,128)(2,1)S(1)}, bf16[8,160,128]{2,1,0:T(8,128)(2,1)S(1)}, u32[]{:S(2)}, u32[]{:S(2)}) %collective-permute-start.1) | collective-permute-done | bytes 327712 | tf_op jit(solution)/shard_map/ppermute | solution.py:514
  20.6 1.3 %collective-permute-start.5 = (bf16[8,160,128]{2,1,0:T(8,128)(2,1)S(1)}, bf16[8,160,128]{2,1,0:T(8,128)(2,1)S(1)}, u32[]{:S(2)}, u32[]{:S(2)}) collective-permute-start(bf16[8,160,128]{2,1,0:T(8,128)(2,1)S(1)} %collective-permute-done.refs_0_), channel_id=1, source_target_pairs={{0,1},{1,0},{2,3},{3,2},{4,5},{5,4},{6,7},{7,6},{8,9},{9,8},{10,11... | collective-permute-start | bytes 983048 | tf_op jit(solution)/shard_map/ppermute | solution.py:518
  21.9 0.0 collective-permute-start.6
  21.9 0.5 %collective-permute-start.4 = (bf16[144,2,8,128]{3,2,1,0:T(8,128)(2,1)S(1)}, bf16[144,2,8,128]{3,2,1,0:T(8,128)(2,1)S(1)}, u32[]{:S(2)}, u32[]{:S(2)}) collective-permute-start(bf16[144,2,8,128]{3,2,1,0:T(8,128)(2,1)S(1)} %get-tuple-element.25), channel_id=1, source_target_pairs={{0,1},{1,0},{2,3},{3,2},{4,5},{5,4},{6,7},{7,6},{8,9},{9,8},{10,11... | collective-permute-start | bytes 1769480 | tf_op jit(solution)/shard_map/ppermute | solution.py:518
  22.4 0.7 %collective-permute-done.5.refs_1_ = bf16[8,160,128]{2,1,0:T(8,128)(2,1)S(1)} collective-permute-done((bf16[8,160,128]{2,1,0:T(8,128)(2,1)S(1)}, bf16[8,160,128]{2,1,0:T(8,128)(2,1)S(1)}, u32[]{:S(2)}, u32[]{:S(2)}) %collective-permute-start.5) | collective-permute-done | bytes 327712 | tf_op jit(solution)/shard_map/ppermute | solution.py:518
  23.2 0.5 %collective-permute-done.6.refs_3_ = bf16[8,160,128]{2,1,0:T(8,128)(2,1)S(1)} collective-permute-done((bf16[8,160,128]{2,1,0:T(8,128)(2,1)S(1)}, bf16[8,160,128]{2,1,0:T(8,128)(2,1)S(1)}, u32[]{:S(2)}, u32[]{:S(2)}) %collective-permute-start.6) | collective-permute-done | bytes 327712 | tf_op jit(solution)/shard_map/ppermute | solution.py:518
  23.6 5.2 %outer.1 = (bf16[144,6,8,128]{3,2,1,0:T(8,128)(2,1)}, bf16[144,1,8,128]{3,2,1,0:T(8,128)(2,1)S(1)}) custom-call(bf16[144,3168]{1,0:T(8,128)(2,1)S(1)} %get-tuple-element.20.w_ref, bf16[144,3168]{1,0:T(8,128)(2,1)S(1)} %collective-permute-done.2.w2_ref, bf16[11,6,8,128]{3,2,1,0:T(8,128)(2,1)S(1)} %copy-done, ...), custom_call_target="tpu_custom_call", output_to_operand_aliasing={{0}: (9, {})} | custom-call | flops 1868562432 | bytes 5242880 | tf_op jit(solution)/shard_map/outer/pallas_call | solution.py:326
  28.9 0.4 %collective-permute-start.7 = (bf16[144,1,8,128]{3,2,1,0:T(8,128)(2,1)S(1)}, bf16[144,1,8,128]{3,2,1,0:T(8,128)(2,1)S(1)}, u32[]{:S(2)}, u32[]{:S(2)}) collective-permute-start(bf16[144,1,8,128]{3,2,1,0:T(8,128)(2,1)S(1)} %get-tuple-element.29), channel_id=1, source_target_pairs={{0,1},{1,0},{2,3},{3,2},{4,5},{5,4},{6,7},{7,6},{8,9},{9,8},{10,11... | collective-permute-start | bytes 884744 | tf_op jit(solution)/shard_map/ppermute | solution.py:518
  29.3 0.0 collective-permute-done.4.a_ref
  29.3 1.2 %collective-permute-done.7.b_ref = bf16[144,1,8,128]{3,2,1,0:T(8,128)(2,1)S(1)} collective-permute-done((bf16[144,1,8,128]{3,2,1,0:T(8,128)(2,1)S(1)}, bf16[144,1,8,128]{3,2,1,0:T(8,128)(2,1)S(1)}, u32[]{:S(2)}, u32[]{:S(2)}) %collective-permute-start.7) | collective-permute-done | bytes 294944 | tf_op jit(solution)/shard_map/ppermute | solution.py:518
  30.5 0.9 %join.1 = bf16[144,6,8,128]{3,2,1,0:T(8,128)(2,1)} custom-call(bf16[144,2,8,128]{3,2,1,0:T(8,128)(2,1)S(1)} %collective-permute-done.4.a_ref, bf16[144,1,8,128]{3,2,1,0:T(8,128)(2,1)S(1)} %collective-permute-done.7.b_ref, bf16[144,6,8,128]{3,2,1,0:T(8,128)(2,1)} %get-tuple-element.30._), custom_call_target="tpu_custom_call", output_to_operand_aliasing={{}: (2, {})} | custom-call | tf_op jit(solution)/shard_map/join/pallas_call | solution.py:362
Async XLA Ops:
  0.0 8.2 %copy-start = (bf16[11,6,8,128]{3,2,1,0:T(8,128)(2,1)S(1)}, bf16[11,6,8,128]{3,2,1,0:T(8,128)(2,1)}, u32[]{:S(2)}) copy-start(bf16[11,6,8,128]{3,2,1,0:T(8,128)(2,1)} %a_ref.3) | copy-start | bytes 405508
  3.0 5.2 %collective-permute-start.3 = (bf16[4,8,144,128]{3,2,1,0:T(8,128)(2,1)S(1)}, bf16[4,8,144,128]{3,2,1,0:T(8,128)(2,1)S(1)}, u32[]{:S(2)}, u32[]{:S(2)}) collective-permute-start(bf16[4,8,144,128]{3,2,1,0:T(8,128)(2,1)S(1)} %get-tuple-element.22), channel_id=1, source_target_pairs={{0,1},{1,0},{2,3},{3,2},{4,5},{5,4},{6,7},{7,6},{8,9},{9,8},{10,11... | collective-permute-start | bytes 3538952 | tf_op jit(solution)/shard_map/ppermute | solution.py:518
  3.7 4.4 %collective-permute-start.2 = (bf16[144,3168]{1,0:T(8,128)(2,1)S(1)}, bf16[144,3168]{1,0:T(8,128)(2,1)S(1)}, u32[]{:S(2)}, u32[]{:S(2)}) collective-permute-start(bf16[144,3168]{1,0:T(8,128)(2,1)S(1)} %get-tuple-element.20.w_ref), channel_id=1, source_target_pairs={{0,1},{1,0},{2,3},{3,2},{4,5},{5,4},{6,7},{7,6},{8,9},{9,8},{10,11... | collective-permute-start | bytes 2737160 | tf_op jit(solution)/shard_map/ppermute | solution.py:518
  3.8 15.3 %collective-permute-start = (bf16[8,160,128]{2,1,0:T(8,128)(2,1)S(1)}, bf16[8,160,128]{2,1,0:T(8,128)(2,1)S(1)}, u32[]{:S(2)}, u32[]{:S(2)}) collective-permute-start(bf16[8,160,128]{2,1,0:T(8,128)(2,1)S(1)} %get-tuple-element.18), channel_id=1, source_target_pairs={{0,2},{4,6},{8,10},{12,14},{16,18},{20,22},{24,26},{28,30},{2,0},{... | collective-permute-start | bytes 983048 | tf_op jit(solution)/shard_map/ppermute | solution.py:514
  4.1 16.6 %collective-permute-start.1 = (bf16[8,160,128]{2,1,0:T(8,128)(2,1)S(1)}, bf16[8,160,128]{2,1,0:T(8,128)(2,1)S(1)}, u32[]{:S(2)}, u32[]{:S(2)}) collective-permute-start(bf16[8,160,128]{2,1,0:T(8,128)(2,1)S(1)} %get-tuple-element.19), channel_id=1, source_target_pairs={{2,4},{6,8},{10,12},{14,16},{18,20},{22,24},{26,28},{4,2},{8,6},{1... | collective-permute-start | bytes 983048 | tf_op jit(solution)/shard_map/ppermute | solution.py:514
  20.6 2.5 %collective-permute-start.5 = (bf16[8,160,128]{2,1,0:T(8,128)(2,1)S(1)}, bf16[8,160,128]{2,1,0:T(8,128)(2,1)S(1)}, u32[]{:S(2)}, u32[]{:S(2)}) collective-permute-start(bf16[8,160,128]{2,1,0:T(8,128)(2,1)S(1)} %collective-permute-done.refs_0_), channel_id=1, source_target_pairs={{0,1},{1,0},{2,3},{3,2},{4,5},{5,4},{6,7},{7,6},{8,9},{9,8},{10,11... | collective-permute-start | bytes 983048 | tf_op jit(solution)/shard_map/ppermute | solution.py:518
  21.9 1.7 %collective-permute-start.6 = (bf16[8,160,128]{2,1,0:T(8,128)(2,1)S(1)}, bf16[8,160,128]{2,1,0:T(8,128)(2,1)S(1)}, u32[]{:S(2)}, u32[]{:S(2)}) collective-permute-start(bf16[8,160,128]{2,1,0:T(8,128)(2,1)S(1)} %collective-permute-done.1.refs_2_), channel_id=1, source_target_pairs={{0,1},{1,0},{2,3},{3,2},{4,5},{5,4},{6,7},{7,6},{8,9},{9,8},{10,11... | collective-permute-start | bytes 983048 | tf_op jit(solution)/shard_map/ppermute | solution.py:518
  21.9 7.4 %collective-permute-start.4 = (bf16[144,2,8,128]{3,2,1,0:T(8,128)(2,1)S(1)}, bf16[144,2,8,128]{3,2,1,0:T(8,128)(2,1)S(1)}, u32[]{:S(2)}, u32[]{:S(2)}) collective-permute-start(bf16[144,2,8,128]{3,2,1,0:T(8,128)(2,1)S(1)} %get-tuple-element.25), channel_id=1, source_target_pairs={{0,1},{1,0},{2,3},{3,2},{4,5},{5,4},{6,7},{7,6},{8,9},{9,8},{10,11... | collective-permute-start | bytes 1769480 | tf_op jit(solution)/shard_map/ppermute | solution.py:518
  28.9 1.6 %collective-permute-start.7 = (bf16[144,1,8,128]{3,2,1,0:T(8,128)(2,1)S(1)}, bf16[144,1,8,128]{3,2,1,0:T(8,128)(2,1)S(1)}, u32[]{:S(2)}, u32[]{:S(2)}) collective-permute-start(bf16[144,1,8,128]{3,2,1,0:T(8,128)(2,1)S(1)} %get-tuple-element.29), channel_id=1, source_target_pairs={{0,1},{1,0},{2,3},{3,2},{4,5},{5,4},{6,7},{7,6},{8,9},{9,8},{10,11... | collective-permute-start | bytes 884744 | tf_op jit(solution)/shard_map/ppermute | solution.py:518

commit v6 on v5

--- a/solution.py
+++ b/solution.py
@@ -84,8 +84,14 @@
     odd = lax.rem(lax.axis_index(GRID), 2)
     for out, x in ((e_ref, (1 - odd) * (nx - 1)), (d_ref, odd * (nx - 1))):
         out[:, :modes, :] = o_ref[x]
-        for k in range(terms):
-            coef_rows(out, k, modes, ny)[...] = a_ref[k, x]
+        if send:
+            for k in range(terms):
+                @pl.when(k // ny % 2 == lax.axis_index(MODE))
+                def _():
+                    coef_rows(out, k // (2 * ny) * ny + k % ny, modes, ny)[...] = a_ref[k, x]
+        else:
+            for k in range(terms):
+                coef_rows(out, k, modes, ny)[...] = a_ref[k, x]
     arrange(c_ref, w_ref)
     for out in send:
         count = out.shape[0]
@@ -96,7 +102,7 @@
     modes, nx, ny, nz = field.shape
     terms, outs, total = coupling.shape
     chunk = divisor(modes, (48, 72, 64, 32, 16, 8))
-    outer = (ny, modes + extra_of(terms, ny), nz)
+    outer = (ny, modes + extra_of(-(-terms // 2) if sent else terms, ny), nz)
     block = block_of(chunk)
     shapes = [(nx, ny, modes, nz), outer, outer, (outs, terms * total)] + [(sent, ny, modes, nz)] * (sent > 0)
     shapes = [jax.ShapeDtypeStruct(shape, BF16) for shape in shapes]
@@ -275,7 +281,8 @@
             def _():
                 engine.widen(end, [(rows, ref.at[:, :modes, :]) for rows, ref in zip(places, halo)])
                 for k in range(terms):
-                    coef[end, k] = 0.5 * coef_rows(halo[0], k, modes, ny)[...].astype(F32)
+                    tiles = [coef_rows(ref, k // (2 * ny) * ny + k % ny, modes, ny)[...].astype(F32) for ref in halo]
+                    coef[end, k] = 0.5 * jnp.where(k // ny % 2 == me, tiles[0], tiles[1])
     else:
         layer_of = [(slot, first + slot) for slot in range(slots)]
     for slot, x in layer_of:

time: 31.6 us -> 30.8 us (0.975)
  waiting for transfers between devices: 3.9 us -> 3.15 us
    ppermute x2, waiting for transfers between devices: 1.47 us -> 0.77 us  [exchange(): return lax.ppermute(block, GRID, pairs + [(b, a) for a, b in pairs])]
  transfers between devices with their start and end apart: 8 -> 8, of which waited for: 4 -> 4; matrix products, arithmetic and copies ran while one was open for 0% -> 0% of each run, Pallas kernels for 52% -> 53%
where the time goes in v6:
time: 30.8 us; the launch traced here: 30.6 us
  Pallas kernels  20 us (65%)
  starting transfers between devices  7.38 us (24%)
  waiting for transfers between devices  3.15 us (10%)
    pallas_call x2, Pallas kernels, half_layers(): pl.pallas_call(functools.partial(half_kernel, outer), in_specs=[VMEM] * (...  16.2 us
    ppermute x2, starting transfers between devices, exchange(): return lax.ppermute(block, GRID, pairs + [(b, a) for a, b in pairs])  4.32 us
    ppermute x6, starting transfers between devices, swap(): return lax.ppermute(block, MODE, [(0, 1), (1, 0)])  3.07 us
    pallas_call x1, Pallas kernels, turn(): pl.pallas_call(functools.partial(turn_kernel, chunk), in_specs=[pl.BlockS...  2.93 us
    ppermute x6, waiting for transfers between devices, swap(): return lax.ppermute(block, MODE, [(0, 1), (1, 0)])  2.38 us
    pallas_call x1, Pallas kernels, join(): pl.pallas_call(join_kernel, in_specs=[VMEM, VMEM, HBM], out_specs=HBM, ou...  0.92 us
    ppermute x2, waiting for transfers between devices, exchange(): return lax.ppermute(block, GRID, pairs + [(b, a) for a, b in pairs])  0.77 us
  transfers between devices with their start and end apart: 8, of which 4 were waited for; matrix products, arithmetic and copies ran while one was open for 0% of the time, Pallas kernels for 53%

profile of v6, /device:TPU:27, one launch (start us, length us, event | category | flops | bytes accessed | tf_op | source)
XLA Modules:
  0.0 30.6 jit_solution(4936822547524070972)
XLA Ops:
  0.0 0.0 copy-start
  0.0 2.9 %turn.1 = (bf16[6,8,144,128]{3,2,1,0:T(8,128)(2,1)S(1)}, bf16[8,152,128]{2,1,0:T(8,128)(2,1)S(1)}, bf16[8,152,128]{2,1,0:T(8,128)(2,1)S(1)}, bf16[144,3168]{1,0:T(8,128)(2,1)S(1)}, bf16[4,8,144,128]{3,2,1,0:T(8,128)(2,1)S(1)}) custom-call(bf16[144,6,8,128]{3,2,1,0:T(8,128)(2,1)} %f_hbm.1, bf16[11,6,8,128]{3,2,1,0:T(8,128)(2,1)} %a_ref.3, ...), custom_call_target="tpu_custom_call" | custom-call | tf_op jit(solution)/shard_map/turn/pallas_call | solution.py:110
  2.9 0.7 %collective-permute-start.3 = (bf16[4,8,144,128]{3,2,1,0:T(8,128)(2,1)S(1)}, bf16[4,8,144,128]{3,2,1,0:T(8,128)(2,1)S(1)}, u32[]{:S(2)}, u32[]{:S(2)}) collective-permute-start(bf16[4,8,144,128]{3,2,1,0:T(8,128)(2,1)S(1)} %get-tuple-element.22), channel_id=1, source_target_pairs={{0,1},{1,0},{2,3},{3,2},{4,5},{5,4},{6,7},{7,6},{8,9},{9,8},{10,11... | collective-permute-start | bytes 3538952 | tf_op jit(solution)/shard_map/ppermute | solution.py:525
  3.7 0.1 collective-permute-start.2
  3.8 0.3 collective-permute-start
  4.0 4.1 %collective-permute-start.1 = (bf16[8,152,128]{2,1,0:T(8,128)(2,1)S(1)}, bf16[8,152,128]{2,1,0:T(8,128)(2,1)S(1)}, u32[]{:S(2)}, u32[]{:S(2)}) collective-permute-start(bf16[8,152,128]{2,1,0:T(8,128)(2,1)S(1)} %get-tuple-element.19), channel_id=1, source_target_pairs={{2,4},{6,8},{10,12},{14,16},{18,20},{22,24},{26,28},{4,2},{8,6},{1... | collective-permute-start | bytes 933896 | tf_op jit(solution)/shard_map/ppermute | solution.py:521
  8.1 0.0 collective-permute-done.2.w2_ref
  8.1 0.0 collective-permute-done.3.other
  8.1 0.0 copy-done
  8.1 11.0 %inner.1 = (bf16[144,6,8,128]{3,2,1,0:T(8,128)(2,1)}, bf16[144,2,8,128]{3,2,1,0:T(8,128)(2,1)S(1)}) custom-call(bf16[144,3168]{1,0:T(8,128)(2,1)S(1)} %get-tuple-element.20.w_ref, bf16[144,3168]{1,0:T(8,128)(2,1)S(1)} %collective-permute-done.2.w2_ref, bf16[11,6,8,128]{3,2,1,0:T(8,128)(2,1)S(1)} %copy-done, ...), custom_call_target="tpu_custom_call" | custom-call | flops 3737124864 | bytes 5242880 | tf_op jit(solution)/shard_map/inner/pallas_call | solution.py:333
  19.1 0.0 collective-permute-done.refs_0_
  19.1 0.8 %collective-permute-done.1.refs_2_ = bf16[8,152,128]{2,1,0:T(8,128)(2,1)S(1)} collective-permute-done((bf16[8,152,128]{2,1,0:T(8,128)(2,1)S(1)}, bf16[8,152,128]{2,1,0:T(8,128)(2,1)S(1)}, u32[]{:S(2)}, u32[]{:S(2)}) %collective-permute-start.1) | collective-permute-done | bytes 311328 | tf_op jit(solution)/shard_map/ppermute | solution.py:521
  19.9 1.3 %collective-permute-start.5 = (bf16[8,152,128]{2,1,0:T(8,128)(2,1)S(1)}, bf16[8,152,128]{2,1,0:T(8,128)(2,1)S(1)}, u32[]{:S(2)}, u32[]{:S(2)}) collective-permute-start(bf16[8,152,128]{2,1,0:T(8,128)(2,1)S(1)} %collective-permute-done.refs_0_), channel_id=1, source_target_pairs={{0,1},{1,0},{2,3},{3,2},{4,5},{5,4},{6,7},{7,6},{8,9},{9,8},{10,11... | collective-permute-start | bytes 933896 | tf_op jit(solution)/shard_map/ppermute | solution.py:525
  21.2 0.0 collective-permute-start.6
  21.2 0.5 %collective-permute-start.4 = (bf16[144,2,8,128]{3,2,1,0:T(8,128)(2,1)S(1)}, bf16[144,2,8,128]{3,2,1,0:T(8,128)(2,1)S(1)}, u32[]{:S(2)}, u32[]{:S(2)}) collective-permute-start(bf16[144,2,8,128]{3,2,1,0:T(8,128)(2,1)S(1)} %get-tuple-element.25), channel_id=1, source_target_pairs={{0,1},{1,0},{2,3},{3,2},{4,5},{5,4},{6,7},{7,6},{8,9},{9,8},{10,11... | collective-permute-start | bytes 1769480 | tf_op jit(solution)/shard_map/ppermute | solution.py:525
  21.7 0.7 %collective-permute-done.5.refs_1_ = bf16[8,152,128]{2,1,0:T(8,128)(2,1)S(1)} collective-permute-done((bf16[8,152,128]{2,1,0:T(8,128)(2,1)S(1)}, bf16[8,152,128]{2,1,0:T(8,128)(2,1)S(1)}, u32[]{:S(2)}, u32[]{:S(2)}) %collective-permute-start.5) | collective-permute-done | bytes 311328 | tf_op jit(solution)/shard_map/ppermute | solution.py:525
  22.4 0.4 %collective-permute-done.6.refs_3_ = bf16[8,152,128]{2,1,0:T(8,128)(2,1)S(1)} collective-permute-done((bf16[8,152,128]{2,1,0:T(8,128)(2,1)S(1)}, bf16[8,152,128]{2,1,0:T(8,128)(2,1)S(1)}, u32[]{:S(2)}, u32[]{:S(2)}) %collective-permute-start.6) | collective-permute-done | bytes 311328 | tf_op jit(solution)/shard_map/ppermute | solution.py:525
  22.8 5.2 %outer.1 = (bf16[144,6,8,128]{3,2,1,0:T(8,128)(2,1)}, bf16[144,1,8,128]{3,2,1,0:T(8,128)(2,1)S(1)}) custom-call(bf16[144,3168]{1,0:T(8,128)(2,1)S(1)} %get-tuple-element.20.w_ref, bf16[144,3168]{1,0:T(8,128)(2,1)S(1)} %collective-permute-done.2.w2_ref, bf16[11,6,8,128]{3,2,1,0:T(8,128)(2,1)S(1)} %copy-done, ...), custom_call_target="tpu_custom_call", output_to_operand_aliasing={{0}: (9, {})} | custom-call | flops 1868562432 | bytes 5242880 | tf_op jit(solution)/shard_map/outer/pallas_call | solution.py:333
  28.1 0.4 %collective-permute-start.7 = (bf16[144,1,8,128]{3,2,1,0:T(8,128)(2,1)S(1)}, bf16[144,1,8,128]{3,2,1,0:T(8,128)(2,1)S(1)}, u32[]{:S(2)}, u32[]{:S(2)}) collective-permute-start(bf16[144,1,8,128]{3,2,1,0:T(8,128)(2,1)S(1)} %get-tuple-element.29), channel_id=1, source_target_pairs={{0,1},{1,0},{2,3},{3,2},{4,5},{5,4},{6,7},{7,6},{8,9},{9,8},{10,11... | collective-permute-start | bytes 884744 | tf_op jit(solution)/shard_map/ppermute | solution.py:525
  28.5 0.0 collective-permute-done.4.a_ref
  28.5 1.2 %collective-permute-done.7.b_ref = bf16[144,1,8,128]{3,2,1,0:T(8,128)(2,1)S(1)} collective-permute-done((bf16[144,1,8,128]{3,2,1,0:T(8,128)(2,1)S(1)}, bf16[144,1,8,128]{3,2,1,0:T(8,128)(2,1)S(1)}, u32[]{:S(2)}, u32[]{:S(2)}) %collective-permute-start.7) | collective-permute-done | bytes 294944 | tf_op jit(solution)/shard_map/ppermute | solution.py:525
  29.7 0.9 %join.1 = bf16[144,6,8,128]{3,2,1,0:T(8,128)(2,1)} custom-call(bf16[144,2,8,128]{3,2,1,0:T(8,128)(2,1)S(1)} %collective-permute-done.4.a_ref, bf16[144,1,8,128]{3,2,1,0:T(8,128)(2,1)S(1)} %collective-permute-done.7.b_ref, bf16[144,6,8,128]{3,2,1,0:T(8,128)(2,1)} %get-tuple-element.30._), custom_call_target="tpu_custom_call", output_to_operand_aliasing={{}: (2, {})} | custom-call | tf_op jit(solution)/shard_map/join/pallas_call | solution.py:369
Async XLA Ops:
  0.0 8.1 %copy-start = (bf16[11,6,8,128]{3,2,1,0:T(8,128)(2,1)S(1)}, bf16[11,6,8,128]{3,2,1,0:T(8,128)(2,1)}, u32[]{:S(2)}) copy-start(bf16[11,6,8,128]{3,2,1,0:T(8,128)(2,1)} %a_ref.3) | copy-start | bytes 405508
  2.9 5.2 %collective-permute-start.3 = (bf16[4,8,144,128]{3,2,1,0:T(8,128)(2,1)S(1)}, bf16[4,8,144,128]{3,2,1,0:T(8,128)(2,1)S(1)}, u32[]{:S(2)}, u32[]{:S(2)}) collective-permute-start(bf16[4,8,144,128]{3,2,1,0:T(8,128)(2,1)S(1)} %get-tuple-element.22), channel_id=1, source_target_pairs={{0,1},{1,0},{2,3},{3,2},{4,5},{5,4},{6,7},{7,6},{8,9},{9,8},{10,11... | collective-permute-start | bytes 3538952 | tf_op jit(solution)/shard_map/ppermute | solution.py:525
  3.7 4.4 %collective-permute-start.2 = (bf16[144,3168]{1,0:T(8,128)(2,1)S(1)}, bf16[144,3168]{1,0:T(8,128)(2,1)S(1)}, u32[]{:S(2)}, u32[]{:S(2)}) collective-permute-start(bf16[144,3168]{1,0:T(8,128)(2,1)S(1)} %get-tuple-element.20.w_ref), channel_id=1, source_target_pairs={{0,1},{1,0},{2,3},{3,2},{4,5},{5,4},{6,7},{7,6},{8,9},{9,8},{10,11... | collective-permute-start | bytes 2737160 | tf_op jit(solution)/shard_map/ppermute | solution.py:525
  3.8 15.3 %collective-permute-start = (bf16[8,152,128]{2,1,0:T(8,128)(2,1)S(1)}, bf16[8,152,128]{2,1,0:T(8,128)(2,1)S(1)}, u32[]{:S(2)}, u32[]{:S(2)}) collective-permute-start(bf16[8,152,128]{2,1,0:T(8,128)(2,1)S(1)} %get-tuple-element.18), channel_id=1, source_target_pairs={{0,2},{4,6},{8,10},{12,14},{16,18},{20,22},{24,26},{28,30},{2,0},{... | collective-permute-start | bytes 933896 | tf_op jit(solution)/shard_map/ppermute | solution.py:521
  4.0 15.9 %collective-permute-start.1 = (bf16[8,152,128]{2,1,0:T(8,128)(2,1)S(1)}, bf16[8,152,128]{2,1,0:T(8,128)(2,1)S(1)}, u32[]{:S(2)}, u32[]{:S(2)}) collective-permute-start(bf16[8,152,128]{2,1,0:T(8,128)(2,1)S(1)} %get-tuple-element.19), channel_id=1, source_target_pairs={{2,4},{6,8},{10,12},{14,16},{18,20},{22,24},{26,28},{4,2},{8,6},{1... | collective-permute-start | bytes 933896 | tf_op jit(solution)/shard_map/ppermute | solution.py:521
  19.9 2.5 %collective-permute-start.5 = (bf16[8,152,128]{2,1,0:T(8,128)(2,1)S(1)}, bf16[8,152,128]{2,1,0:T(8,128)(2,1)S(1)}, u32[]{:S(2)}, u32[]{:S(2)}) collective-permute-start(bf16[8,152,128]{2,1,0:T(8,128)(2,1)S(1)} %collective-permute-done.refs_0_), channel_id=1, source_target_pairs={{0,1},{1,0},{2,3},{3,2},{4,5},{5,4},{6,7},{7,6},{8,9},{9,8},{10,11... | collective-permute-start | bytes 933896 | tf_op jit(solution)/shard_map/ppermute | solution.py:525
  21.2 1.7 %collective-permute-start.6 = (bf16[8,152,128]{2,1,0:T(8,128)(2,1)S(1)}, bf16[8,152,128]{2,1,0:T(8,128)(2,1)S(1)}, u32[]{:S(2)}, u32[]{:S(2)}) collective-permute-start(bf16[8,152,128]{2,1,0:T(8,128)(2,1)S(1)} %collective-permute-done.1.refs_2_), channel_id=1, source_target_pairs={{0,1},{1,0},{2,3},{3,2},{4,5},{5,4},{6,7},{7,6},{8,9},{9,8},{10,11... | collective-permute-start | bytes 933896 | tf_op jit(solution)/shard_map/ppermute | solution.py:525
  21.2 7.3 %collective-permute-start.4 = (bf16[144,2,8,128]{3,2,1,0:T(8,128)(2,1)S(1)}, bf16[144,2,8,128]{3,2,1,0:T(8,128)(2,1)S(1)}, u32[]{:S(2)}, u32[]{:S(2)}) collective-permute-start(bf16[144,2,8,128]{3,2,1,0:T(8,128)(2,1)S(1)} %get-tuple-element.25), channel_id=1, source_target_pairs={{0,1},{1,0},{2,3},{3,2},{4,5},{5,4},{6,7},{7,6},{8,9},{9,8},{10,11... | collective-permute-start | bytes 1769480 | tf_op jit(solution)/shard_map/ppermute | solution.py:525
  28.1 1.7 %collective-permute-start.7 = (bf16[144,1,8,128]{3,2,1,0:T(8,128)(2,1)S(1)}, bf16[144,1,8,128]{3,2,1,0:T(8,128)(2,1)S(1)}, u32[]{:S(2)}, u32[]{:S(2)}) collective-permute-start(bf16[144,1,8,128]{3,2,1,0:T(8,128)(2,1)S(1)} %get-tuple-element.29), channel_id=1, source_target_pairs={{0,1},{1,0},{2,3},{3,2},{4,5},{5,4},{6,7},{7,6},{8,9},{9,8},{10,11... | collective-permute-start | bytes 884744 | tf_op jit(solution)/shard_map/ppermute | solution.py:525
